TPU v7x, 32 devices: a whole 2x2x4 slice. The times are simulated.
32 devices in a mesh: lat: 4 (over y, x), lon: 8 (over z, core).
Axes of the slice: x: 2, y: 2, z: 4, core: 2. Of those that a mesh axis runs over, the one named last changes fastest.
Arguments:
- features: bfloat16 [4, 96, 96, 512], P(None, 'lat', 'lon'), may hold values from -6 to 6
- packed_first: bfloat16 [512, 1536], replicated, may hold values from -0.25 to 0.25
- scale_first: float32 [8], replicated, may hold values from 2 to 16
- output_first: bfloat16 [512, 512], replicated, may hold values from -0.25 to 0.25
- gain_first: float32 [512], replicated, may hold values from 0.5 to 1.5
- offset_first: float32 [512], replicated, may hold values from -1.5 to 1.5
- merge_weight: bfloat16 [2048, 1024], replicated, may hold values from -0.125 to 0.125
- merge_gain: float32 [1024], replicated, may hold values from 0.5 to 1.5
- merge_offset: float32 [1024], replicated, may hold values from -1.5 to 1.5
- packed_second: bfloat16 [1024, 1536], replicated, may hold values from -0.1875 to 0.1875
- scale_second: float32 [8], replicated, may hold values from 2 to 16
- output_second: bfloat16 [512, 1024], replicated, may hold values from -0.25 to 0.25
- gain_second: float32 [1024], replicated, may hold values from 0.5 to 1.5
- offset_second: float32 [1024], replicated, may hold values from -1.5 to 1.5
Outputs:
- coarse_out: bfloat16 [48, 8, 2, 12, 1024], P('lat', 'lon')
All inputs are finite; a program needn't handle non-finite values.
Results may differ from a plain program's by a relative error of at most 0.019.
Values may be sent and summed in bfloat16 or wider, within the bound.
No kernel may reach another device: no remote copies, remote signals or barrier semaphores. Data moves between devices by JAX's collectives and lax.ppermute only.
A program may use at most 128 MiB of HBM per device.

v0:
```python
import jax
import jax.numpy as jnp
from jax import lax
from jax.sharding import PartitionSpec as P

WLEV = 2
WLAT = 6
WLON = 12


norm_eps = 1e-05
unit_eps = 1e-06


def passed_along(value, axis, by):
    devices = lax.axis_size(axis)
    return lax.ppermute(value, axis, [(i, (i + by) % devices) for i in range(devices)])


def from_partner(value, axis, distance):
    return lax.ppermute(value, axis, [(i, i ^ 1 << distance) for i in range(lax.axis_size(axis))])


def layer_norm(values, norm_gain, offset):
    average = jnp.mean(values, axis=-1, keepdims=True)
    centred = values - average
    spread = jnp.mean(centred * centred, axis=-1, keepdims=True)
    return centred * lax.rsqrt(spread + norm_eps) * norm_gain + offset


def unit_heads(tensor_in, head_count):
    shaped = tensor_in.reshape(
        tensor_in.shape[:-1] + (head_count, tensor_in.shape[-1] // head_count)
    ).astype(jnp.float32)
    scaled = shaped * lax.rsqrt(jnp.sum(shaped * shaped, axis=-1, keepdims=True) + unit_eps)
    return scaled.astype(jnp.bfloat16)


def attend(queries, keys_in, values_in, query_region, key_region, scales):
    head_count = scales.shape[0]
    query_unit = unit_heads(queries, head_count)
    key_unit = unit_heads(keys_in, head_count)
    scores = jnp.einsum("nahd,nbhd->nhab", query_unit, key_unit, preferred_element_type=jnp.float32)
    scores = scores * scales[None, :, None, None]
    allowed = (query_region[:, :, None] == key_region[:, None, :])[:, None]
    weights = jnp.where(allowed, jnp.exp(scores), jnp.zeros_like(scores))
    totals = jnp.sum(weights, axis=-1)
    value_heads = values_in.reshape(
        values_in.shape[:-1] + (head_count, values_in.shape[-1] // head_count)
    )
    mixture = jnp.einsum(
        "nhab,nbhd->nahd",
        weights.astype(jnp.bfloat16),
        value_heads,
        preferred_element_type=jnp.float32,
    )
    mixture = mixture / jnp.transpose(totals, (0, 2, 1))[..., None]
    return mixture.reshape(queries.shape).astype(jnp.bfloat16)


def to_windows(flat_tile, col_count):
    levels, row_count, joined = flat_tile.shape
    shaped = flat_tile.reshape(levels // WLEV, WLEV, row_count // WLAT, WLAT, joined)
    shaped = jnp.transpose(shaped, (0, 2, 1, 3, 4))
    return shaped.reshape(
        levels // WLEV * (row_count // WLAT), WLEV * WLAT * col_count, joined // col_count
    )


def from_windows(windows, levels, row_count):
    count, tokens, width = windows.shape
    col_count = tokens // (WLEV * WLAT)
    shaped = windows.reshape(levels // WLEV, row_count // WLAT, WLEV, WLAT, col_count * width)
    shaped = jnp.transpose(shaped, (0, 2, 1, 3, 4))
    return shaped.reshape(levels, row_count, col_count * width)


def lat_rows(row_count, lat_pos, lat_total):
    row_index = lat_pos * row_count + jnp.arange(row_count, dtype=jnp.int32)
    return (row_index >= lat_total - WLAT // 2).astype(jnp.int32)


def window_regions(level_wrapped, row_wrapped, col_count):
    levels = level_wrapped.shape[0]
    row_count = row_wrapped.shape[0]
    region = 2 * row_wrapped[None, :] + level_wrapped.astype(jnp.int32)[:, None]
    region = region.reshape(levels // WLEV, WLEV, row_count // WLAT, WLAT)
    region = jnp.transpose(region, (0, 2, 1, 3)).reshape(-1, WLEV * WLAT, 1)
    region = jnp.broadcast_to(region, (region.shape[0], WLEV * WLAT, col_count))
    return region.reshape(region.shape[0], WLEV * WLAT * col_count)


def project(windows, weight):
    product = jnp.dot(
        windows.reshape(-1, windows.shape[-1]), weight, preferred_element_type=jnp.float32
    )
    return product.astype(jnp.bfloat16).reshape(windows.shape[:-1] + (weight.shape[1],))


def finish(context, residual, output_weight, norm_gain, offset):
    width = output_weight.shape[0]
    projected = jnp.dot(
        context.reshape(-1, width), output_weight, preferred_element_type=jnp.float32
    )
    branch = layer_norm(projected, norm_gain, offset).reshape(residual.shape)
    return (residual.astype(jnp.float32) + branch).astype(jnp.bfloat16)


def body(
    features,
    packed_first,
    scale_first,
    output_first,
    gain_first,
    offset_first,
    merge_weight,
    merge_gain,
    merge_offset,
    packed_second,
    scale_second,
    output_second,
    gain_second,
    offset_second,
):
    levels, row_count, col_count, channels = features.shape
    lat_total = row_count * lax.axis_size("lat")
    lat_pos = lax.axis_index("lat")
    lon_pos = lax.axis_index("lon")
    half_lat = WLAT // 2
    half_lon = WLON // 2
    inner_width = packed_first.shape[1] // 3
    query_weight = packed_first[:, :inner_width]
    pair_weight = packed_first[:, inner_width:]
    flat_grid = features.reshape(levels, row_count, col_count * channels)
    rim_rows = passed_along(flat_grid[:, :half_lat], "lat", -1)
    rolled = jnp.concatenate([flat_grid[:, half_lat:], rim_rows], axis=1)
    rolled = jnp.concatenate([rolled[WLEV // 2 :], rolled[: WLEV // 2]], axis=0)
    level_wrapped = jnp.arange(levels) >= levels - WLEV // 2
    row_wrapped = lat_rows(row_count, lat_pos, lat_total)
    split_in = half_lon * channels
    split_out = half_lon * inner_width
    incoming = passed_along(rolled[:, :, :split_in], "lon", -1)
    tile_grid = jnp.concatenate([rolled[:, :, split_in:], incoming], axis=2)
    windows = to_windows(tile_grid, col_count)
    region = window_regions(level_wrapped, row_wrapped, col_count)
    queries = project(windows, query_weight)
    pairs = project(windows, pair_weight)
    context = attend(
        queries, pairs[..., :inner_width], pairs[..., inner_width:], region, region, scale_first
    )
    context = from_windows(context, levels, row_count)
    returned = passed_along(context[:, :, split_out:], "lon", 1)
    context = jnp.concatenate([returned, context[:, :, :split_out]], axis=2)
    context = jnp.concatenate(
        [context[levels - WLEV // 2 :], context[: levels - WLEV // 2]], axis=0
    )
    returned = passed_along(context[:, row_count - half_lat :], "lat", 1)
    context = jnp.concatenate([returned, context[:, : row_count - half_lat]], axis=1)
    first_out = finish(context, features, output_first, gain_first, offset_first)
    half_rows = row_count // 2
    half_cols = col_count // 2
    pair_rows = first_out.reshape(levels, half_rows, 2, half_cols, 2 * channels)
    merge_total = None
    for parity in range(2):
        stacked = jnp.concatenate(
            [
                merge_weight[parity * channels : (parity + 1) * channels],
                merge_weight[(2 + parity) * channels : (3 + parity) * channels],
            ],
            axis=0,
        )
        term = jnp.dot(
            pair_rows[:, :, parity].reshape(-1, 2 * channels),
            stacked,
            preferred_element_type=jnp.float32,
        )
        merge_total = term if merge_total is None else merge_total + term
    merged = layer_norm(merge_total, merge_gain, merge_offset).astype(jnp.bfloat16)
    wide = merged.shape[-1]
    merged = merged.reshape(levels, half_rows, half_cols * wide)
    is_even = lon_pos % 2 == 0
    outgoing = jnp.where(is_even, merged[WLEV:], merged[:WLEV])
    keep_part = jnp.where(is_even, merged[:WLEV], merged[WLEV:])
    incoming = from_partner(outgoing, "lon", 0)
    own_levels = jnp.where(
        is_even,
        jnp.concatenate([keep_part, incoming], axis=2),
        jnp.concatenate([incoming, keep_part], axis=2),
    )
    level_edge = from_partner(own_levels[:1], "lon", 0)
    rolled = jnp.concatenate([own_levels[1:], level_edge], axis=0)
    rim_rows = passed_along(rolled[:, :half_lat], "lat", -1)
    rolled = jnp.concatenate([rolled[:, half_lat:], rim_rows], axis=1)
    split_wide = half_lon * wide
    incoming = passed_along(rolled[:, :, :split_wide], "lon", -2)
    tile_grid = jnp.concatenate([rolled[:, :, split_wide:], incoming], axis=2)
    second_width = packed_second.shape[1] // 3
    level_wrapped = jnp.logical_and(jnp.arange(WLEV) == WLEV - 1, jnp.logical_not(is_even))
    row_wrapped = lat_rows(half_rows, lat_pos, lat_total // 2)
    region = window_regions(level_wrapped, row_wrapped, WLON)
    windows = to_windows(tile_grid, WLON)
    queries = project(windows, packed_second[:, :second_width])
    pairs = project(windows, packed_second[:, second_width:])
    context = attend(
        queries, pairs[..., :second_width], pairs[..., second_width:], region, region, scale_second
    )
    context = from_windows(context, WLEV, half_rows)
    split_back = half_lon * second_width
    returned = passed_along(context[:, :, split_back:], "lon", 2)
    context = jnp.concatenate([returned, context[:, :, :split_back]], axis=2)
    returned = passed_along(context[:, half_rows - half_lat :], "lat", 1)
    context = jnp.concatenate([returned, context[:, : half_rows - half_lat]], axis=1)
    returned = from_partner(context[1:], "lon", 0)
    context = jnp.concatenate([returned, context[:1]], axis=0)
    second = finish(
        context,
        own_levels.reshape(WLEV, half_rows, WLON, wide),
        output_second,
        gain_second,
        offset_second,
    )
    return jnp.transpose(second, (1, 0, 2, 3))[:, None]


def solution(mesh):
    return jax.shard_map(
        body,
        mesh=mesh,
        in_specs=(
            P(None, "lat", "lon", None),
            P(),
            P(),
            P(),
            P(),
            P(),
            P(),
            P(),
            P(),
            P(),
            P(),
            P(),
            P(),
            P(),
        ),
        out_specs=P("lat", "lon", None, None, None),
        check_vma=False,
    )
```

profile of v0, /device:TPU:0, one launch (start us, length us, event | category | flops | bytes accessed | tf_op | source)
XLA Modules:
  0.0 180.6 jit_solution(11221878761812928604)
XLA Ops:
  1.5 4.0 %collective-permute-start = (bf16[4,3,6144]{2,1,0:T(4,128)(2,1)S(1)}, bf16[4,3,6144]{2,1,0:T(4,128)(2,1)S(1)}, u32[]{:S(2)}, u32[]{:S(2)}) collective-permute-start(bf16[4,3,6144]{2,1,0:T(4,128)(2,1)S(1)} %slice.165), channel_id=1, source_target_pairs={{0,24},{8,0},{16,8},{24,16},{1,25},{9,1},{17,9},{25,17},{2,26},{10... | collective-permute-start | bytes 442376 | tf_op jit(solution)/shard_map/ppermute | solution.py:17
  5.8 3.9 %collective-permute-done = bf16[4,3,6144]{2,1,0:T(4,128)(2,1)S(1)} collective-permute-done((bf16[4,3,6144]{2,1,0:T(4,128)(2,1)S(1)}, bf16[4,3,6144]{2,1,0:T(4,128)(2,1)S(1)}, u32[]{:S(2)}, u32[]{:S(2)}) %collective-permute-start) | collective-permute-done | bytes 147488 | tf_op jit(solution)/shard_map/ppermute | solution.py:17
  13.6 6.1 %collective-permute-done.1 = bf16[4,24,3072]{2,1,0:T(8,128)(2,1)S(1)} collective-permute-done((bf16[4,24,3072]{2,1,0:T(8,128)(2,1)S(1)}, bf16[4,24,3072]{2,1,0:T(8,128)(2,1)S(1)}, u32[]{:S(2)}, u32[]{:S(2)}) %collective-permute-start.1) | collective-permute-done | bytes 589856 | tf_op jit(solution)/shard_map/ppermute | solution.py:17
  26.8 3.8 %fusion.8 = f32[1152,512]{1,0:T(8,128)} fusion(bf16[1152,512]{1,0:T(8,128)(2,1)} %reshape_reshape.4, bf16[512,1536]{1,0:T(8,128)(2,1)} %param.15), kind=kOutput, calls=%fused_computation.16 | convolution fusion | flops 605159424 | bytes 4063232 | tf_op jit(solution)/shard_map/dot_general | solution.py:94
  30.6 2.8 %convolution_convert_fusion = bf16[1152,1024]{1,0:T(8,128)(2,1)} fusion(bf16[1152,512]{1,0:T(8,128)(2,1)S(1)} %copy-done.3, bf16[512,1536]{1,0:T(8,128)(2,1)S(1)} %copy-done.17), kind=kOutput, calls=%fused_computation.13 | convolution fusion | flops 1209139200 | bytes 4587520 | tf_op jit(solution)/shard_map/dot_general | solution.py:94
  35.4 4.1 %reshape.235 = f32[8,144,8,64]{1,0,3,2:T(8,128)} reshape(f32[1152,512]{0,1:T(8,128)S(1)} %copy.140) | data formatting | bytes 4718592 | tf_op jit(solution)/shard_map/convert_element_type | solution.py:34
  39.5 2.7 %multiply_reduce_fusion.1 = f32[8,144,8]{1,0,2:T(8,128)S(1)} fusion(f32[8,144,8,64]{1,0,3,2:T(8,128)} %reshape.235), kind=kLoop, calls=%fused_computation.12 | loop fusion | flops 1170432 | bytes 2396160 | tf_op jit(solution)/shard_map/reduce_sum | solution.py:35
  46.9 3.3 %copy.141 = f32[8,144,512]{1,2,0:T(8,128)} copy(f32[8,144,512]{2,1,0:T(8,128)S(1)} %get-tuple-element.9) | data formatting | bytes 4718592 | tf_op jit(solution)/shard_map/convert_element_type | solution.py:34
  50.2 2.8 %multiply_reduce_fusion = f32[8,144,8]{1,2,0:T(8,128)S(1)} fusion(f32[8,144,512]{1,2,0:T(8,128)} %copy.141), kind=kLoop, calls=%fused_computation.10 | loop fusion | flops 1170432 | bytes 2396160 | tf_op jit(solution)/shard_map/reduce_sum | solution.py:35
  53.1 3.7 %copy.139 = bf16[8,144,512]{1,2,0:T(8,128)(2,1)} copy(bf16[8,144,512]{2,1,0:T(8,128)(2,1)} %get-tuple-element.10) | data formatting | bytes 2359296 | tf_op jit(solution)/shard_map/slice | solution.py:149
  56.9 4.8 %fusion = (f32[8,8,144]{2,1,0:T(8,128)S(1)}, f32[8,8,144,144]{2,3,1,0:T(8,128)S(1)}) fusion(f32[8]{0:T(128)S(1)} %copy-done.24, pred[8,144,144]{1,2,0:T(8,128)(4,1)S(1)} %copy-done.8, f32[8,144,8,64]{1,3,2,0:T(8,128)} %bitcast.57, f32[8,144,8]{1,2,0:T(8,128)S(1)} %copy.143, bf16[8,144,8,64]{1,0,3,2:T(8,128)(2,1)S(1)} %copy-done.2), kind=kOutput, calls=%fused_computation.1 | convolution fusion | flops 175021056 | bytes 9087008 | tf_op jit(solution)/shard_map/nahd,nbhd->nhab/dot_general | solution.py:43
  61.7 3.2 %fusion.7 = bf16[8,144,8,64]{1,3,2,0:T(8,128)(2,1)} fusion(bf16[8,144,8,64]{1,3,2,0:T(8,128)(2,1)S(1)} %bitcast.66, f32[8,8,144,144]{2,3,1,0:T(8,128)S(1)} %get-tuple-element.30, f32[8]{0:T(128)S(1)} %copy-done.24, pred[8,144,144]{1,2,0:T(8,128)(4,1)S(1)} %copy-done.8, f32[8,144,8]{1,2,0:T(8,128)S(1)} %bitcast.71), kind=kOutput, calls=%fused_computation.8 | convolution fusion | flops 175030272 | bytes 7870496 | tf_op jit(solution)/shard_map/nhab,nbhd->nahd/dot_general | solution.py:51
  64.9 3.2 %copy.146 = bf16[8,144,8,64]{3,2,1,0:T(8,128)(2,1)S(1)} copy(bf16[8,144,8,64]{1,3,2,0:T(8,128)(2,1)} %fusion.7) | data formatting | bytes 2359296 | tf_op jit(solution)/shard_map/convert_element_type | solution.py:58
  68.1 2.9 %convert_element_type.119 = bf16[2,4,2,6,6144]{4,3,2,1,0:T(8,128)(2,1)} reshape(bf16[8,144,8,64]{3,2,1,0:T(8,128)(2,1)S(1)} %copy.146) | data formatting | bytes 2359296 | tf_op jit(solution)/shard_map/convert_element_type | solution.py:58
  71.0 3.6 %copy.147 = bf16[2,2,4,6,6144]{4,1,0,3,2:T(2,128)(2,1)} copy(bf16[2,2,4,6,6144]{4,3,1,2,0:T(8,128)(2,1)} %bitcast.59) | data formatting | bytes 2359296 | tf_op jit(solution)/shard_map/transpose | solution.py:74
  74.7 3.3 %reshape.225 = bf16[4,24,6144]{2,0,1:T(4,128)(2,1)S(1)} reshape(bf16[2,2,4,6,6144]{4,1,0,3,2:T(2,128)(2,1)} %copy.147) | data formatting | bytes 2359296 | tf_op jit(solution)/shard_map/reshape | solution.py:75
  78.5 11.3 %collective-permute-done.2 = bf16[4,24,3072]{2,0,1:T(4,128)(2,1)S(1)} collective-permute-done((bf16[4,24,3072]{2,0,1:T(4,128)(2,1)S(1)}, bf16[4,24,3072]{2,0,1:T(4,128)(2,1)S(1)}, u32[]{:S(2)}, u32[]{:S(2)}) %collective-permute-start.2) | collective-permute-done | bytes 589856 | tf_op jit(solution)/shard_map/ppermute | solution.py:17
  105.4 4.1 %add_convert_fusion = bf16[4,24,12,512]{3,2,1,0:T(8,128)(2,1)} fusion(f32[4,24,12,512]{3,2,1,0:T(8,128)} %reshape.227, bf16[4,24,12,512]{3,1,2,0:T(8,128)(2,1)} %param.14), kind=kLoop, calls=%fused_computation.14 | loop fusion | flops 1769472 | bytes 4718592 | tf_op jit(solution)/shard_map/convert_element_type | solution.py:106
  109.5 2.4 %reshape.228 = bf16[4,12,2,6,1024]{4,3,2,1,0:T(8,128)(2,1)S(1)} reshape(bf16[4,24,12,512]{3,2,1,0:T(8,128)(2,1)} %add_convert_fusion) | data formatting | bytes 2359296 | tf_op jit(solution)/shard_map/reshape | solution.py:162
  126.9 4.7 %collective-permute-done.6 = bf16[2,3,12288]{2,1,0:T(4,128)(2,1)S(1)} collective-permute-done((bf16[2,3,12288]{2,1,0:T(4,128)(2,1)S(1)}, bf16[2,3,12288]{2,1,0:T(4,128)(2,1)S(1)}, u32[]{:S(2)}, u32[]{:S(2)}) %collective-permute-start.6) | collective-permute-done | bytes 147488 | tf_op jit(solution)/shard_map/ppermute | solution.py:17
  133.4 8.7 %collective-permute-done.7 = bf16[2,12,6144]{2,1,0:T(8,128)(2,1)S(1)} collective-permute-done((bf16[2,12,6144]{2,1,0:T(8,128)(2,1)S(1)}, bf16[2,12,6144]{2,1,0:T(8,128)(2,1)S(1)}, u32[]{:S(2)}, u32[]{:S(2)}) %collective-permute-start.7) | collective-permute-done | bytes 294944 | tf_op jit(solution)/shard_map/ppermute | solution.py:17
  146.8 3.2 %fusion.30 = bf16[288,1024]{1,0:T(8,128)(2,1)} fusion(bf16[288,1024]{1,0:T(8,128)(2,1)S(1)} %copy-done.14, bf16[1024,1536]{1,0:T(8,128)(2,1)} %param.23), kind=kOutput, calls=%fused_computation.39 | convolution fusion | flops 604274688 | bytes 3276800 | tf_op jit(solution)/shard_map/dot_general | solution.py:94
  158.6 6.9 %collective-permute-done.8 = bf16[2,12,3072]{2,0,1:T(2,128)(2,1)S(1)} collective-permute-done((bf16[2,12,3072]{2,0,1:T(2,128)(2,1)S(1)}, bf16[2,12,3072]{2,0,1:T(2,128)(2,1)S(1)}, u32[]{:S(2)}, u32[]{:S(2)}) %collective-permute-start.8) | collective-permute-done | bytes 147488 | tf_op jit(solution)/shard_map/ppermute | solution.py:17
  167.9 3.3 %collective-permute-done.9 = bf16[2,3,6144]{2,0,1:T(2,128)(2,1)S(1)} collective-permute-done((bf16[2,3,6144]{2,0,1:T(2,128)(2,1)S(1)}, bf16[2,3,6144]{2,0,1:T(2,128)(2,1)S(1)}, u32[]{:S(2)}, u32[]{:S(2)}) %collective-permute-start.9) | collective-permute-done | bytes 73760 | tf_op jit(solution)/shard_map/ppermute | solution.py:17
  (165 shorter events, 76.8 us)
Async XLA Ops:
  0.0 174.7 %copy-start = (bf16[512,1024]{1,0:T(8,128)(2,1)S(1)}, bf16[512,1024]{1,0:T(8,128)(2,1)}, u32[]{:S(2)}) copy-start(bf16[512,1024]{1,0:T(8,128)(2,1)} %param.25) | copy-start | bytes 3145732
  1.5 8.1 %collective-permute-start = (bf16[4,3,6144]{2,1,0:T(4,128)(2,1)S(1)}, bf16[4,3,6144]{2,1,0:T(4,128)(2,1)S(1)}, u32[]{:S(2)}, u32[]{:S(2)}) collective-permute-start(bf16[4,3,6144]{2,1,0:T(4,128)(2,1)S(1)} %slice.165), channel_id=1, source_target_pairs={{0,24},{8,0},{16,8},{24,16},{1,25},{9,1},{17,9},{25,17},{2,26},{10... | collective-permute-start | bytes 442376 | tf_op jit(solution)/shard_map/ppermute | solution.py:17
  10.0 9.7 %collective-permute-start.1 = (bf16[4,24,3072]{2,1,0:T(8,128)(2,1)S(1)}, bf16[4,24,3072]{2,1,0:T(8,128)(2,1)S(1)}, u32[]{:S(2)}, u32[]{:S(2)}) collective-permute-start(bf16[4,24,3072]{2,1,0:T(8,128)(2,1)S(1)} %get-tuple-element.16), channel_id=1, source_target_pairs={{0,7},{1,0},{2,1},{3,2},{4,3},{5,4},{6,5},{7,6},{8,15},{9,8},{10,9... | collective-permute-start | bytes 1769480 | tf_op jit(solution)/shard_map/ppermute | solution.py:17
  26.8 3.8 %copy-start.3 = (bf16[1152,512]{1,0:T(8,128)(2,1)S(1)}, bf16[1152,512]{1,0:T(8,128)(2,1)}, u32[]{:S(2)}) copy-start(bf16[1152,512]{1,0:T(8,128)(2,1)} %reshape_reshape.4) | copy-start | bytes 3538948
  26.8 3.8 %copy-start.17 = (bf16[512,1536]{1,0:T(8,128)(2,1)S(1)}, bf16[512,1536]{1,0:T(8,128)(2,1)}, u32[]{:S(2)}) copy-start(bf16[512,1536]{1,0:T(8,128)(2,1)} %param.15) | copy-start | bytes 4718596
  39.5 3.4 %copy-start.1 = (f32[8,144,8,64]{1,0,3,2:T(8,128)S(1)}, f32[8,144,8,64]{1,0,3,2:T(8,128)}, u32[]{:S(2)}) copy-start(f32[8,144,8,64]{1,0,3,2:T(8,128)} %reshape.235) | copy-start | bytes 7077892
  43.0 2.4 %copy-start.5 = (bf16[1152,1024]{1,0:T(8,128)(2,1)S(1)}, bf16[1152,1024]{1,0:T(8,128)(2,1)}, u32[]{:S(2)}) copy-start(bf16[1152,1024]{1,0:T(8,128)(2,1)} %convolution_convert_fusion) | copy-start | bytes 7077892
  53.0 3.9 %copy-start.2 = (bf16[8,144,8,64]{1,0,3,2:T(8,128)(2,1)S(1)}, bf16[8,144,8,64]{1,0,3,2:T(8,128)(2,1)}, u32[]{:S(2)}) copy-start(bf16[8,144,8,64]{1,0,3,2:T(8,128)(2,1)} %multiply_convert_fusion.1) | copy-start | bytes 3538948
  53.1 3.8 %copy-start.8 = (pred[8,144,144]{1,2,0:T(8,128)(4,1)S(1)}, pred[8,144,144]{1,2,0:T(8,128)(4,1)}, u32[]{:S(2)}) copy-start(pred[8,144,144]{1,2,0:T(8,128)(4,1)} %broadcast_compare_fusion) | copy-start | bytes 497668
  53.1 3.8 %copy-start.24 = (f32[8]{0:T(128)S(1)}, f32[8]{0:T(128)}, u32[]{:S(2)}) copy-start(f32[8]{0:T(128)} %param.16) | copy-start | bytes 100
  56.9 4.8 %copy-start.6 = (bf16[8,144,512]{1,2,0:T(8,128)(2,1)S(1)}, bf16[8,144,512]{1,2,0:T(8,128)(2,1)}, u32[]{:S(2)}) copy-start(bf16[8,144,512]{1,2,0:T(8,128)(2,1)} %copy.139) | copy-start | bytes 3538948
  78.0 15.1 %copy-start.4 = (bf16[2048,1024]{1,0:T(8,128)(2,1)S(1)}, bf16[2048,1024]{1,0:T(8,128)(2,1)}, u32[]{:S(2)}) copy-start(bf16[2048,1024]{1,0:T(8,128)(2,1)} %param.20) | copy-start | bytes 12582916
  78.4 11.3 %collective-permute-start.2 = (bf16[4,24,3072]{2,0,1:T(4,128)(2,1)S(1)}, bf16[4,24,3072]{2,0,1:T(4,128)(2,1)S(1)}, u32[]{:S(2)}, u32[]{:S(2)}) collective-permute-start(bf16[4,24,3072]{2,0,1:T(4,128)(2,1)S(1)} %get-tuple-element.14), channel_id=1, source_target_pairs={{0,1},{1,2},{2,3},{3,4},{4,5},{5,6},{6,7},{7,0},{8,9},{9,10},{10,1... | collective-permute-start | bytes 1769480 | tf_op jit(solution)/shard_map/ppermute | solution.py:17
  90.7 6.5 %collective-permute-start.3 = (bf16[4,3,6144]{2,0,1:T(4,128)(2,1)S(1)}, bf16[4,3,6144]{2,0,1:T(4,128)(2,1)S(1)}, u32[]{:S(2)}, u32[]{:S(2)}) collective-permute-start(bf16[4,3,6144]{2,0,1:T(4,128)(2,1)S(1)} %pad_maximum_fusion.9), channel_id=1, source_target_pairs={{0,8},{8,16},{16,24},{24,0},{1,9},{9,17},{17,25},{25,1},{2,10},{10... | collective-permute-start | bytes 442376 | tf_op jit(solution)/shard_map/ppermute | solution.py:17
  113.0 3.2 %copy-start.11 = (bf16[512,1024]{1,0:T(8,128)(2,1)S(1)}, bf16[512,1024]{1,0:T(8,128)(2,1)}, u32[]{:S(2)}) copy-start(bf16[512,1024]{1,0:T(8,128)(2,1)} %get-tuple-element.6) | copy-start | bytes 3145732
  116.2 2.4 %copy-start.13 = (bf16[288,1024]{1,0:T(8,128)(2,1)S(1)}, bf16[288,1024]{1,0:T(8,128)(2,1)}, u32[]{:S(2)}) copy-start(bf16[288,1024]{1,0:T(8,128)(2,1)} %reshape_squeeze.7) | copy-start | bytes 1769476
  120.4 1.8 collective-permute-start.4
  122.5 1.8 collective-permute-start.5
  124.3 7.2 %collective-permute-start.6 = (bf16[2,3,12288]{2,1,0:T(4,128)(2,1)S(1)}, bf16[2,3,12288]{2,1,0:T(4,128)(2,1)S(1)}, u32[]{:S(2)}, u32[]{:S(2)}) collective-permute-start(bf16[2,3,12288]{2,1,0:T(4,128)(2,1)S(1)} %pad_maximum_fusion.8), channel_id=1, source_target_pairs={{0,24},{8,0},{16,8},{24,16},{1,25},{9,1},{17,9},{25,17},{2,26},{10... | collective-permute-start | bytes 442376 | tf_op jit(solution)/shard_map/ppermute | solution.py:17
  131.7 10.4 %collective-permute-start.7 = (bf16[2,12,6144]{2,1,0:T(8,128)(2,1)S(1)}, bf16[2,12,6144]{2,1,0:T(8,128)(2,1)S(1)}, u32[]{:S(2)}, u32[]{:S(2)}) collective-permute-start(bf16[2,12,6144]{2,1,0:T(8,128)(2,1)S(1)} %get-tuple-element.18), channel_id=1, source_target_pairs={{0,6},{1,7},{2,0},{3,1},{4,2},{5,3},{6,4},{7,5},{8,14},{9,15},{10,... | collective-permute-start | bytes 884744 | tf_op jit(solution)/shard_map/ppermute | solution.py:17
  158.6 7.0 %collective-permute-start.8 = (bf16[2,12,3072]{2,0,1:T(2,128)(2,1)S(1)}, bf16[2,12,3072]{2,0,1:T(2,128)(2,1)S(1)}, u32[]{:S(2)}, u32[]{:S(2)}) collective-permute-start(bf16[2,12,3072]{2,0,1:T(2,128)(2,1)S(1)} %get-tuple-element.27), channel_id=1, source_target_pairs={{0,2},{1,3},{2,4},{3,5},{4,6},{5,7},{6,0},{7,1},{8,10},{9,11},{10,... | collective-permute-start | bytes 442376 | tf_op jit(solution)/shard_map/ppermute | solution.py:17
  165.6 5.6 %collective-permute-start.9 = (bf16[2,3,6144]{2,0,1:T(2,128)(2,1)S(1)}, bf16[2,3,6144]{2,0,1:T(2,128)(2,1)S(1)}, u32[]{:S(2)}, u32[]{:S(2)}) collective-permute-start(bf16[2,3,6144]{2,0,1:T(2,128)(2,1)S(1)} %pad_maximum_fusion.10), channel_id=1, source_target_pairs={{0,8},{8,16},{16,24},{24,0},{1,9},{9,17},{17,25},{25,1},{2,10},{10... | collective-permute-start | bytes 221192 | tf_op jit(solution)/shard_map/ppermute | solution.py:17
  171.8 1.6 collective-permute-start.10
  175.6 2.7 %copy-start.7 = (bf16[2,12,6,1024]{3,2,1,0:T(8,128)(2,1)S(1)}, bf16[2,12,6,1024]{3,2,1,0:T(8,128)(2,1)}, u32[]{:S(2)}) copy-start(bf16[2,12,6,1024]{3,2,1,0:T(8,128)(2,1)} %select_n.55) | copy-start | bytes 884740
  (13 other events, 19.7 us)
where the time goes:
time: 184 us; the launch traced here: 181 us
  local copies, waits for them, and re-layouts  62.1 us (34%)
  waiting for transfers between devices  50.2 us (27%)
  matrix products  27.9 us (15%)
  other arithmetic  25.1 us (14%)
  starting transfers between devices  14.3 us (8%)
    ppermute x8, waiting for transfers between devices, passed_along(): lax.ppermute(value, axis, [(i, (i + by) % devices) for i in range(devices)])  46.8 us
    ppermute x8, starting transfers between devices, passed_along(): lax.ppermute(value, axis, [(i, (i + by) % devices) for i in range(devices)])  14 us
    dot_general x4, matrix products, project(): jnp.dot(windows.reshape(-1, windows.shape[-1]), weight, preferred_element...  11.7 us
    convert_element_type x5, local copies, waits for them, and re-layouts, unit_heads(): shaped = tensor_in.reshape(tensor_in.shape[:-1] + (head_count, tensor_in....  9.97 us
    convert_element_type x4, local copies, waits for them, and re-layouts, attend(): return mixture.reshape(queries.shape).astype(jnp.bfloat16)  6.99 us
    dot_general x2, matrix products, attend(): jnp.einsum('nahd,nbhd->nhab', query_unit, key_unit, preferred_element_typ...  6.73 us
    reduce_sum x4, other arithmetic, unit_heads(): jnp.sum(shaped * shaped, axis=-1, keepdims=True) + unit_eps  6.02 us
    convert_element_type x1, other arithmetic, finish(): return (residual.astype(jnp.float32) + branch).astype(jnp.bfloat16)  4.12 us
  transfers between devices with their start and end apart: 11, of which 11 were waited for; matrix products, arithmetic and copies ran while one was open for 4% of the time, Pallas kernels for 0%

commit v1 on v0

v1 whole, which is shorter than its diff:
```python
import functools
import math

import jax
import jax.numpy as jnp
import numpy as np
from jax import lax
from jax.experimental import pallas as pl
from jax.experimental.pallas import tpu as pltpu
from jax.sharding import PartitionSpec as P

WLEV = 2
WLAT = 6
WLON = 12
HALF_LAT = WLAT // 2
HALF_LON = WLON // 2
LANES = 128
SHUT = -30000.0

norm_eps = 1e-05
unit_eps = 1e-06

PART = WLEV * HALF_LAT * HALF_LON
GROUP = -(-2 * PART // 16) * 16


def rolled_levels(levels):
    return [(l + WLEV // 2) % levels for l in range(levels)]


def window_slots(levels):
    order = rolled_levels(levels)
    for place, level in enumerate(order):
        pair, lev = divmod(place, WLEV)
        for side in range(2):
            for i in range(HALF_LAT):
                for c in range(HALF_LON):
                    t = (i * WLEV + lev) * HALF_LON + c
                    yield pair * GROUP + side * PART + t, side, level, i, c


def slot_table(levels):
    table = {}
    for row, side, level, i, c in window_slots(levels):
        table[(side, level, i, c)] = row
    return table


def column(values):
    return np.asarray(values, np.int32).reshape(-1, 1)


def fine_gather(levels):
    rows = levels // WLEV * GROUP
    out = [np.full(rows, -1), np.full(rows, -1)]
    for row, side, level, i, c in window_slots(levels):
        out[side][row] = (i * levels + level) * HALF_LON + c
    return column(out[0]), column(out[1])


def patch_gather(levels, row_count):
    span = levels // WLEV * GROUP
    slots = slot_table(levels)
    out = []
    for g in range(4):
        dc, dr = divmod(g, 2)
        rows = []
        for i in range(row_count // 2):
            for level in range(levels):
                for cc in range(HALF_LON // 2):
                    r = 2 * i + dr
                    chunk = r // HALF_LAT + 1
                    w, side = divmod(chunk, 2)
                    rows.append(w * span + slots[(side, level, r % HALF_LAT, 2 * cc + dc)])
        out.append(column(rows))
    return np.stack(out)


def coarse_gather(levels, row_count):
    span = levels // WLEV * GROUP
    chunks = row_count // HALF_LAT
    windows = (chunks + 2) // 2
    third = HALF_LON // 2
    small = HALF_LAT * levels * third
    out = np.full((3, windows * span, 1), -1, np.int32)
    for w in range(windows):
        for row, side, level, i, c in window_slots(levels):
            chunk = 2 * w + side - 1
            which, cc = divmod(c, third)
            cell = (i * levels + level) * third + cc
            at = w * span + row
            if 0 <= chunk < chunks:
                out[which, at, 0] = chunk * small + cell
            else:
                out[2, at, 0] = (0 if chunk < 0 else 2 * small) + which * small + cell
    return out


def edge_gather(levels, row_count):
    third = HALF_LON // 2
    small = HALF_LAT * levels * third
    chunks = row_count // HALF_LAT
    out = np.full((2, 2, 2 * small, 1), -1, np.int32)
    for end in range(2):
        base = 0 if end == 0 else (chunks - 1) * small
        for which in range(2):
            out[end, which, which * small : (which + 1) * small, 0] = base + np.arange(small)
    return out


def final_gather(levels, row_count, even):
    span = levels // WLEV * GROUP
    slots = slot_table(levels)
    third = HALF_LON // 2
    halves = []
    for part in range(2):
        h = part if even else 1 - part
        rows = []
        for r in range(row_count):
            for e in range(levels // 2):
                for c in range(HALF_LON):
                    place = (c + third) % HALF_LON if even else c
                    w, side = divmod(r // HALF_LAT + 1, 2)
                    level = h * (levels // 2) + e
                    rows.append(w * span + slots[(side, level, r % HALF_LAT, place)])
        halves.append(column(rows))
    return np.stack(halves)


def aux_tables(levels):
    pairs = levels // WLEV
    order = rolled_levels(levels)
    hot = np.zeros((2, GROUP, LANES), np.float32)
    shut = np.zeros((pairs, 2, 2, GROUP, LANES), np.float32)
    sides = np.arange(GROUP) // PART
    levs = np.arange(GROUP) % PART // HALF_LON % WLEV
    valid = np.arange(GROUP) < 2 * PART
    for half in range(2):
        base = LANES // 2 * (1 - half)
        for side in range(2):
            for lev in range(WLEV):
                lane = base + side * WLEV + lev
                member = valid & (sides == side) & (levs == lev)
                if side == 0 and lev == 0:
                    member = member | ~valid
                hot[half, :, lane] = member
                for pair in range(pairs):
                    wrapped = [order[pair * WLEV + v] < WLEV // 2 for v in range(WLEV)]
                    same = np.asarray([wrapped[v] == wrapped[lev] for v in range(WLEV)])[levs]
                    for wrap in range(2):
                        allowed = valid & same
                        if wrap:
                            allowed = allowed & (sides == side)
                        shut[pair, wrap, half, :, lane] = np.where(allowed, 0.0, SHUT)
    return hot, shut


def one_hot(index, width):
    lanes = lax.broadcasted_iota(jnp.int32, (index.shape[0], width), 1)
    return (lanes == index).astype(jnp.float32).astype(jnp.bfloat16)


def mm(a, b):
    return jnp.dot(a, b, preferred_element_type=jnp.float32)


def layer_norm(values, norm_gain, offset):
    average = jnp.mean(values, axis=-1, keepdims=True)
    centred = values - average
    spread = jnp.mean(centred * centred, axis=-1, keepdims=True)
    return centred * lax.rsqrt(spread + norm_eps) * norm_gain + offset


def window_context(own, other, weight_ref, scale, wrap, hot_ref, shut_ref, ctx_ref):
    width = weight_ref.shape[1] // 3
    pairs = own.shape[0] // GROUP
    mine = mm(own, weight_ref[...])
    theirs = mm(other, weight_ref[:, width:])
    rows = lax.broadcasted_iota(jnp.int32, (LANES, LANES), 0) // (LANES // 2)
    cols = lax.broadcasted_iota(jnp.int32, (LANES, LANES), 1) // (LANES // 2)
    same = (rows == cols).astype(jnp.float32).astype(jnp.bfloat16)
    lane = lax.broadcasted_iota(jnp.int32, (1, LANES), 1)
    first = (lane < LANES // 2).astype(jnp.float32)
    keep = [first.astype(jnp.bfloat16), (1.0 - first).astype(jnp.bfloat16)]
    fill = [keep[1], keep[0]]
    is_first = lax.broadcasted_iota(jnp.int32, (GROUP, LANES), 1) < LANES // 2

    def unit(block):
        total = mm((block * block).astype(jnp.bfloat16), same)
        return block * lax.rsqrt(total + unit_eps)

    for j in range(width // LANES):
        at = slice(j * LANES, (j + 1) * LANES)
        q = (unit(mine[:, at]) * scale[:, at]).astype(jnp.bfloat16)
        k_at = slice(width + j * LANES, width + (j + 1) * LANES)
        k_own = unit(mine[:, k_at]).astype(jnp.bfloat16)
        k_other = unit(theirs[:, at]).astype(jnp.bfloat16)
        v_own = mine[:, 2 * width + j * LANES : 2 * width + (j + 1) * LANES].astype(jnp.bfloat16)
        v_other = theirs[:, k_at].astype(jnp.bfloat16)
        for pair in range(pairs):
            part = slice(pair * GROUP, (pair + 1) * GROUP)
            out = []
            for half in range(2):
                shut = shut_ref[pair, wrap, half]
                qh = q[part] * keep[half] + hot_ref[half]
                kh = jnp.concatenate(
                    [k_own[part] * keep[half] + shut, k_other[part] * keep[half] + shut], axis=0
                )
                vh = jnp.concatenate(
                    [v_own[part] * keep[half] + fill[half], v_other[part] * keep[half] + fill[half]],
                    axis=0,
                )
                score = lax.dot_general(
                    qh, kh, (((1,), (1,)), ((), ())), preferred_element_type=jnp.float32
                )
                out.append(mm(jnp.exp2(score).astype(jnp.bfloat16), vh))
            top = jnp.where(is_first, out[0], out[1])
            total = pltpu.roll(jnp.where(is_first, out[1], out[0]), LANES // 2, 1)
            ctx_ref[part, at] = (top / total).astype(jnp.bfloat16)


def side_kernel(
    with_edges,
    flags,
    own_ref,
    other_ref,
    own_rim_ref,
    other_rim_ref,
    packed_ref,
    scale_ref,
    output_ref,
    gain_ref,
    offset_ref,
    merge_ref,
    merge_gain_ref,
    merge_offset_ref,
    hot_ref,
    shut_ref,
    index_a_ref,
    index_b_ref,
    patch_ref,
    *rest,
):
    if with_edges:
        near_ref, edge_ref, merged_ref, up_ref, down_ref, own, other, ctx_ref, first_ref = rest
    else:
        merged_ref, own, other, ctx_ref, first_ref = rest
    chunks = own_ref.shape[0]
    for dst, src, rim in ((own, own_ref, own_rim_ref), (other, other_ref, other_rim_ref)):
        dst[0] = rim[0]
        dst[1 : chunks + 1] = src[...]
        dst[chunks + 1] = rim[1]
    windows = (chunks + 2) // 2
    tokens = own_ref.shape[1]
    pick_a = one_hot(index_a_ref[...], tokens)
    pick_b = one_hot(index_b_ref[...], tokens)

    @pl.loop(0, windows)
    def _(w):
        wrap = jnp.where(w == 0, flags[0], jnp.where(w == windows - 1, flags[1], 0))
        mine = mm(pick_a, own[2 * w]) + mm(pick_b, own[2 * w + 1])
        theirs = mm(pick_a, other[2 * w]) + mm(pick_b, other[2 * w + 1])
        window_context(
            mine.astype(jnp.bfloat16),
            theirs.astype(jnp.bfloat16),
            packed_ref,
            scale_ref[...],
            wrap,
            hot_ref,
            shut_ref,
            ctx_ref,
        )
        branch = layer_norm(mm(ctx_ref[...], output_ref[...]), gain_ref[...], offset_ref[...])
        first_ref[w] = (mine + branch).astype(jnp.bfloat16)

    first = first_ref[...].reshape(-1, first_ref.shape[-1])
    channels = first.shape[1]
    total = None
    for g in range(4):
        part = mm(one_hot(patch_ref[g], first.shape[0]), first).astype(jnp.bfloat16)
        term = mm(part, merge_ref[g * channels : (g + 1) * channels])
        total = term if total is None else total + term
    merged = layer_norm(total, merge_gain_ref[...], merge_offset_ref[...]).astype(jnp.bfloat16)
    merged_ref[...] = merged
    if with_edges:
        for end, dst in ((0, up_ref), (1, down_ref)):
            dst[...] = (
                mm(one_hot(edge_ref[end, 0], merged.shape[0]), near_ref[...])
                + mm(one_hot(edge_ref[end, 1], merged.shape[0]), merged)
            ).astype(jnp.bfloat16)


def second_kernel(
    flags,
    near_ref,
    far_ref,
    rim_ref,
    other_near_ref,
    other_far_ref,
    other_rim_ref,
    packed_ref,
    scale_ref,
    output_ref,
    gain_ref,
    offset_ref,
    hot_ref,
    shut_ref,
    coarse_ref,
    final_ref,
    keep_ref,
    send_ref,
    ctx_ref,
    second_ref,
):
    windows, span, _ = second_ref.shape

    @pl.loop(0, windows)
    def _(w):
        wrap = jnp.where(w == 0, flags[0], jnp.where(w == windows - 1, flags[1], 0))
        rows = pl.ds(pl.multiple_of(w * span, 8), span)
        pick = [one_hot(coarse_ref[s, rows], near_ref.shape[0]) for s in range(3)]
        mine = mm(pick[0], near_ref[...]) + mm(pick[1], far_ref[...]) + mm(pick[2], rim_ref[...])
        theirs = (
            mm(pick[0], other_near_ref[...])
            + mm(pick[1], other_far_ref[...])
            + mm(pick[2], other_rim_ref[...])
        )
        window_context(
            mine.astype(jnp.bfloat16),
            theirs.astype(jnp.bfloat16),
            packed_ref,
            scale_ref[...],
            wrap,
            hot_ref,
            shut_ref,
            ctx_ref,
        )
        branch = layer_norm(mm(ctx_ref[...], output_ref[...]), gain_ref[...], offset_ref[...])
        second_ref[w] = (mine + branch).astype(jnp.bfloat16)

    second = second_ref[...].reshape(windows * span, -1)
    keep_ref[...] = mm(one_hot(final_ref[0], windows * span), second).astype(jnp.bfloat16)
    send_ref[...] = mm(one_hot(final_ref[1], windows * span), second).astype(jnp.bfloat16)


def call(kernel, outs, scratch, operands):
    vmem = pl.BlockSpec(memory_space=pltpu.VMEM)
    return pl.pallas_call(
        kernel,
        out_shape=outs,
        in_specs=[pl.BlockSpec(memory_space=pltpu.SMEM)] + [vmem] * (len(operands) - 1),
        out_specs=[vmem] * len(outs),
        scratch_shapes=scratch,
    )(*operands)


def near_swap(value):
    return lax.ppermute(value, "lon", [(i, i ^ 1) for i in range(lax.axis_size("lon"))])


def far_swap(value):
    n = lax.axis_size("lon")
    return lax.ppermute(value, "lon", [(i, (i + (1 if i % 2 else -1)) % n) for i in range(n)])


def up(value):
    return lax.ppermute(value, "lat", [(i, i - 1) for i in range(1, lax.axis_size("lat"))])


def down(value):
    return lax.ppermute(value, "lat", [(i, i + 1) for i in range(lax.axis_size("lat") - 1)])


def lane_scale(scales, head):
    return jnp.repeat(scales * math.log2(math.e), head)[None]


def body(
    features,
    packed_first,
    scale_first,
    output_first,
    gain_first,
    offset_first,
    merge_weight,
    merge_gain,
    merge_offset,
    packed_second,
    scale_second,
    output_second,
    gain_second,
    offset_second,
):
    levels, row_count, col_count, channels = features.shape
    inner = packed_first.shape[1] // 3
    second_inner = packed_second.shape[1] // 3
    wide = merge_weight.shape[1]
    half_rows = row_count // 2
    lat_pos = lax.axis_index("lat")
    is_even = lax.axis_index("lon") % 2 == 0
    flags = jnp.stack([lat_pos == 0, lat_pos == lax.axis_size("lat") - 1]).astype(jnp.int32)
    bf16 = jnp.bfloat16
    span = levels // WLEV * GROUP
    tokens = HALF_LAT * levels * HALF_LON
    chunks = row_count // HALF_LAT

    turned = jnp.transpose(features, (1, 0, 2, 3))
    left, right = turned[:, :, :HALF_LON], turned[:, :, HALF_LON:]
    near = jnp.where(is_even, right, left).reshape(chunks, tokens, channels)
    far = jnp.where(is_even, left, right).reshape(chunks, tokens, channels)

    far_other = far_swap(far)
    near_other = near_swap(near)
    bottom = up(jnp.stack([near[0], far[0]]))
    top = down(jnp.stack([near[-1], far[-1]]))
    near_rim = jnp.stack([top[0], bottom[0]])
    far_rim = jnp.stack([top[1], bottom[1]])
    near_other_rim = near_swap(near_rim)
    far_other_rim = far_swap(far_rim)

    hot, shut = aux_tables(levels)
    hot, shut = jnp.asarray(hot, bf16), jnp.asarray(shut, bf16)
    index_a, index_b = fine_gather(levels)
    head = inner // scale_first.shape[0]
    shared = [
        packed_first,
        lane_scale(scale_first, head),
        output_first,
        gain_first[None],
        offset_first[None],
        merge_weight,
        merge_gain[None],
        merge_offset[None],
        hot,
        shut,
        jnp.asarray(index_a),
        jnp.asarray(index_b),
        jnp.asarray(patch_gather(levels, row_count)),
    ]
    cells = half_rows * levels * HALF_LON // 2
    small = jax.ShapeDtypeStruct((cells, wide), bf16)
    edge = jax.ShapeDtypeStruct((HALF_LAT * levels * HALF_LON, wide), bf16)
    scratch = [
        pltpu.VMEM((chunks + 2, tokens, channels), bf16),
        pltpu.VMEM((chunks + 2, tokens, channels), bf16),
        pltpu.VMEM((span, inner), bf16),
        pltpu.VMEM(((chunks + 2) // 2, span, channels), bf16),
    ]
    (merged_near,) = call(
        functools.partial(side_kernel, False),
        [small],
        scratch,
        [flags, near, near_other, near_rim, near_other_rim] + shared,
    )
    merged_far, edge_up, edge_down = call(
        functools.partial(side_kernel, True),
        [small, edge, edge],
        scratch,
        [flags, far, far_other, far_rim, far_other_rim]
        + shared
        + [merged_near, jnp.asarray(edge_gather(levels, half_rows))],
    )
    other_near = far_swap(merged_near)
    other_far = far_swap(merged_far)
    bottom = up(edge_up)
    top = down(edge_down)
    rim = jnp.concatenate([top, bottom])
    other_rim = far_swap(rim)

    finals = jnp.where(
        is_even,
        jnp.asarray(final_gather(levels, half_rows, True)),
        jnp.asarray(final_gather(levels, half_rows, False)),
    )
    windows = (half_rows // HALF_LAT + 2) // 2
    share = jax.ShapeDtypeStruct((half_rows * levels // 2 * HALF_LON, wide), bf16)
    keep, send = call(
        second_kernel,
        [share, share],
        [pltpu.VMEM((span, second_inner), bf16), pltpu.VMEM((windows, span, wide), bf16)],
        [
            flags,
            merged_near,
            merged_far,
            rim,
            other_near,
            other_far,
            other_rim,
            packed_second,
            lane_scale(scale_second, second_inner // scale_second.shape[0]),
            output_second,
            gain_second[None],
            offset_second[None],
            hot,
            shut,
            jnp.asarray(coarse_gather(levels, half_rows)),
            finals,
        ],
    )
    received = near_swap(send)
    shape = (half_rows, levels // 2, HALF_LON, wide)
    keep, received = keep.reshape(shape), received.reshape(shape)
    out = jnp.where(
        is_even,
        jnp.concatenate([keep, received], axis=2),
        jnp.concatenate([received, keep], axis=2),
    )
    return out[:, None]


def solution(mesh):
    return jax.shard_map(
        body,
        mesh=mesh,
        in_specs=(P(None, "lat", "lon", None),) + (P(),) * 13,
        out_specs=P("lat", "lon", None, None, None),
        check_vma=False,
    )
```

time: 184 us -> 133 us (0.72); the launches traced: 181 us -> 133 us
  Pallas kernels: 0 us -> 77.4 us
  local copies, waits for them, and re-layouts: 62.1 us -> 9.3 us
  waiting for transfers between devices: 50.2 us -> 19.6 us
  matrix products: 27.9 us -> 0 us
  other arithmetic: 25.1 us -> 3.8 us
  starting transfers between devices: 14.3 us -> 22.7 us
    pallas_call x0 -> x3, Pallas kernels: none -> 77.4 us  [call(): pl.pallas_call(kernel, out_shape=outs, in_specs=[pl.BlockSpec(memory_spac...]
    ppermute x11 -> x12, waiting for transfers between devices: 50.2 us -> 19.6 us  [the longest x5 14.3 us: far_swap(): lax.ppermute(value, 'lon', [(i, (i + (1 if i % 2 else -1)) % n) for i in...]
    dot_general x12 -> x0, matrix products: 27.9 us -> none  [the longest x4 11.7 us: project(): jnp.dot(windows.reshape(-1, windows.shape[-1]), weight, preferred_element...]
    convert_element_type x9 -> x0, local copies, waits for them, and re-layouts: 17 us -> none  [the longest x5 9.97 us: unit_heads(): shaped = tensor_in.reshape(tensor_in.shape[:-1] + (head_count, tensor_in....]
    reshape x8 -> x2, local copies, waits for them, and re-layouts: 14.3 us -> 0.39 us  [the longest x1 0.2 us: body(): near = jnp.where(is_even, right, left).reshape(chunks, tokens, channels)]
    convert_element_type x8 -> x1, other arithmetic: 9.59 us -> 0.59 us  [body(): jnp.stack([lat_pos == 0, lat_pos == lax.axis_size('lat') - 1])]
    ppermute x11 -> x12, starting transfers between devices: 14.3 us -> 22.7 us  [the longest x5 10.7 us: far_swap(): lax.ppermute(value, 'lon', [(i, (i + (1 if i % 2 else -1)) % n) for i in...]
    slice x11, local copies, waits for them, and re-layouts: 9.49 us -> 1.32 us  [the longest x2 0.94 us: body(): far_rim = jnp.stack([top[1], bottom[1]])]
  transfers between devices with their start and end apart: 11 -> 12, of which waited for: 11 -> 5; matrix products, arithmetic and copies ran while one was open for 4% -> 5% of each run, Pallas kernels for 0% -> 21%
where the time goes in v1:
time: 133 us
  Pallas kernels  77.4 us (58%)
  starting transfers between devices  22.7 us (17%)
  waiting for transfers between devices  19.6 us (15%)
  local copies, waits for them, and re-layouts  9.3 us (7%)
  other arithmetic  3.8 us (3%)
    pallas_call x3, Pallas kernels, call(): pl.pallas_call(kernel, out_shape=outs, in_specs=[pl.BlockSpec(memory_spac...  77.4 us
    ppermute x5, waiting for transfers between devices, far_swap(): lax.ppermute(value, 'lon', [(i, (i + (1 if i % 2 else -1)) % n) for i in...  14.3 us
    ppermute x5, starting transfers between devices, far_swap(): lax.ppermute(value, 'lon', [(i, (i + (1 if i % 2 else -1)) % n) for i in...  10.7 us
    ppermute x2, starting transfers between devices, down(): lax.ppermute(value, 'lat', [(i, i + 1) for i in range(lax.axis_size('lat'...  9.17 us
    ppermute x2, waiting for transfers between devices, up(): lax.ppermute(value, 'lat', [(i, i - 1) for i in range(1, lax.axis_size('l...  4.52 us
    unnamed x35, local copies, waits for them, and re-layouts  3.13 us
    ppermute x2, starting transfers between devices, up(): lax.ppermute(value, 'lat', [(i, i - 1) for i in range(1, lax.axis_size('l...  2.75 us
  transfers between devices with their start and end apart: 12, of which 5 were waited for; matrix products, arithmetic and copies ran while one was open for 5% of the time, Pallas kernels for 21%

profile of v1, /device:TPU:0, one launch (start us, length us, event | category | flops | bytes accessed | tf_op | source)
XLA Modules:
  0.0 133.2 jit_solution(17934953696624623160)
XLA Ops:
  0.0 1.3 broadcast_select_fusion
  1.7 4.9 %collective-permute-start.1 = (bf16[2,72,512]{2,1,0:T(8,128)(2,1)S(1)}, bf16[2,72,512]{2,1,0:T(8,128)(2,1)S(1)}, u32[]{:S(2)}, u32[]{:S(2)}) collective-permute-start(bf16[2,72,512]{2,1,0:T(8,128)(2,1)S(1)} %pad_maximum_fusion), channel_id=1, source_target_pairs={{0,8},{8,16},{16,24},{1,9},{9,17},{17,25},{2,10},{10,18},{18,26},{... | collective-permute-start | bytes 442376 | tf_op jit(solution)/shard_map/ppermute | solution.py:371
  6.7 0.7 pad_maximum_fusion.1
  7.4 1.3 collective-permute-start.2
  9.6 3.8 %collective-permute-start.4 = (bf16[8,72,512]{2,1,0:T(8,128)(2,1)S(1)}, bf16[8,72,512]{2,1,0:T(8,128)(2,1)S(1)}, u32[]{:S(2)}, u32[]{:S(2)}) collective-permute-start(bf16[8,72,512]{2,1,0:T(8,128)(2,1)S(1)} %reshape.72.own_ref), channel_id=1, source_target_pairs={{0,7},{1,2},{2,1},{3,4},{4,3},{5,6},{6,5},{7,0},{8,15},{9,10},{10,... | collective-permute-start | bytes 1769480 | tf_op jit(solution)/shard_map/ppermute | solution.py:363
  13.4 1.5 %collective-permute-done.2 = bf16[2,72,512]{2,1,0:T(8,128)(2,1)} collective-permute-done((bf16[2,72,512]{2,1,0:T(8,128)(2,1)}, bf16[2,72,512]{2,1,0:T(8,128)(2,1)}, u32[]{:S(2)}, u32[]{:S(2)}) %collective-permute-start.2) | collective-permute-done | bytes 147488 | tf_op jit(solution)/shard_map/ppermute | solution.py:367
  14.9 0.9 fusion.3
  15.8 2.0 %collective-permute-start.5 = (bf16[2,72,512]{2,1,0:T(8,128)(2,1)S(1)}, bf16[2,72,512]{2,1,0:T(8,128)(2,1)S(1)}, u32[]{:S(2)}, u32[]{:S(2)}) collective-permute-start(bf16[2,72,512]{2,1,0:T(8,128)(2,1)S(1)} %pad_maximum_fusion.3.own_rim_ref), channel_id=1, source_target_pairs={{0,7},{1,2},{2,1},{3,4},{4,3},{5,6},{6,5},{7,0},{8,15},{9,10},{10,... | collective-permute-start | bytes 442376 | tf_op jit(solution)/shard_map/ppermute | solution.py:363
  20.2 28.3 %shard_map.217.rest_0_.near_ref = bf16[144,1024]{1,0:T(8,128)(2,1)} custom-call(s32[2]{0:T(128)} %add_convert_fusion.flags, bf16[8,72,512]{2,1,0:T(8,128)(2,1)} %copy-done.2, bf16[8,72,512]{2,1,0:T(8,128)(2,1)} %copy-done.5, bf16[2,72,512]{2,1,0:T(8,128)(2,1)} %copy-done.7, bf16[2,72,512]{2,1,0:T(8,128)(2,1)} %copy-done.14, bf16[512,1536]{1,0:T(8,128)(2,1)} %packed_ref.4, ...), custom_call_target="tpu_custom_call" | custom-call | tf_op jit(solution)/shard_map/pallas_call | solution.py:348
  49.3 0.8 copy-done.4
  50.1 28.6 %shard_map.218 = (bf16[144,1024]{1,0:T(8,128)(2,1)}, bf16[72,1024]{1,0:T(8,128)(2,1)}, bf16[72,1024]{1,0:T(8,128)(2,1)}) custom-call(s32[2]{0:T(128)} %add_convert_fusion.flags, bf16[8,72,512]{2,1,0:T(8,128)(2,1)} %copy-done.1, bf16[8,72,512]{2,1,0:T(8,128)(2,1)} %copy-done.4, bf16[2,72,512]{2,1,0:T(8,128)(2,1)} %copy-done.6, ...), custom_call_target="tpu_custom_call" | custom-call | tf_op jit(solution)/shard_map/pallas_call | solution.py:348
  78.7 4.3 %collective-permute-start.6 = (bf16[72,1024]{1,0:T(8,128)(2,1)}, bf16[72,1024]{1,0:T(8,128)(2,1)S(1)}, u32[]{:S(2)}, u32[]{:S(2)}) collective-permute-start(bf16[72,1024]{1,0:T(8,128)(2,1)} %get-tuple-element.11), channel_id=1, source_target_pairs={{0,8},{8,16},{16,24},{1,9},{9,17},{17,25},{2,10},{10,18},{18,26},{... | collective-permute-start | bytes 442376 | tf_op jit(solution)/shard_map/ppermute | solution.py:371
  83.0 1.5 %collective-permute-start.7 = (bf16[72,1024]{1,0:T(8,128)(2,1)}, bf16[72,1024]{1,0:T(8,128)(2,1)S(1)}, u32[]{:S(2)}, u32[]{:S(2)}) collective-permute-start(bf16[72,1024]{1,0:T(8,128)(2,1)} %get-tuple-element.12), channel_id=1, source_target_pairs={{8,0},{16,8},{24,16},{9,1},{17,9},{25,17},{10,2},{18,10},{26,18},{... | collective-permute-start | bytes 442376 | tf_op jit(solution)/shard_map/ppermute | solution.py:367
  84.5 1.6 %collective-permute-start.8 = (bf16[144,1024]{1,0:T(8,128)(2,1)S(1)}, bf16[144,1024]{1,0:T(8,128)(2,1)S(1)}, u32[]{:S(2)}, u32[]{:S(2)}) collective-permute-start(bf16[144,1024]{1,0:T(8,128)(2,1)S(1)} %copy-done), channel_id=1, source_target_pairs={{0,7},{1,2},{2,1},{3,4},{4,3},{5,6},{6,5},{7,0},{8,15},{9,10},{10,... | collective-permute-start | bytes 884744 | tf_op jit(solution)/shard_map/ppermute | solution.py:363
  86.1 2.0 %collective-permute-start.9 = (bf16[144,1024]{1,0:T(8,128)(2,1)}, bf16[144,1024]{1,0:T(8,128)(2,1)S(1)}, u32[]{:S(2)}, u32[]{:S(2)}) collective-permute-start(bf16[144,1024]{1,0:T(8,128)(2,1)} %get-tuple-element.10.far_ref), channel_id=1, source_target_pairs={{0,7},{1,2},{2,1},{3,4},{4,3},{5,6},{6,5},{7,0},{8,15},{9,10},{10,... | collective-permute-start | bytes 884744 | tf_op jit(solution)/shard_map/ppermute | solution.py:363
  88.1 3.0 %collective-permute-done.7 = bf16[72,1024]{1,0:T(8,128)(2,1)S(1)} collective-permute-done((bf16[72,1024]{1,0:T(8,128)(2,1)}, bf16[72,1024]{1,0:T(8,128)(2,1)S(1)}, u32[]{:S(2)}, u32[]{:S(2)}) %collective-permute-start.7) | collective-permute-done | bytes 147488 | tf_op jit(solution)/shard_map/ppermute | solution.py:367
  91.2 1.3 collective-permute-start.10
  93.9 8.1 %collective-permute-done.9.other_far_ref = bf16[144,1024]{1,0:T(8,128)(2,1)S(1)} collective-permute-done((bf16[144,1024]{1,0:T(8,128)(2,1)}, bf16[144,1024]{1,0:T(8,128)(2,1)S(1)}, u32[]{:S(2)}, u32[]{:S(2)}) %collective-permute-start.9) | collective-permute-done | bytes 294944 | tf_op jit(solution)/shard_map/ppermute | solution.py:363
  102.0 6.2 %collective-permute-done.10.other_rim_ref = bf16[144,1024]{1,0:T(8,128)(2,1)S(1)} collective-permute-done((bf16[144,1024]{1,0:T(8,128)(2,1)S(1)}, bf16[144,1024]{1,0:T(8,128)(2,1)S(1)}, u32[]{:S(2)}, u32[]{:S(2)}) %collective-permute-start.10) | collective-permute-done | bytes 294944 | tf_op jit(solution)/shard_map/ppermute | solution.py:363
  108.3 0.7 copy-done.10
  109.0 20.4 %shard_map.219 = (bf16[144,1024]{1,0:T(8,128)(2,1)}, bf16[144,1024]{1,0:T(8,128)(2,1)}) custom-call(s32[2]{0:T(128)} %add_convert_fusion.flags, bf16[144,1024]{1,0:T(8,128)(2,1)} %shard_map.217.rest_0_.near_ref, bf16[144,1024]{1,0:T(8,128)(2,1)} %get-tuple-element.10.far_ref, bf16[144,1024]{1,0:T(8,128)(2,1)} %copy-done.3, bf16[144,1024]{1,0:T(8,128)(2,1)} %copy-done.8, ...), custom_call_target="tpu_custom_call" | custom-call | tf_op jit(solution)/shard_map/pallas_call | solution.py:348
  129.4 1.1 concatenate.28
  130.4 0.7 collective-permute-done.11
  131.8 1.4 %copy.40 = bf16[12,1,2,12,1024]{4,2,3,1,0:T(2,128)(2,1)} copy(bf16[12,1,2,12,1024]{4,3,2,0,1:T(8,128)(2,1)S(1)} %maximum_select_fusion) | data formatting | bytes 1179648 | tf_op jit(solution)/shard_map/jit(_where)/select_n | solution.py:503
  (71 shorter events, 6.3 us)
Async XLA Ops:
  1.7 11.7 %collective-permute-start.1 = (bf16[2,72,512]{2,1,0:T(8,128)(2,1)S(1)}, bf16[2,72,512]{2,1,0:T(8,128)(2,1)S(1)}, u32[]{:S(2)}, u32[]{:S(2)}) collective-permute-start(bf16[2,72,512]{2,1,0:T(8,128)(2,1)S(1)} %pad_maximum_fusion), channel_id=1, source_target_pairs={{0,8},{8,16},{16,24},{1,9},{9,17},{17,25},{2,10},{10,18},{18,26},{... | collective-permute-start | bytes 442376 | tf_op jit(solution)/shard_map/ppermute | solution.py:371
  7.4 7.5 %collective-permute-start.2 = (bf16[2,72,512]{2,1,0:T(8,128)(2,1)}, bf16[2,72,512]{2,1,0:T(8,128)(2,1)}, u32[]{:S(2)}, u32[]{:S(2)}) collective-permute-start(bf16[2,72,512]{2,1,0:T(8,128)(2,1)} %pad_maximum_fusion.1), channel_id=1, source_target_pairs={{8,0},{16,8},{24,16},{9,1},{17,9},{25,17},{10,2},{18,10},{26,18},{... | collective-permute-start | bytes 442376 | tf_op jit(solution)/shard_map/ppermute | solution.py:367
  9.1 6.7 %copy-start.2 = (bf16[8,72,512]{2,1,0:T(8,128)(2,1)}, bf16[8,72,512]{2,1,0:T(8,128)(2,1)S(1)}, u32[]{:S(2)}) copy-start(bf16[8,72,512]{2,1,0:T(8,128)(2,1)S(1)} %reshape.71.own_ref) | copy-start | bytes 1769476
  9.1 10.2 %collective-permute-start = (bf16[8,72,512]{2,1,0:T(8,128)(2,1)S(1)}, bf16[8,72,512]{2,1,0:T(8,128)(2,1)S(1)}, u32[]{:S(2)}, u32[]{:S(2)}) collective-permute-start(bf16[8,72,512]{2,1,0:T(8,128)(2,1)S(1)} %reshape.71.own_ref), channel_id=1, source_target_pairs={{0,1},{1,0},{2,3},{3,2},{4,5},{5,4},{6,7},{7,6},{8,9},{9,8},{10,11... | collective-permute-start | bytes 1769480 | tf_op jit(solution)/shard_map/ppermute | solution.py:358
  9.4 8.6 %copy-start.15 = (f32[8]{0:T(128)S(1)}, f32[8]{0:T(128)}, u32[]{:S(2)}) copy-start(f32[8]{0:T(128)} %param.25) | copy-start | bytes 100
  9.6 39.0 %copy-start.1 = (bf16[8,72,512]{2,1,0:T(8,128)(2,1)}, bf16[8,72,512]{2,1,0:T(8,128)(2,1)S(1)}, u32[]{:S(2)}) copy-start(bf16[8,72,512]{2,1,0:T(8,128)(2,1)S(1)} %reshape.72.own_ref) | copy-start | bytes 1769476
  9.6 39.1 %collective-permute-start.4 = (bf16[8,72,512]{2,1,0:T(8,128)(2,1)S(1)}, bf16[8,72,512]{2,1,0:T(8,128)(2,1)S(1)}, u32[]{:S(2)}, u32[]{:S(2)}) collective-permute-start(bf16[8,72,512]{2,1,0:T(8,128)(2,1)S(1)} %reshape.72.own_ref), channel_id=1, source_target_pairs={{0,7},{1,2},{2,1},{3,4},{4,3},{5,6},{6,5},{7,0},{8,15},{9,10},{10,... | collective-permute-start | bytes 1769480 | tf_op jit(solution)/shard_map/ppermute | solution.py:363
  15.8 32.7 %copy-start.6 = (bf16[2,72,512]{2,1,0:T(8,128)(2,1)}, bf16[2,72,512]{2,1,0:T(8,128)(2,1)S(1)}, u32[]{:S(2)}) copy-start(bf16[2,72,512]{2,1,0:T(8,128)(2,1)S(1)} %pad_maximum_fusion.3.own_rim_ref) | copy-start | bytes 442372
  15.8 32.8 %collective-permute-start.5 = (bf16[2,72,512]{2,1,0:T(8,128)(2,1)S(1)}, bf16[2,72,512]{2,1,0:T(8,128)(2,1)S(1)}, u32[]{:S(2)}, u32[]{:S(2)}) collective-permute-start(bf16[2,72,512]{2,1,0:T(8,128)(2,1)S(1)} %pad_maximum_fusion.3.own_rim_ref), channel_id=1, source_target_pairs={{0,7},{1,2},{2,1},{3,4},{4,3},{5,6},{6,5},{7,0},{8,15},{9,10},{10,... | collective-permute-start | bytes 442376 | tf_op jit(solution)/shard_map/ppermute | solution.py:363
  17.8 1.5 %copy-start.7 = (bf16[2,72,512]{2,1,0:T(8,128)(2,1)}, bf16[2,72,512]{2,1,0:T(8,128)(2,1)S(1)}, u32[]{:S(2)}) copy-start(bf16[2,72,512]{2,1,0:T(8,128)(2,1)S(1)} %pad_maximum_fusion.2.own_rim_ref) | copy-start | bytes 442372
  17.8 1.4 %collective-permute-start.3 = (bf16[2,72,512]{2,1,0:T(8,128)(2,1)S(1)}, bf16[2,72,512]{2,1,0:T(8,128)(2,1)S(1)}, u32[]{:S(2)}, u32[]{:S(2)}) collective-permute-start(bf16[2,72,512]{2,1,0:T(8,128)(2,1)S(1)} %pad_maximum_fusion.2.own_rim_ref), channel_id=1, source_target_pairs={{0,1},{1,0},{2,3},{3,2},{4,5},{5,4},{6,7},{7,6},{8,9},{9,8},{10,11... | collective-permute-start | bytes 442376 | tf_op jit(solution)/shard_map/ppermute | solution.py:358
  48.6 35.9 %copy-start = (bf16[144,1024]{1,0:T(8,128)(2,1)S(1)}, bf16[144,1024]{1,0:T(8,128)(2,1)}, u32[]{:S(2)}) copy-start(bf16[144,1024]{1,0:T(8,128)(2,1)} %shard_map.217.rest_0_.near_ref) | copy-start | bytes 884740
  48.6 43.9 %copy-start.16 = (f32[8]{0:T(128)S(1)}, f32[8]{0:T(128)}, u32[]{:S(2)}) copy-start(f32[8]{0:T(128)} %param.33) | copy-start | bytes 100
  48.6 44.7 %copy-start.11 = (s32[2,144,1]{2,1,0:T(8,128)S(1)}, s32[2,144,1]{2,1,0:T(8,128)}, u32[]{:S(2)}) copy-start(s32[2,144,1]{2,1,0:T(8,128)} %constant.50.clone) | copy-start | bytes 3460
  48.6 44.7 %copy-start.12 = (s32[2,144,1]{2,1,0:T(8,128)S(1)}, s32[2,144,1]{2,1,0:T(8,128)}, u32[]{:S(2)}) copy-start(s32[2,144,1]{2,1,0:T(8,128)} %constant.51.clone) | copy-start | bytes 3460
  78.7 9.4 %collective-permute-start.6 = (bf16[72,1024]{1,0:T(8,128)(2,1)}, bf16[72,1024]{1,0:T(8,128)(2,1)S(1)}, u32[]{:S(2)}, u32[]{:S(2)}) collective-permute-start(bf16[72,1024]{1,0:T(8,128)(2,1)} %get-tuple-element.11), channel_id=1, source_target_pairs={{0,8},{8,16},{16,24},{1,9},{9,17},{17,25},{2,10},{10,18},{18,26},{... | collective-permute-start | bytes 442376 | tf_op jit(solution)/shard_map/ppermute | solution.py:371
  83.0 8.1 %collective-permute-start.7 = (bf16[72,1024]{1,0:T(8,128)(2,1)}, bf16[72,1024]{1,0:T(8,128)(2,1)S(1)}, u32[]{:S(2)}, u32[]{:S(2)}) collective-permute-start(bf16[72,1024]{1,0:T(8,128)(2,1)} %get-tuple-element.12), channel_id=1, source_target_pairs={{8,0},{16,8},{24,16},{9,1},{17,9},{25,17},{10,2},{18,10},{26,18},{... | collective-permute-start | bytes 442376 | tf_op jit(solution)/shard_map/ppermute | solution.py:367
  84.5 17.5 %collective-permute-start.8 = (bf16[144,1024]{1,0:T(8,128)(2,1)S(1)}, bf16[144,1024]{1,0:T(8,128)(2,1)S(1)}, u32[]{:S(2)}, u32[]{:S(2)}) collective-permute-start(bf16[144,1024]{1,0:T(8,128)(2,1)S(1)} %copy-done), channel_id=1, source_target_pairs={{0,7},{1,2},{2,1},{3,4},{4,3},{5,6},{6,5},{7,0},{8,15},{9,10},{10,... | collective-permute-start | bytes 884744 | tf_op jit(solution)/shard_map/ppermute | solution.py:363
  86.1 15.9 %collective-permute-start.9 = (bf16[144,1024]{1,0:T(8,128)(2,1)}, bf16[144,1024]{1,0:T(8,128)(2,1)S(1)}, u32[]{:S(2)}, u32[]{:S(2)}) collective-permute-start(bf16[144,1024]{1,0:T(8,128)(2,1)} %get-tuple-element.10.far_ref), channel_id=1, source_target_pairs={{0,7},{1,2},{2,1},{3,4},{4,3},{5,6},{6,5},{7,0},{8,15},{9,10},{10,... | collective-permute-start | bytes 884744 | tf_op jit(solution)/shard_map/ppermute | solution.py:363
  91.2 17.1 %copy-start.3 = (bf16[144,1024]{1,0:T(8,128)(2,1)}, bf16[144,1024]{1,0:T(8,128)(2,1)S(1)}, u32[]{:S(2)}) copy-start(bf16[144,1024]{1,0:T(8,128)(2,1)S(1)} %constant_dynamic-update-slice_fusion.rim_ref) | copy-start | bytes 884740
  91.2 17.1 %collective-permute-start.10 = (bf16[144,1024]{1,0:T(8,128)(2,1)S(1)}, bf16[144,1024]{1,0:T(8,128)(2,1)S(1)}, u32[]{:S(2)}, u32[]{:S(2)}) collective-permute-start(bf16[144,1024]{1,0:T(8,128)(2,1)S(1)} %constant_dynamic-update-slice_fusion.rim_ref), channel_id=1, source_target_pairs={{0,7},{1,2},{2,1},{3,4},{4,3},{5,6},{6,5},{7,0},{8,15},{9,10},{10,... | collective-permute-start | bytes 884744 | tf_op jit(solution)/shard_map/ppermute | solution.py:363
  102.0 6.2 %copy-start.9 = (bf16[144,1024]{1,0:T(8,128)(2,1)}, bf16[144,1024]{1,0:T(8,128)(2,1)S(1)}, u32[]{:S(2)}) copy-start(bf16[144,1024]{1,0:T(8,128)(2,1)S(1)} %collective-permute-done.9.other_far_ref) | copy-start | bytes 884740
  102.0 6.2 %copy-start.8 = (bf16[144,1024]{1,0:T(8,128)(2,1)}, bf16[144,1024]{1,0:T(8,128)(2,1)S(1)}, u32[]{:S(2)}) copy-start(bf16[144,1024]{1,0:T(8,128)(2,1)S(1)} %collective-permute-done.8.other_near_ref) | copy-start | bytes 884740
  129.4 1.8 %collective-permute-start.11 = (bf16[144,1024]{1,0:T(8,128)(2,1)}, bf16[144,1024]{1,0:T(8,128)(2,1)S(1)}, u32[]{:S(2)}, u32[]{:S(2)}) collective-permute-start(bf16[144,1024]{1,0:T(8,128)(2,1)} %get-tuple-element.14), channel_id=1, source_target_pairs={{0,1},{1,0},{2,3},{3,2},{4,5},{5,4},{6,7},{7,6},{8,9},{9,8},{10,11... | collective-permute-start | bytes 884744 | tf_op jit(solution)/shard_map/ppermute | solution.py:358
  (5 other events, 3.8 us)

commit v2 on v1

v2 whole, which is shorter than its diff:
```python
import math

import jax
import jax.numpy as jnp
import numpy as np
from jax import lax
from jax.experimental import pallas as pl
from jax.experimental.pallas import tpu as pltpu
from jax.sharding import PartitionSpec as P

WLEV = 2
WLAT = 6
WLON = 12
HALF_LAT = WLAT // 2
HALF_LON = WLON // 2
LANES = 128

norm_eps = 1e-05
unit_eps = 1e-06

PART = WLEV * HALF_LAT * HALF_LON
GROUP = -(-2 * PART // 16) * 16


def rolled_levels(levels):
    return [(l + WLEV // 2) % levels for l in range(levels)]


def window_slots(levels):
    order = rolled_levels(levels)
    for place, level in enumerate(order):
        pair, lev = divmod(place, WLEV)
        for side in range(2):
            for i in range(HALF_LAT):
                for c in range(HALF_LON):
                    t = (i * WLEV + lev) * HALF_LON + c
                    yield pair * GROUP + side * PART + t, side, level, i, c


def slot_table(levels):
    table = {}
    for row, side, level, i, c in window_slots(levels):
        table[(side, level, i, c)] = row
    return table


def column(values):
    return np.asarray(values, np.int32).reshape(-1, 1)


def fine_gather(levels):
    rows = levels // WLEV * GROUP
    out = [np.full(rows, -1), np.full(rows, -1)]
    for row, side, level, i, c in window_slots(levels):
        out[side][row] = (i * levels + level) * HALF_LON + c
    return column(out[0]), column(out[1])


def patch_gather(levels, row_count):
    span = levels // WLEV * GROUP
    slots = slot_table(levels)
    out = []
    for g in range(4):
        dc, dr = divmod(g, 2)
        rows = []
        for i in range(row_count // 2):
            for level in range(levels):
                for cc in range(HALF_LON // 2):
                    r = 2 * i + dr
                    chunk = r // HALF_LAT + 1
                    w, side = divmod(chunk, 2)
                    rows.append(w * span + slots[(side, level, r % HALF_LAT, 2 * cc + dc)])
        out.append(column(rows))
    return np.concatenate(out)


def coarse_gather(levels, row_count):
    span = levels // WLEV * GROUP
    chunks = row_count // HALF_LAT
    third = HALF_LON // 2
    small = HALF_LAT * levels * third
    out = np.full((3, chunks // 2 * span, 1), -(1 << 20), np.int32)
    for w in range(chunks // 2):
        for row, side, level, i, c in window_slots(levels):
            chunk = 2 * w + side + 1
            which, cc = divmod(c, third)
            cell = (i * levels + level) * third + cc
            at = w * span + row
            if chunk < chunks:
                low = coarse_reach(w, small, chunks * small)[0]
                out[which, at, 0] = chunk * small + cell - low
            else:
                out[2, at, 0] = which * small + cell
    return out


def coarse_reach(w, small, count):
    return (2 * w + 1) * small // 16 * 16, min(padded((2 * w + 3) * small), count)


def edge_gather(levels):
    small = HALF_LAT * levels * HALF_LON // 2
    out = np.full((2, 2 * small, 1), -1, np.int32)
    for which in range(2):
        out[which, which * small : (which + 1) * small, 0] = np.arange(small)
    return out


def coarse_slot(levels, even, r, level, c):
    third = HALF_LON // 2
    place = (c + third) % HALF_LON if even else c
    w, side = divmod(r // HALF_LAT - 1, 2)
    return w * (levels // WLEV * GROUP) + slot_table(levels)[(side, level, r % HALF_LAT, place)]


def padded(count):
    return -(-count // 16) * 16


def send_gather(levels, row_count, even):
    half = levels // 2
    mine, theirs = (0, half) if even else (half, 0)
    parts = []
    for base, low, high in (
        (theirs, HALF_LAT, row_count),
        (mine, row_count, row_count + HALF_LAT),
        (theirs, row_count, row_count + HALF_LAT),
    ):
        rows = [
            coarse_slot(levels, even, r, base + e, c)
            for r in range(low, high)
            for e in range(half)
            for c in range(HALF_LON)
        ]
        parts += rows + [-1] * (padded(len(rows)) - len(rows))
    return column(parts)


def place_gather(levels, row_count, even):
    half = levels // 2
    out = np.full((4, row_count, WLON, half), -1)
    base = 0 if even else half
    for r in range(row_count):
        for e in range(half):
            for c in range(HALF_LON):
                mine, theirs = (c, c + HALF_LON) if even else (c + HALF_LON, c)
                if r >= HALF_LAT:
                    out[0, r, mine, e] = coarse_slot(levels, even, r, base + e, c)
                    out[1, r, theirs, e] = ((r - HALF_LAT) * half + e) * HALF_LON + c
                else:
                    out[2, r, mine, e] = (r * half + e) * HALF_LON + c
                    out[3, r, theirs, e] = (r * half + e) * HALF_LON + c
    return out.reshape(4, -1, 1).astype(np.int32)


def open_tables(levels):
    order = rolled_levels(levels)
    sides = np.arange(GROUP) // PART
    levs = np.arange(GROUP) % PART // HALF_LON % WLEV
    valid = np.arange(GROUP) < 2 * PART
    out = np.zeros((levels // WLEV, 2, GROUP, GROUP), np.float32)
    for pair in range(levels // WLEV):
        wrapped = np.asarray([order[pair * WLEV + v] < WLEV // 2 for v in range(WLEV)])[levs]
        seen = (wrapped[:, None] == wrapped[None]) & valid[None]
        out[pair, 0] = seen
        out[pair, 1] = seen & ((sides[:, None] == sides[None]) | ~valid[:, None])
    return np.tile(out, (1, 1, 2, 2))


def one_hot(index, width, zero):
    index = jnp.asarray(index) + zero
    return (index == lax.broadcasted_iota(jnp.int32, (1, width), 1)).astype(jnp.bfloat16)


def mm(a, b):
    return jnp.dot(a, b, preferred_element_type=jnp.float32)


def layer_norm(values, norm_gain, offset):
    average = jnp.mean(values, axis=-1, keepdims=True)
    centred = values - average
    spread = jnp.mean(centred * centred, axis=-1, keepdims=True)
    return centred * lax.rsqrt(spread + norm_eps) * norm_gain + offset


def staged(tasks, stages):
    held = {}
    for step in range(len(tasks) + len(stages) - 1):
        for depth, stage in enumerate(stages):
            at = step - depth
            if 0 <= at < len(tasks):
                held[at] = stage(tasks[at], held.get(at))


def project(own, other, packed_ref, scale_ref, query, key, value):
    width = packed_ref.shape[1] // 3
    block = 2 * LANES
    rows = lax.broadcasted_iota(jnp.int32, (block, block), 0) // (LANES // 2)
    cols = lax.broadcasted_iota(jnp.int32, (block, block), 1) // (LANES // 2)
    same = (rows == cols).astype(jnp.float32).astype(jnp.bfloat16)
    lane = lax.broadcasted_iota(jnp.int32, (1, block), 1)
    first = (lane % LANES < LANES // 2).astype(jnp.float32)
    head = lane // (LANES // 2)
    tasks = []
    for j in range(width // block):
        tasks += [("q", 0, j), ("k", 0, j), ("k", 1, j), ("v", 0, j), ("v", 1, j)]

    def multiply(task, _):
        kind, s, j = task
        start = "qkv".index(kind) * width + j * block
        return mm((own, other)[s][...], packed_ref[:, start : start + block])

    def measure(task, rows):
        if task[0] == "v":
            return rows
        return rows, mm((rows * rows).astype(jnp.bfloat16), same)

    def keep(task, held):
        kind, s, j = task
        at = slice(j * block, (j + 1) * block)
        if kind == "v":
            value[s, :, at] = held.astype(jnp.bfloat16)
            return
        rows, total = held
        rows = rows * lax.rsqrt(total + unit_eps)
        if kind == "k":
            key[s, :, at] = rows.astype(jnp.bfloat16)
            return
        scale = jnp.zeros((1, block), jnp.float32)
        for h in range(2 * block // LANES):
            scale = jnp.where(head == h, scale_ref[j * 2 * block // LANES + h], scale)
        scale = scale * math.log2(math.e)
        query[0, :, at] = (rows * (scale * first)).astype(jnp.bfloat16)
        query[1, :, at] = (rows * (scale * (1.0 - first))).astype(jnp.bfloat16)

    staged(tasks, [multiply, measure, keep])


def attend(wraps, query, key, value, open_ref, prob, ctx):
    width = query.shape[2]
    windows = len(wraps)
    pairs = query.shape[1] // windows // GROUP
    is_first = lax.broadcasted_iota(jnp.int32, (GROUP, LANES), 1) < LANES // 2
    ones = jnp.ones((2 * GROUP, LANES), jnp.bfloat16)
    tasks = [
        (w, pair, slice(j * LANES, (j + 1) * LANES))
        for w in range(windows)
        for pair in range(pairs)
        for j in range(width // LANES)
    ]
    slots = {task[:2] + (task[2].start,): u % prob.shape[0] for u, task in enumerate(tasks)}

    def place(task):
        w, pair, at = task
        base = (w * pairs + pair) * GROUP
        return slice(base, base + GROUP), at, slots[(w, pair, at.start)]

    def score(task, _):
        rows, at, slot = place(task)
        wrap = 0 if wraps[task[0]] is None else wraps[task[0]]
        q = jnp.concatenate([query[0, rows, at], query[1, rows, at]], axis=0)
        k = jnp.concatenate([key[0, rows, at], key[1, rows, at]], axis=0)
        raw = lax.dot_general(q, k, (((1,), (1,)), ((), ())), preferred_element_type=jnp.float32)
        prob[slot] = jnp.exp2(raw).astype(jnp.bfloat16) * open_ref[task[1], wrap]

    def wait(task, _):
        return None

    def mix(task, _):
        rows, at, slot = place(task)
        v = jnp.concatenate([value[0, rows, at], value[1, rows, at]], axis=0)
        out = mm(prob[slot], jnp.concatenate([v, ones], axis=1))
        top = jnp.where(is_first, out[:GROUP, :LANES], out[GROUP:, :LANES])
        total = jnp.where(is_first, out[:GROUP, LANES:], out[GROUP:, LANES:])
        ctx[rows, at] = (top / total).astype(jnp.bfloat16)

    staged(tasks, [score, wait, mix])


def attention_scratch(rows, width):
    bf16 = jnp.bfloat16
    return [
        pltpu.VMEM((2, rows, width), bf16),
        pltpu.VMEM((2, rows, width), bf16),
        pltpu.VMEM((2, rows, width), bf16),
        pltpu.VMEM((8, 2 * GROUP, 2 * GROUP), bf16),
        pltpu.VMEM((rows, width), bf16),
    ]


def fill_windows(dst, pick, sources):
    span = dst.shape[0] // len(sources)
    for w, chunks in enumerate(sources):
        rows = sum(mm(p, chunk) for p, chunk in zip(pick, chunks))
        dst[w * span : (w + 1) * span] = rows.astype(jnp.bfloat16)


def block_rows(own, ctx, output_ref, gain_ref, offset_ref):
    branch = layer_norm(mm(ctx[...], output_ref[...]), gain_ref[...], offset_ref[...])
    return (own[...].astype(jnp.float32) + branch).astype(jnp.bfloat16)


def merge_rows(first, patch_ref, merge_ref, gain_ref, offset_ref):
    cells = patch_ref.shape[0] // 4
    channels = first.shape[1]
    part = mm(patch_ref[...], first[...]).astype(jnp.bfloat16)
    total = None
    for g in range(4):
        term = mm(part[g * cells : (g + 1) * cells], merge_ref[g * channels : (g + 1) * channels])
        total = term if total is None else total + term
    return layer_norm(total, gain_ref[...], offset_ref[...]).astype(jnp.bfloat16)


def side_kernel(
    scale_ref,
    flags,
    own_ref,
    other_ref,
    top_ref,
    bottom_ref,
    other_rim_ref,
    packed_ref,
    output_ref,
    gain_ref,
    offset_ref,
    merge_ref,
    merge_gain_ref,
    merge_offset_ref,
    open_ref,
    pick_ref,
    patch_ref,
    *rest,
):
    if len(rest) == 9:
        side, (merged_ref, *rest) = 0, rest
    else:
        side, (near_ref, edge_ref, merged_ref, up_ref, *rest) = 1, rest
    own, other, query, key, value, prob, ctx, first = rest
    chunks = own_ref.shape[0]
    pick = [pick_ref[0], pick_ref[1]]
    for dst, src, top, bottom in (
        (own, own_ref, top_ref[side], bottom_ref[side]),
        (other, other_ref, other_rim_ref[0], other_rim_ref[1]),
    ):
        line = [top] + [src[e] for e in range(chunks)] + [bottom]
        fill_windows(dst, pick, list(zip(line[::2], line[1::2])))
    project(own, other, packed_ref, scale_ref, query, key, value)
    wraps = [flags[0]] + [None] * (chunks // 2 - 1) + [flags[1]]
    attend(wraps, query, key, value, open_ref, prob, ctx)
    first[...] = block_rows(own, ctx, output_ref, gain_ref, offset_ref)
    merged = merge_rows(first, patch_ref, merge_ref, merge_gain_ref, merge_offset_ref)
    merged_ref[...] = merged
    if side:
        reach = edge_ref.shape[2]
        up_ref[...] = (
            mm(edge_ref[0], near_ref[:reach]) + mm(edge_ref[1], merged[:reach])
        ).astype(jnp.bfloat16)


def second_kernel(
    scale_ref,
    flags,
    near_ref,
    far_ref,
    rim_ref,
    other_near_ref,
    other_far_ref,
    other_rim_ref,
    packed_ref,
    output_ref,
    gain_ref,
    offset_ref,
    open_ref,
    coarse_ref,
    send_at_ref,
    second_ref,
    send_ref,
    return_ref,
    return_near_ref,
    own,
    other,
    query,
    key,
    value,
    prob,
    ctx,
):
    span = open_ref.shape[0] * GROUP
    windows = own.shape[0] // span
    small = rim_ref.shape[0] // 2
    for w in range(windows):
        low, high = coarse_reach(w, small, near_ref.shape[0])
        reach = [(0, low, high), (1, low, high)]
        if w == windows - 1:
            reach.append((2, 0, 2 * small))
        at = slice(w * span, (w + 1) * span)
        mine = theirs = 0.0
        for s, low, high in reach:
            pick = coarse_ref[s, at, : high - low]
            mine += mm(pick, (near_ref, far_ref, rim_ref)[s][low:high])
            theirs += mm(pick, (other_near_ref, other_far_ref, other_rim_ref)[s][low:high])
        own[at] = mine.astype(jnp.bfloat16)
        other[at] = theirs.astype(jnp.bfloat16)
    project(own, other, packed_ref, scale_ref, query, key, value)
    attend([None] * (windows - 1) + [flags[1]], query, key, value, open_ref, prob, ctx)
    second = block_rows(own, ctx, output_ref, gain_ref, offset_ref)
    second_ref[...] = second
    rows = mm(send_at_ref[...], second).astype(jnp.bfloat16)
    at = 0
    for dst in (send_ref, return_ref, return_near_ref):
        count = dst.shape[0]
        dst[...] = rows[at : at + count]
        at += padded(count)


def place_kernel(second_ref, near_ref, back_ref, back_near_ref, a_ref, b_ref, c_ref, out_ref):
    rows, _, columns, pair, _ = out_ref.shape
    step = columns * pair
    edge = HALF_LAT * step
    early = mm(c_ref[0], back_ref[...]) + mm(c_ref[1], back_near_ref[...])
    late = mm(a_ref[...], second_ref[...]) + mm(b_ref[...], near_ref[...])
    for r in range(rows):
        block, base = (early, r * step) if r < HALF_LAT else (late, r * step - edge)
        for c in range(columns):
            out_ref[r, 0, c] = block[base + c * pair : base + (c + 1) * pair].astype(jnp.bfloat16)


def call(kernel, outs, scratch, scalars, operands):
    vmem = pl.BlockSpec(memory_space=pltpu.VMEM)
    return pl.pallas_call(
        kernel,
        out_shape=outs,
        in_specs=[pl.BlockSpec(memory_space=pltpu.SMEM)] * len(scalars) + [vmem] * len(operands),
        out_specs=[vmem] * len(outs),
        scratch_shapes=scratch,
    )(*scalars, *operands)


def far_of(i, n):
    return (i + (1 if i % 2 else -1)) % n


def near_swap(value):
    return lax.ppermute(value, "lon", [(i, i ^ 1) for i in range(lax.axis_size("lon"))])


def far_swap(value):
    n = lax.axis_size("lon")
    return lax.ppermute(value, "lon", [(i, far_of(i, n)) for i in range(n)])


def ring(value, by, turn):
    n, m = lax.axis_size("lat"), lax.axis_size("lon")
    links = [(i * m + j, (i + by) % n * m + turn(j, m)) for i in range(n) for j in range(m)]
    return lax.ppermute(value, ("lat", "lon"), links)


def shift(value, by):
    n = lax.axis_size("lat")
    return lax.ppermute(value, "lat", [(i, i + by) for i in range(n) if 0 <= i + by < n])


def body(
    features,
    packed_first,
    scale_first,
    output_first,
    gain_first,
    offset_first,
    merge_weight,
    merge_gain,
    merge_offset,
    packed_second,
    scale_second,
    output_second,
    gain_second,
    offset_second,
):
    levels, row_count, _, channels = features.shape
    inner = packed_first.shape[1] // 3
    second_inner = packed_second.shape[1] // 3
    wide = merge_weight.shape[1]
    half_rows = row_count // 2
    lat_pos = lax.axis_index("lat")
    odd = lax.axis_index("lon") % 2
    is_even = odd == 0
    last = lax.axis_size("lat") - 1
    place = jnp.stack([lat_pos, lat_pos, 1 - odd])
    flags = (place == jnp.asarray([0, last, 1], jnp.int32)).astype(jnp.int32)
    bf16 = jnp.bfloat16
    span = levels // WLEV * GROUP
    tokens = HALF_LAT * levels * HALF_LON
    chunks = row_count // HALF_LAT
    windows = chunks // 2 + 1

    turned = jnp.transpose(features, (1, 0, 2, 3))
    left, right = turned[:, :, :HALF_LON], turned[:, :, HALF_LON:]
    near = jnp.where(is_even, right, left).reshape(chunks, tokens, channels)
    far = jnp.where(is_even, left, right).reshape(chunks, tokens, channels)

    near_other = near_swap(near)
    bottom = shift(jnp.stack([near[0], far[0]]), -1)
    top = shift(jnp.stack([near[-1], far[-1]]), 1)
    far_other = far_swap(far)
    near_other_rim = near_swap(jnp.stack([top[0], bottom[0]]))
    far_other_rim = far_swap(jnp.stack([top[1], bottom[1]]))

    zero = jnp.minimum(lat_pos, 0)
    opened = jnp.asarray(open_tables(levels), bf16)
    cells = half_rows * levels * HALF_LON // 2
    small = jax.ShapeDtypeStruct((cells, wide), bf16)
    edge = jax.ShapeDtypeStruct((tokens, wide), bf16)

    def scratch(count, width, depth):
        rows = count * span
        return [pltpu.VMEM((rows, depth), bf16)] * 2 + attention_scratch(rows, width)

    shared = [packed_first, output_first, gain_first[None], offset_first[None]]
    shared += [merge_weight, merge_gain[None], merge_offset[None], opened]
    shared += [
        one_hot(np.stack(fine_gather(levels)), tokens, zero),
        one_hot(patch_gather(levels, row_count), windows * span, zero),
    ]
    buffers = scratch(windows, inner, channels) + [pltpu.VMEM((windows * span, channels), bf16)]
    (merged_near,) = call(
        side_kernel,
        [small],
        buffers,
        [scale_first, flags],
        [near, near_other, top, bottom, near_other_rim] + shared,
    )
    other_near = far_swap(merged_near)
    merged_far, edge_up = call(
        side_kernel,
        [small, edge],
        buffers,
        [scale_first, flags],
        [far, far_other, top, bottom, far_other_rim]
        + shared
        + [merged_near, one_hot(edge_gather(levels), padded(tokens // 2), zero)],
    )
    other_far = far_swap(merged_far)
    other_rim = ring(edge_up, -1, far_of)
    rim = ring(edge_up, -1, lambda j, m: j)

    windows = half_rows // WLAT
    share = levels // 2 * HALF_LON

    def chosen(table):
        odd_table, even_table = (jnp.asarray(table(levels, half_rows, e)) for e in (False, True))
        return jnp.where(is_even, even_table, odd_table)

    places = chosen(place_gather)
    start = HALF_LAT * WLON * levels // 2
    back = jax.ShapeDtypeStruct((HALF_LAT * share, wide), bf16)
    second, send, back_same, back_near = call(
        second_kernel,
        [
            jax.ShapeDtypeStruct((windows * span, wide), bf16),
            jax.ShapeDtypeStruct(((half_rows - HALF_LAT) * share, wide), bf16),
            back,
            back,
        ],
        scratch(windows, second_inner, wide),
        [scale_second, flags],
        [
            merged_near,
            merged_far,
            rim,
            other_near,
            other_far,
            other_rim,
            packed_second,
            output_second,
            gain_second[None],
            offset_second[None],
            opened,
            one_hot(coarse_gather(levels, half_rows), padded(tokens), zero),
            one_hot(chosen(send_gather), windows * span, zero),
        ],
    )
    back_near = ring(back_near, 1, lambda j, m: j ^ 1)
    back_same = ring(back_same, 1, lambda j, m: j)
    received = near_swap(send)
    (out,) = call(
        place_kernel,
        [jax.ShapeDtypeStruct((half_rows, 1, WLON, levels // 2, wide), bf16)],
        [],
        [],
        [
            second,
            received,
            back_same,
            back_near,
            one_hot(places[0, start:], second.shape[0], zero),
            one_hot(places[1, start:], received.shape[0], zero),
            one_hot(places[2:, :start], back_same.shape[0], zero),
        ],
    )
    return jnp.transpose(out, (0, 1, 3, 2, 4))


def solution(mesh):
    return jax.shard_map(
        body,
        mesh=mesh,
        in_specs=(P(None, "lat", "lon", None),) + (P(),) * 13,
        out_specs=P("lat", "lon", None, None, None),
        check_vma=False,
    )
```

time: 133 us -> 86.7 us (0.65)
  Pallas kernels: 77.4 us -> 36.1 us
  other arithmetic: 3.8 us -> 8.59 us
  waiting for transfers between devices: 19.6 us -> 15 us
  local copies, waits for them, and re-layouts: 9.3 us -> 5.18 us
  starting transfers between devices: 22.7 us -> 21.3 us
    pallas_call x3 -> x4, Pallas kernels: 77.4 us -> 36.1 us  [call(): pl.pallas_call(kernel, out_shape=outs, in_specs=[pl.BlockSpec(memory_spac...]
    convert_element_type x1 -> x9, other arithmetic: 0.59 us -> 7.08 us  [the longest x8 6.5 us: one_hot(): (index == lax.broadcasted_iota(jnp.int32, (1, width), 1)).astype(jnp.bflo...]
    ppermute x9 -> x10, waiting for transfers between devices: 18.9 us -> 14.2 us  [the longest x4 14.2 us: ring(): return lax.ppermute(value, ('lat', 'lon'), links)]
    ppermute x9 -> x10, starting transfers between devices: 22.6 us -> 21.1 us  [the longest x4 7.99 us: far_swap(): return lax.ppermute(value, 'lon', [(i, far_of(i, n)) for i in range(n)])]
    select_n x1 -> x0, local copies, waits for them, and re-layouts: 1.43 us -> none  [body(): jnp.where(is_even, jnp.concatenate([keep, received], axis=2), jnp.concate...]
    unnamed x35 -> x48, local copies, waits for them, and re-layouts: 3.13 us -> 3.99 us
  transfers between devices with their start and end apart: 12 -> 13, of which waited for: 5 -> 5; matrix products, arithmetic and copies ran while one was open for 5% -> 9% of each run, Pallas kernels for 21% -> 29%
where the time goes in v2:
time: 86.7 us; the launch traced here: 86.5 us
  Pallas kernels  36.1 us (42%)
  starting transfers between devices  21.3 us (25%)
  waiting for transfers between devices  15 us (17%)
  other arithmetic  8.59 us (10%)
  local copies, waits for them, and re-layouts  5.18 us (6%)
    pallas_call x4, Pallas kernels, call(): pl.pallas_call(kernel, out_shape=outs, in_specs=[pl.BlockSpec(memory_spac...  36.1 us
    ppermute x4, waiting for transfers between devices, ring(): return lax.ppermute(value, ('lat', 'lon'), links)  14.2 us
    ppermute x4, starting transfers between devices, far_swap(): return lax.ppermute(value, 'lon', [(i, far_of(i, n)) for i in range(n)])  7.99 us
    ppermute x2, starting transfers between devices, shift(): lax.ppermute(value, 'lat', [(i, i + by) for i in range(n) if 0 <= i + by...  6.8 us
    convert_element_type x8, other arithmetic, one_hot(): (index == lax.broadcasted_iota(jnp.int32, (1, width), 1)).astype(jnp.bflo...  6.5 us
    ppermute x4, starting transfers between devices, ring(): return lax.ppermute(value, ('lat', 'lon'), links)  6.35 us
    unnamed x48, local copies, waits for them, and re-layouts  3.99 us
  transfers between devices with their start and end apart: 13, of which 5 were waited for; matrix products, arithmetic and copies ran while one was open for 9% of the time, Pallas kernels for 29%

profile of v2, /device:TPU:0, one launch (start us, length us, event | category | flops | bytes accessed | tf_op | source)
XLA Modules:
  0.0 86.5 jit_solution(14392177737862603474)
XLA Ops:
  0.0 1.3 %broadcast_select_fusion = (bf16[24,4,6,512]{3,0,2,1:T(8,128)(2,1)S(1)}, bf16[24,4,6,512]{3,0,2,1:T(8,128)(2,1)S(1)}) fusion(pred[]{:T(512)S(6)} %eq.125, bf16[24,4,12,512]{3,0,2,1:T(8,128)(2,1)} %bitcast.21), kind=kLoop, calls=%fused_computation.2 | loop fusion | flops 589824 | bytes 2359297 | tf_op jit(solution)/shard_map/jit(_where)/select_n | solution.py:499
  1.7 1.3 %collective-permute-start.2 = (bf16[2,72,512]{2,1,0:T(8,128)(2,1)S(1)}, bf16[2,72,512]{2,1,0:T(8,128)(2,1)S(1)}, u32[]{:S(2)}, u32[]{:S(2)}) collective-permute-start(bf16[2,72,512]{2,1,0:T(8,128)(2,1)S(1)} %pad_maximum_fusion.1), channel_id=1, source_target_pairs={{8,0},{16,8},{24,16},{9,1},{17,9},{25,17},{10,2},{18,10},{26,18},{... | collective-permute-start | bytes 442376 | tf_op jit(solution)/shard_map/ppermute | solution.py:460
  3.1 5.5 %collective-permute-start.1 = (bf16[2,72,512]{2,1,0:T(8,128)(2,1)S(1)}, bf16[2,72,512]{2,1,0:T(8,128)(2,1)S(1)}, u32[]{:S(2)}, u32[]{:S(2)}) collective-permute-start(bf16[2,72,512]{2,1,0:T(8,128)(2,1)S(1)} %pad_maximum_fusion), channel_id=1, source_target_pairs={{0,8},{8,16},{16,24},{1,9},{9,17},{17,25},{2,10},{10,18},{18,26},{... | collective-permute-start | bytes 442376 | tf_op jit(solution)/shard_map/ppermute | solution.py:460
  9.7 4.3 %collective-permute-start.4 = (bf16[8,72,512]{2,1,0:T(8,128)(2,1)S(1)}, bf16[8,72,512]{2,1,0:T(8,128)(2,1)S(1)}, u32[]{:S(2)}, u32[]{:S(2)}) collective-permute-start(bf16[8,72,512]{2,1,0:T(8,128)(2,1)S(1)} %reshape.29.own_ref), channel_id=1, source_target_pairs={{0,7},{1,2},{2,1},{3,4},{4,3},{5,6},{6,5},{7,0},{8,15},{9,10},{10,... | collective-permute-start | bytes 1769480 | tf_op jit(solution)/shard_map/ppermute | solution.py:449
  14.0 1.2 %fusion.patch_ref = bf16[576,800]{1,0:T(8,128)(2,1)} fusion(s32[576]{0:T(1024)S(1)} %add_reduce_fusion), kind=kLoop, calls=%fused_computation.1 | loop fusion | flops 921600 | bytes 923904 | tf_op jit(solution)/shard_map/convert_element_type | solution.py:172
  15.2 0.7 fusion.4.pick_ref
  16.0 0.7 fusion.3.send_at_ref
  16.7 0.9 %fusion.1.coarse_ref = bf16[3,320,80]{2,1,0:T(8,128)(2,1)} fusion(s32[3,320]{1,0:T(4,128)S(1)} %add_bitcast_fusion), kind=kLoop, calls=%fused_computation.5 | loop fusion | flops 153600 | bytes 157440 | tf_op jit(solution)/shard_map/convert_element_type | solution.py:172
  17.7 0.8 fusion.2.a_ref
  18.5 0.7 fusion.6.rest_1_
  20.1 0.8 collective-permute-done.3.other_rim_ref
  21.7 12.2 %shard_map.226.rest_0_.near_ref = bf16[144,1024]{1,0:T(8,128)(2,1)} custom-call(f32[8]{0:T(128)} %scale_ref.4, s32[3]{0:T(128)} %compare_convert_fusion.flags, bf16[8,72,512]{2,1,0:T(8,128)(2,1)} %copy-done.1, bf16[8,72,512]{2,1,0:T(8,128)(2,1)} %copy-done.5, bf16[2,72,512]{2,1,0:T(8,128)(2,1)} %copy-done.3, bf16[2,72,512]{2,1,0:T(8,128)(2,1)} %copy-done.2, ...), custom_call_target="tpu_custom_call" | custom-call | tf_op jit(solution)/shard_map/pallas_call | solution.py:430
  34.0 3.6 %collective-permute-start.7 = (bf16[144,1024]{1,0:T(8,128)(2,1)}, bf16[144,1024]{1,0:T(8,128)(2,1)S(1)}, u32[]{:S(2)}, u32[]{:S(2)}) collective-permute-start(bf16[144,1024]{1,0:T(8,128)(2,1)} %shard_map.226.rest_0_.near_ref), channel_id=1, source_target_pairs={{0,7},{1,2},{2,1},{3,4},{4,3},{5,6},{6,5},{7,0},{8,15},{9,10},{10,... | collective-permute-start | bytes 884744 | tf_op jit(solution)/shard_map/ppermute | solution.py:449
  38.2 0.8 copy-done.4
  39.0 12.7 %shard_map.227 = (bf16[144,1024]{1,0:T(8,128)(2,1)}, bf16[72,1024]{1,0:T(8,128)(2,1)}) custom-call(f32[8]{0:T(128)} %scale_ref.4, s32[3]{0:T(128)} %compare_convert_fusion.flags, bf16[8,72,512]{2,1,0:T(8,128)(2,1)} %copy-done, bf16[8,72,512]{2,1,0:T(8,128)(2,1)} %copy-done.4, bf16[2,72,512]{2,1,0:T(8,128)(2,1)} %copy-done.3, bf16[2,72,512]{2,1,0:T(8,128)(2,1)} %copy-done.2, ...), custom_call_target="tpu_custom_call" | custom-call | tf_op jit(solution)/shard_map/pallas_call | solution.py:430
  51.8 0.7 fusion.5.b_ref
  52.8 5.3 %collective-permute-start.9 = (bf16[72,1024]{1,0:T(8,128)(2,1)}, bf16[72,1024]{1,0:T(8,128)(2,1)S(1)}, u32[]{:S(2)}, u32[]{:S(2)}) collective-permute-start(bf16[72,1024]{1,0:T(8,128)(2,1)} %get-tuple-element.12), channel_id=1, source_target_pairs={{0,31},{1,26},{2,25},{3,28},{4,27},{5,30},{6,29},{7,24},{8,7},{9,2... | collective-permute-start | bytes 442376 | tf_op jit(solution)/shard_map/ppermute | solution.py:455
  58.1 1.6 %collective-permute-done.6.rim_ref = bf16[72,1024]{1,0:T(8,128)(2,1)S(1)} collective-permute-done((bf16[72,1024]{1,0:T(8,128)(2,1)}, bf16[72,1024]{1,0:T(8,128)(2,1)S(1)}, u32[]{:S(2)}, u32[]{:S(2)}) %collective-permute-start.6) | collective-permute-done | bytes 147488 | tf_op jit(solution)/shard_map/ppermute | solution.py:455
  59.8 6.8 %collective-permute-done.9.other_rim_ref = bf16[72,1024]{1,0:T(8,128)(2,1)S(1)} collective-permute-done((bf16[72,1024]{1,0:T(8,128)(2,1)}, bf16[72,1024]{1,0:T(8,128)(2,1)S(1)}, u32[]{:S(2)}, u32[]{:S(2)}) %collective-permute-start.9) | collective-permute-done | bytes 147488 | tf_op jit(solution)/shard_map/ppermute | solution.py:455
  67.4 8.5 %shard_map.228 = (bf16[320,1024]{1,0:T(8,128)(2,1)}, bf16[108,1024]{1,0:T(8,128)(2,1)}, bf16[36,1024]{1,0:T(8,128)(2,1)}, bf16[36,1024]{1,0:T(8,128)(2,1)}) custom-call(f32[8]{0:T(128)} %scale_ref.5, s32[3]{0:T(128)} %compare_convert_fusion.flags, bf16[144,1024]{1,0:T(8,128)(2,1)} %shard_map.226.rest_0_.near_ref, ...), custom_call_target="tpu_custom_call" | custom-call | tf_op jit(solution)/shard_map/pallas_call | solution.py:430
  76.6 0.7 fusion.7.c_ref
  77.3 5.1 %collective-permute-done.11.back_ref = bf16[36,1024]{1,0:T(8,128)(2,1)S(1)} collective-permute-done((bf16[36,1024]{1,0:T(8,128)(2,1)}, bf16[36,1024]{1,0:T(8,128)(2,1)S(1)}, u32[]{:S(2)}, u32[]{:S(2)}) %collective-permute-start.11) | collective-permute-done | bytes 73760 | tf_op jit(solution)/shard_map/ppermute | solution.py:455
  82.3 0.7 collective-permute-done.12.back_near_ref
  83.8 2.7 %shard_map.229 = bf16[12,1,12,2,1024]{4,3,2,1,0:T(2,128)(2,1)} custom-call(bf16[320,1024]{1,0:T(8,128)(2,1)} %get-tuple-element.13.second_ref, bf16[108,1024]{1,0:T(8,128)(2,1)} %copy-done.8, bf16[36,1024]{1,0:T(8,128)(2,1)} %copy-done.13, bf16[36,1024]{1,0:T(8,128)(2,1)} %copy-done.14, bf16[216,320]{1,0:T(8,128)(2,1)} %fusion.2.a_ref, ...), custom_call_target="tpu_custom_call" | custom-call | tf_op jit(solution)/shard_map/pallas_call | solution.py:430
  (91 shorter events, 6.5 us)
Async XLA Ops:
  1.7 17.5 %collective-permute-start.2 = (bf16[2,72,512]{2,1,0:T(8,128)(2,1)S(1)}, bf16[2,72,512]{2,1,0:T(8,128)(2,1)S(1)}, u32[]{:S(2)}, u32[]{:S(2)}) collective-permute-start(bf16[2,72,512]{2,1,0:T(8,128)(2,1)S(1)} %pad_maximum_fusion.1), channel_id=1, source_target_pairs={{8,0},{16,8},{24,16},{9,1},{17,9},{25,17},{10,2},{18,10},{26,18},{... | collective-permute-start | bytes 442376 | tf_op jit(solution)/shard_map/ppermute | solution.py:460
  3.1 16.1 %collective-permute-start.1 = (bf16[2,72,512]{2,1,0:T(8,128)(2,1)S(1)}, bf16[2,72,512]{2,1,0:T(8,128)(2,1)S(1)}, u32[]{:S(2)}, u32[]{:S(2)}) collective-permute-start(bf16[2,72,512]{2,1,0:T(8,128)(2,1)S(1)} %pad_maximum_fusion), channel_id=1, source_target_pairs={{0,8},{8,16},{16,24},{1,9},{9,17},{17,25},{2,10},{10,18},{18,26},{... | collective-permute-start | bytes 442376 | tf_op jit(solution)/shard_map/ppermute | solution.py:460
  9.1 8.6 %copy-start.1 = (bf16[8,72,512]{2,1,0:T(8,128)(2,1)}, bf16[8,72,512]{2,1,0:T(8,128)(2,1)S(1)}, u32[]{:S(2)}) copy-start(bf16[8,72,512]{2,1,0:T(8,128)(2,1)S(1)} %reshape.28.own_ref) | copy-start | bytes 1769476
  9.1 6.1 %copy-start.19 = (s32[2,160,1]{1,0,2:T(2,128)S(1)}, s32[2,160,1]{1,0,2:T(2,128)}, u32[]{:S(2)}) copy-start(s32[2,160,1]{1,0,2:T(2,128)} %constant.45.clone) | copy-start | bytes 3844
  9.1 6.9 %copy-start.20 = (s32[2,72,1]{1,0,2:T(2,128)S(1)}, s32[2,72,1]{1,0,2:T(2,128)}, u32[]{:S(2)}) copy-start(s32[2,72,1]{1,0,2:T(2,128)} %constant.47.clone) | copy-start | bytes 1732
  9.1 6.9 %copy-start.21 = (s32[208,1]{0,1:T(1,128)S(1)}, s32[208,1]{0,1:T(1,128)}, u32[]{:S(2)}) copy-start(s32[208,1]{0,1:T(1,128)} %constant.51.clone) | copy-start | bytes 2500
  9.1 6.8 %copy-start.22 = (s32[208,1]{0,1:T(1,128)S(1)}, s32[208,1]{0,1:T(1,128)}, u32[]{:S(2)}) copy-start(s32[208,1]{0,1:T(1,128)} %constant.52.clone) | copy-start | bytes 2500
  9.1 7.6 %copy-start.15 = (s32[3,320,1]{1,0,2:T(4,128)S(1)}, s32[3,320,1]{1,0,2:T(4,128)}, u32[]{:S(2)}) copy-start(s32[3,320,1]{1,0,2:T(4,128)} %constant.50.clone) | copy-start | bytes 11524
  9.1 8.5 %copy-start.16 = (s32[4,288,1]{1,0,2:T(4,128)S(1)}, s32[4,288,1]{1,0,2:T(4,128)}, u32[]{:S(2)}) copy-start(s32[4,288,1]{1,0,2:T(4,128)} %constant.48.clone) | copy-start | bytes 13828
  9.1 8.5 %copy-start.17 = (s32[4,288,1]{1,0,2:T(4,128)S(1)}, s32[4,288,1]{1,0,2:T(4,128)}, u32[]{:S(2)}) copy-start(s32[4,288,1]{1,0,2:T(4,128)} %constant.49.clone) | copy-start | bytes 13828
  9.2 11.7 %collective-permute-start = (bf16[8,72,512]{2,1,0:T(8,128)(2,1)S(1)}, bf16[8,72,512]{2,1,0:T(8,128)(2,1)S(1)}, u32[]{:S(2)}, u32[]{:S(2)}) collective-permute-start(bf16[8,72,512]{2,1,0:T(8,128)(2,1)S(1)} %reshape.28.own_ref), channel_id=1, source_target_pairs={{0,1},{1,0},{2,3},{3,2},{4,5},{5,4},{6,7},{7,6},{8,9},{9,8},{10,11... | collective-permute-start | bytes 1769480 | tf_op jit(solution)/shard_map/ppermute | solution.py:444
  9.4 10.0 %copy-start.23 = (s32[3]{0:T(128)S(1)}, s32[3]{0:T(128)}, u32[]{:S(2)}) copy-start(s32[3]{0:T(128)} %constant.43.clone) | copy-start | bytes 40
  9.7 24.3 %copy-start = (bf16[8,72,512]{2,1,0:T(8,128)(2,1)}, bf16[8,72,512]{2,1,0:T(8,128)(2,1)S(1)}, u32[]{:S(2)}) copy-start(bf16[8,72,512]{2,1,0:T(8,128)(2,1)S(1)} %reshape.29.own_ref) | copy-start | bytes 1769476
  9.7 27.9 %collective-permute-start.4 = (bf16[8,72,512]{2,1,0:T(8,128)(2,1)S(1)}, bf16[8,72,512]{2,1,0:T(8,128)(2,1)S(1)}, u32[]{:S(2)}, u32[]{:S(2)}) collective-permute-start(bf16[8,72,512]{2,1,0:T(8,128)(2,1)S(1)} %reshape.29.own_ref), channel_id=1, source_target_pairs={{0,7},{1,2},{2,1},{3,4},{4,3},{5,6},{6,5},{7,0},{8,15},{9,10},{10,... | collective-permute-start | bytes 1769480 | tf_op jit(solution)/shard_map/ppermute | solution.py:449
  19.3 18.3 %collective-permute-start.5 = (bf16[2,72,512]{2,1,0:T(8,128)(2,1)S(1)}, bf16[2,72,512]{2,1,0:T(8,128)(2,1)S(1)}, u32[]{:S(2)}, u32[]{:S(2)}) collective-permute-start(bf16[2,72,512]{2,1,0:T(8,128)(2,1)S(1)} %pad_maximum_fusion.3), channel_id=1, source_target_pairs={{0,7},{1,2},{2,1},{3,4},{4,3},{5,6},{6,5},{7,0},{8,15},{9,10},{10,... | collective-permute-start | bytes 442376 | tf_op jit(solution)/shard_map/ppermute | solution.py:449
  19.4 1.4 %collective-permute-start.3 = (bf16[2,72,512]{2,1,0:T(8,128)(2,1)S(1)}, bf16[2,72,512]{2,1,0:T(8,128)(2,1)S(1)}, u32[]{:S(2)}, u32[]{:S(2)}) collective-permute-start(bf16[2,72,512]{2,1,0:T(8,128)(2,1)S(1)} %pad_maximum_fusion.2), channel_id=1, source_target_pairs={{0,1},{1,0},{2,3},{3,2},{4,5},{5,4},{6,7},{7,6},{8,9},{9,8},{10,11... | collective-permute-start | bytes 442376 | tf_op jit(solution)/shard_map/ppermute | solution.py:444
  34.0 32.6 %collective-permute-start.7 = (bf16[144,1024]{1,0:T(8,128)(2,1)}, bf16[144,1024]{1,0:T(8,128)(2,1)S(1)}, u32[]{:S(2)}, u32[]{:S(2)}) collective-permute-start(bf16[144,1024]{1,0:T(8,128)(2,1)} %shard_map.226.rest_0_.near_ref), channel_id=1, source_target_pairs={{0,7},{1,2},{2,1},{3,4},{4,3},{5,6},{6,5},{7,0},{8,15},{9,10},{10,... | collective-permute-start | bytes 884744 | tf_op jit(solution)/shard_map/ppermute | solution.py:449
  51.7 14.8 %collective-permute-start.8 = (bf16[144,1024]{1,0:T(8,128)(2,1)}, bf16[144,1024]{1,0:T(8,128)(2,1)S(1)}, u32[]{:S(2)}, u32[]{:S(2)}) collective-permute-start(bf16[144,1024]{1,0:T(8,128)(2,1)} %get-tuple-element.11.far_ref), channel_id=1, source_target_pairs={{0,7},{1,2},{2,1},{3,4},{4,3},{5,6},{6,5},{7,0},{8,15},{9,10},{10,... | collective-permute-start | bytes 884744 | tf_op jit(solution)/shard_map/ppermute | solution.py:449
  52.5 7.3 %collective-permute-start.6 = (bf16[72,1024]{1,0:T(8,128)(2,1)}, bf16[72,1024]{1,0:T(8,128)(2,1)S(1)}, u32[]{:S(2)}, u32[]{:S(2)}) collective-permute-start(bf16[72,1024]{1,0:T(8,128)(2,1)} %get-tuple-element.12), channel_id=1, source_target_pairs={{0,24},{1,25},{2,26},{3,27},{4,28},{5,29},{6,30},{7,31},{8,0},{9,1... | collective-permute-start | bytes 442376 | tf_op jit(solution)/shard_map/ppermute | solution.py:455
  52.8 13.7 %collective-permute-start.9 = (bf16[72,1024]{1,0:T(8,128)(2,1)}, bf16[72,1024]{1,0:T(8,128)(2,1)S(1)}, u32[]{:S(2)}, u32[]{:S(2)}) collective-permute-start(bf16[72,1024]{1,0:T(8,128)(2,1)} %get-tuple-element.12), channel_id=1, source_target_pairs={{0,31},{1,26},{2,25},{3,28},{4,27},{5,30},{6,29},{7,24},{8,7},{9,2... | collective-permute-start | bytes 442376 | tf_op jit(solution)/shard_map/ppermute | solution.py:455
  59.8 6.8 %copy-start.9 = (bf16[72,1024]{1,0:T(8,128)(2,1)}, bf16[72,1024]{1,0:T(8,128)(2,1)S(1)}, u32[]{:S(2)}) copy-start(bf16[72,1024]{1,0:T(8,128)(2,1)S(1)} %collective-permute-done.6.rim_ref) | copy-start | bytes 442372
  75.9 7.2 %collective-permute-start.10 = (bf16[108,1024]{1,0:T(8,128)(2,1)}, bf16[108,1024]{1,0:T(8,128)(2,1)S(1)}, u32[]{:S(2)}, u32[]{:S(2)}) collective-permute-start(bf16[108,1024]{1,0:T(8,128)(2,1)} %get-tuple-element.14), channel_id=1, source_target_pairs={{0,1},{1,0},{2,3},{3,2},{4,5},{5,4},{6,7},{7,6},{8,9},{9,8},{10,11... | collective-permute-start | bytes 663560 | tf_op jit(solution)/shard_map/ppermute | solution.py:444
  75.9 6.5 %collective-permute-start.11 = (bf16[36,1024]{1,0:T(8,128)(2,1)}, bf16[36,1024]{1,0:T(8,128)(2,1)S(1)}, u32[]{:S(2)}, u32[]{:S(2)}) collective-permute-start(bf16[36,1024]{1,0:T(8,128)(2,1)} %get-tuple-element.15), channel_id=1, source_target_pairs={{0,8},{1,9},{2,10},{3,11},{4,12},{5,13},{6,14},{7,15},{8,16},{9,17... | collective-permute-start | bytes 221192 | tf_op jit(solution)/shard_map/ppermute | solution.py:455
  76.5 6.6 %collective-permute-start.12 = (bf16[36,1024]{1,0:T(8,128)(2,1)}, bf16[36,1024]{1,0:T(8,128)(2,1)S(1)}, u32[]{:S(2)}, u32[]{:S(2)}) collective-permute-start(bf16[36,1024]{1,0:T(8,128)(2,1)} %get-tuple-element.16), channel_id=1, source_target_pairs={{0,9},{1,8},{2,11},{3,10},{4,13},{5,12},{6,15},{7,14},{8,17},{9,16... | collective-permute-start | bytes 221192 | tf_op jit(solution)/shard_map/ppermute | solution.py:455
  (13 other events, 15.8 us)

commit v3 on v2

--- a/solution.py
+++ b/solution.py
@@ -14,12 +14,13 @@
 HALF_LAT = WLAT // 2
 HALF_LON = WLON // 2
 LANES = 128
+FIRST_BYTES, SECOND_BYTES = 48 << 20, 32 << 20
 
 norm_eps = 1e-05
 unit_eps = 1e-06
 
 PART = WLEV * HALF_LAT * HALF_LON
-GROUP = -(-2 * PART // 16) * 16
+GROUP = 2 * PART
 
 
 def rolled_levels(levels):
@@ -157,19 +158,43 @@
     order = rolled_levels(levels)
     sides = np.arange(GROUP) // PART
     levs = np.arange(GROUP) % PART // HALF_LON % WLEV
-    valid = np.arange(GROUP) < 2 * PART
     out = np.zeros((levels // WLEV, 2, GROUP, GROUP), np.float32)
     for pair in range(levels // WLEV):
         wrapped = np.asarray([order[pair * WLEV + v] < WLEV // 2 for v in range(WLEV)])[levs]
-        seen = (wrapped[:, None] == wrapped[None]) & valid[None]
+        seen = wrapped[:, None] == wrapped[None]
         out[pair, 0] = seen
-        out[pair, 1] = seen & ((sides[:, None] == sides[None]) | ~valid[:, None])
+        out[pair, 1] = seen & (sides[:, None] == sides[None])
     return np.tile(out, (1, 1, 2, 2))
 
 
-def one_hot(index, width, zero):
-    index = jnp.asarray(index) + zero
-    return (index == lax.broadcasted_iota(jnp.int32, (1, width), 1)).astype(jnp.bfloat16)
+PATCH, PICK, EDGE, COARSE, SEND, PLACE = 0, 1, 3, 5, 8, 10
+
+
+def index_table(levels, row_count):
+    half_rows = row_count // 2
+    columns = [patch_gather(levels, row_count), *fine_gather(levels), *edge_gather(levels)]
+    columns += [*coarse_gather(levels, half_rows)]
+    columns += [send_gather(levels, half_rows, even) for even in (False, True)]
+    for even in (False, True):
+        columns += [*place_gather(levels, half_rows, even)]
+    out = np.full((padded(max(len(c) for c in columns)), len(columns)), -(1 << 20), np.int32)
+    for at, values in enumerate(columns):
+        out[: len(values), at] = values[:, 0]
+    return out
+
+
+def column_of(table_ref, at, rows):
+    return table_ref[rows, at : at + 1]
+
+
+def parity_column(table_ref, at, step, even, rows):
+    chosen = column_of(table_ref, at + step, rows), column_of(table_ref, at, rows)
+    return jnp.where(even == 1, *chosen)
+
+
+def one_hot(index, width):
+    lanes = lax.broadcasted_iota(jnp.int32, (index.shape[0], width), 1)
+    return (lanes == index).astype(jnp.float32).astype(jnp.bfloat16)
 
 
 def mm(a, b):
@@ -192,7 +217,7 @@
                 held[at] = stage(tasks[at], held.get(at))
 
 
-def project(own, other, packed_ref, scale_ref, query, key, value):
+def project(own, both, packed_ref, scale_ref, query, key, value):
     width = packed_ref.shape[1] // 3
     block = 2 * LANES
     rows = lax.broadcasted_iota(jnp.int32, (block, block), 0) // (LANES // 2)
@@ -201,14 +226,16 @@
     lane = lax.broadcasted_iota(jnp.int32, (1, block), 1)
     first = (lane % LANES < LANES // 2).astype(jnp.float32)
     head = lane // (LANES // 2)
+    half = both.shape[0] // 2
     tasks = []
     for j in range(width // block):
         tasks += [("q", 0, j), ("k", 0, j), ("k", 1, j), ("v", 0, j), ("v", 1, j)]
 
     def multiply(task, _):
-        kind, s, j = task
+        kind, part, j = task
         start = "qkv".index(kind) * width + j * block
-        return mm((own, other)[s][...], packed_ref[:, start : start + block])
+        source = own[...] if kind == "q" else both[part * half : (part + 1) * half]
+        return mm(source, packed_ref[:, start : start + block])
 
     def measure(task, rows):
         if task[0] == "v":
@@ -216,83 +243,97 @@
         return rows, mm((rows * rows).astype(jnp.bfloat16), same)
 
     def keep(task, held):
-        kind, s, j = task
+        kind, part, j = task
         at = slice(j * block, (j + 1) * block)
         if kind == "v":
-            value[s, :, at] = held.astype(jnp.bfloat16)
+            value[part * half : (part + 1) * half, at] = held.astype(jnp.bfloat16)
             return
         rows, total = held
         rows = rows * lax.rsqrt(total + unit_eps)
         if kind == "k":
-            key[s, :, at] = rows.astype(jnp.bfloat16)
+            key[part * half : (part + 1) * half, at] = rows.astype(jnp.bfloat16)
             return
         scale = jnp.zeros((1, block), jnp.float32)
         for h in range(2 * block // LANES):
             scale = jnp.where(head == h, scale_ref[j * 2 * block // LANES + h], scale)
         scale = scale * math.log2(math.e)
-        query[0, :, at] = (rows * (scale * first)).astype(jnp.bfloat16)
-        query[1, :, at] = (rows * (scale * (1.0 - first))).astype(jnp.bfloat16)
+        left, right = rows * (scale * first), rows * (scale * (1.0 - first))
+        for g in range(rows.shape[0] // GROUP):
+            mine = slice(g * GROUP, (g + 1) * GROUP)
+            query[2 * g * GROUP : 2 * (g + 1) * GROUP, at] = jnp.concatenate(
+                [left[mine], right[mine]], axis=0
+            ).astype(jnp.bfloat16)
 
     staged(tasks, [multiply, measure, keep])
 
 
 def attend(wraps, query, key, value, open_ref, prob, ctx):
-    width = query.shape[2]
+    width = query.shape[1]
     windows = len(wraps)
-    pairs = query.shape[1] // windows // GROUP
+    pairs = query.shape[0] // windows // (2 * GROUP)
     is_first = lax.broadcasted_iota(jnp.int32, (GROUP, LANES), 1) < LANES // 2
     ones = jnp.ones((2 * GROUP, LANES), jnp.bfloat16)
     tasks = [
-        (w, pair, slice(j * LANES, (j + 1) * LANES))
-        for w in range(windows)
-        for pair in range(pairs)
-        for j in range(width // LANES)
+        (w, j, pair) for w in range(windows) for j in range(width // LANES) for pair in range(pairs)
     ]
-    slots = {task[:2] + (task[2].start,): u % prob.shape[0] for u, task in enumerate(tasks)}
+    done = []
 
     def place(task):
-        w, pair, at = task
-        base = (w * pairs + pair) * GROUP
-        return slice(base, base + GROUP), at, slots[(w, pair, at.start)]
+        w, j, pair = task
+        rows = slice((w * pairs + pair) * 2 * GROUP, (w * pairs + pair + 1) * 2 * GROUP)
+        return rows, slice(j * LANES, (j + 1) * LANES), tasks.index(task) % prob.shape[0]
 
     def score(task, _):
         rows, at, slot = place(task)
-        wrap = 0 if wraps[task[0]] is None else wraps[task[0]]
-        q = jnp.concatenate([query[0, rows, at], query[1, rows, at]], axis=0)
-        k = jnp.concatenate([key[0, rows, at], key[1, rows, at]], axis=0)
-        raw = lax.dot_general(q, k, (((1,), (1,)), ((), ())), preferred_element_type=jnp.float32)
-        prob[slot] = jnp.exp2(raw).astype(jnp.bfloat16) * open_ref[task[1], wrap]
+        wrap, pair = wraps[task[0]], task[2]
+        raw = lax.dot_general(
+            query[rows, at],
+            key[rows, at],
+            (((1,), (1,)), ((), ())),
+            preferred_element_type=jnp.float32,
+        )
+        raw = jnp.exp2(raw).astype(jnp.bfloat16)
+        if wrap is not None or pair == pairs - 1:
+            raw = raw * open_ref[pair, 0 if wrap is None else wrap]
+        prob[slot] = raw
 
     def wait(task, _):
         return None
 
     def mix(task, _):
         rows, at, slot = place(task)
-        v = jnp.concatenate([value[0, rows, at], value[1, rows, at]], axis=0)
-        out = mm(prob[slot], jnp.concatenate([v, ones], axis=1))
+        out = mm(prob[slot], jnp.concatenate([value[rows, at], ones], axis=1))
         top = jnp.where(is_first, out[:GROUP, :LANES], out[GROUP:, :LANES])
         total = jnp.where(is_first, out[:GROUP, LANES:], out[GROUP:, LANES:])
-        ctx[rows, at] = (top / total).astype(jnp.bfloat16)
+        done.append(top / total)
+        if len(done) == pairs:
+            base = task[0] * pairs * GROUP
+            ctx[base : base + pairs * GROUP, at] = jnp.concatenate(done, axis=0).astype(jnp.bfloat16)
+            done.clear()
 
     staged(tasks, [score, wait, mix])
 
 
-def attention_scratch(rows, width):
+def attention_scratch(rows, width, depth):
     bf16 = jnp.bfloat16
     return [
-        pltpu.VMEM((2, rows, width), bf16),
-        pltpu.VMEM((2, rows, width), bf16),
-        pltpu.VMEM((2, rows, width), bf16),
+        pltpu.VMEM((rows, depth), bf16),
+        pltpu.VMEM((2 * rows, depth), bf16),
+        pltpu.VMEM((2 * rows, width), bf16),
+        pltpu.VMEM((2 * rows, width), bf16),
+        pltpu.VMEM((2 * rows, width), bf16),
         pltpu.VMEM((8, 2 * GROUP, 2 * GROUP), bf16),
         pltpu.VMEM((rows, width), bf16),
     ]
 
 
-def fill_windows(dst, pick, sources):
-    span = dst.shape[0] // len(sources)
-    for w, chunks in enumerate(sources):
-        rows = sum(mm(p, chunk) for p, chunk in zip(pick, chunks))
-        dst[w * span : (w + 1) * span] = rows.astype(jnp.bfloat16)
+def keep_window(w, mine, theirs, own, both):
+    span = mine.shape[0]
+    own[w * span : (w + 1) * span] = mine.astype(jnp.bfloat16)
+    parts = []
+    for at in range(0, span, GROUP):
+        parts += [mine[at : at + GROUP], theirs[at : at + GROUP]]
+    both[2 * w * span : 2 * (w + 1) * span] = jnp.concatenate(parts, axis=0).astype(jnp.bfloat16)
 
 
 def block_rows(own, ctx, output_ref, gain_ref, offset_ref):
@@ -300,10 +341,10 @@
     return (own[...].astype(jnp.float32) + branch).astype(jnp.bfloat16)
 
 
-def merge_rows(first, patch_ref, merge_ref, gain_ref, offset_ref):
-    cells = patch_ref.shape[0] // 4
+def merge_rows(first, patch, merge_ref, gain_ref, offset_ref):
+    cells = patch.shape[0] // 4
     channels = first.shape[1]
-    part = mm(patch_ref[...], first[...]).astype(jnp.bfloat16)
+    part = mm(patch, first[...]).astype(jnp.bfloat16)
     total = None
     for g in range(4):
         term = mm(part[g * cells : (g + 1) * cells], merge_ref[g * channels : (g + 1) * channels])
@@ -323,37 +364,50 @@
     output_ref,
     gain_ref,
     offset_ref,
-    merge_ref,
     merge_gain_ref,
     merge_offset_ref,
     open_ref,
-    pick_ref,
-    patch_ref,
+    table_ref,
+    merge_hbm,
     *rest,
 ):
-    if len(rest) == 9:
+    if len(rest) == 11:
         side, (merged_ref, *rest) = 0, rest
     else:
-        side, (near_ref, edge_ref, merged_ref, up_ref, *rest) = 1, rest
-    own, other, query, key, value, prob, ctx, first = rest
+        side, (near_ref, merged_ref, up_ref, *rest) = 1, rest
+    merge_ref, sem, first, own, both, query, key, value, prob, ctx = rest
+    fetch = pltpu.make_async_copy(merge_hbm, merge_ref, sem)
+    fetch.start()
     chunks = own_ref.shape[0]
-    pick = [pick_ref[0], pick_ref[1]]
-    for dst, src, top, bottom in (
-        (own, own_ref, top_ref[side], bottom_ref[side]),
-        (other, other_ref, other_rim_ref[0], other_rim_ref[1]),
+    tokens = own_ref.shape[1]
+    span = open_ref.shape[0] * GROUP
+    pick = [one_hot(column_of(table_ref, PICK + s, slice(0, span)), tokens) for s in range(2)]
+    lines = []
+    for src, top, bottom in (
+        (own_ref, top_ref[side], bottom_ref[side]),
+        (other_ref, other_rim_ref[0], other_rim_ref[1]),
     ):
-        line = [top] + [src[e] for e in range(chunks)] + [bottom]
-        fill_windows(dst, pick, list(zip(line[::2], line[1::2])))
-    project(own, other, packed_ref, scale_ref, query, key, value)
+        lines.append([top] + [src[e] for e in range(chunks)] + [bottom])
+    for w in range(chunks // 2 + 1):
+        mine, theirs = (
+            mm(pick[0], line[2 * w]) + mm(pick[1], line[2 * w + 1]) for line in lines
+        )
+        keep_window(w, mine, theirs, own, both)
+    project(own, both, packed_ref, scale_ref, query, key, value)
     wraps = [flags[0]] + [None] * (chunks // 2 - 1) + [flags[1]]
     attend(wraps, query, key, value, open_ref, prob, ctx)
     first[...] = block_rows(own, ctx, output_ref, gain_ref, offset_ref)
-    merged = merge_rows(first, patch_ref, merge_ref, merge_gain_ref, merge_offset_ref)
+    fetch.wait()
+    cells = 4 * merged_ref.shape[0]
+    patch = one_hot(column_of(table_ref, PATCH, slice(0, cells)), first.shape[0])
+    merged = merge_rows(first, patch, merge_ref, merge_gain_ref, merge_offset_ref)
     merged_ref[...] = merged
     if side:
-        reach = edge_ref.shape[2]
-        up_ref[...] = (
-            mm(edge_ref[0], near_ref[:reach]) + mm(edge_ref[1], merged[:reach])
+        count = up_ref.shape[0]
+        reach = padded(count // 2)
+        up_ref[...] = sum(
+            mm(one_hot(column_of(table_ref, EDGE + s, slice(0, count)), reach), rows[:reach])
+            for s, rows in enumerate((near_ref, merged))
         ).astype(jnp.bfloat16)
 
 
@@ -371,14 +425,13 @@
     gain_ref,
     offset_ref,
     open_ref,
-    coarse_ref,
-    send_at_ref,
+    table_ref,
     second_ref,
     send_ref,
     return_ref,
     return_near_ref,
     own,
-    other,
+    both,
     query,
     key,
     value,
@@ -393,19 +446,20 @@
         reach = [(0, low, high), (1, low, high)]
         if w == windows - 1:
             reach.append((2, 0, 2 * small))
-        at = slice(w * span, (w + 1) * span)
         mine = theirs = 0.0
         for s, low, high in reach:
-            pick = coarse_ref[s, at, : high - low]
+            at = slice(w * span, (w + 1) * span)
+            pick = one_hot(column_of(table_ref, COARSE + s, at), high - low)
             mine += mm(pick, (near_ref, far_ref, rim_ref)[s][low:high])
             theirs += mm(pick, (other_near_ref, other_far_ref, other_rim_ref)[s][low:high])
-        own[at] = mine.astype(jnp.bfloat16)
-        other[at] = theirs.astype(jnp.bfloat16)
-    project(own, other, packed_ref, scale_ref, query, key, value)
+        keep_window(w, mine, theirs, own, both)
+    project(own, both, packed_ref, scale_ref, query, key, value)
     attend([None] * (windows - 1) + [flags[1]], query, key, value, open_ref, prob, ctx)
     second = block_rows(own, ctx, output_ref, gain_ref, offset_ref)
     second_ref[...] = second
-    rows = mm(send_at_ref[...], second).astype(jnp.bfloat16)
+    counts = [padded(ref.shape[0]) for ref in (send_ref, return_ref, return_near_ref)]
+    index = parity_column(table_ref, SEND, 1, flags[2], slice(0, sum(counts)))
+    rows = mm(one_hot(index, second.shape[0]), second).astype(jnp.bfloat16)
     at = 0
     for dst in (send_ref, return_ref, return_near_ref):
         count = dst.shape[0]
@@ -413,27 +467,52 @@
         at += padded(count)
 
 
-def place_kernel(second_ref, near_ref, back_ref, back_near_ref, a_ref, b_ref, c_ref, out_ref):
-    rows, _, columns, pair, _ = out_ref.shape
-    step = columns * pair
+def place(pieces, out_ref, rows_ref, sem, low):
+    rows, _, columns, pair, _ = rows_ref.shape
+    block = sum(mm(one_hot(index, ref.shape[0]), ref[...]) for index, ref in pieces)
+    for r in range(rows):
+        for c in range(columns):
+            at = (r * columns + c) * pair
+            rows_ref[r, 0, c] = block[at : at + pair].astype(jnp.bfloat16)
+    copy = pltpu.make_async_copy(rows_ref, out_ref.at[low : low + rows], sem)
+    copy.start()
+    copy.wait()
+
+
+def place_columns(flags, table_ref, out_ref, which, early):
+    step = out_ref.shape[2] * out_ref.shape[3]
     edge = HALF_LAT * step
-    early = mm(c_ref[0], back_ref[...]) + mm(c_ref[1], back_near_ref[...])
-    late = mm(a_ref[...], second_ref[...]) + mm(b_ref[...], near_ref[...])
-    for r in range(rows):
-        block, base = (early, r * step) if r < HALF_LAT else (late, r * step - edge)
-        for c in range(columns):
-            out_ref[r, 0, c] = block[base + c * pair : base + (c + 1) * pair].astype(jnp.bfloat16)
-
-
-def call(kernel, outs, scratch, scalars, operands):
+    rows = slice(0, edge) if early else slice(edge, step * out_ref.shape[0])
+    return [parity_column(table_ref, PLACE + s, 4, flags[2], rows) for s in which]
+
+
+def late_kernel(flags, second_ref, near_ref, table_ref, out_ref, rows_ref, sem):
+    index = place_columns(flags, table_ref, out_ref, (0, 1), False)
+    place(zip(index, (second_ref, near_ref)), out_ref, rows_ref, sem, HALF_LAT)
+
+
+def early_kernel(flags, back_ref, back_near_ref, table_ref, _, out_ref, rows_ref, sem):
+    index = place_columns(flags, table_ref, out_ref, (2, 3), True)
+    place(zip(index, (back_ref, back_near_ref)), out_ref, rows_ref, sem, 0)
+
+
+def call(
+    kernel, outs, scratch, scalars, operands, fixed=(), late=(), alias=None, held=False, room=SECOND_BYTES
+):
     vmem = pl.BlockSpec(memory_space=pltpu.VMEM)
+    hbm = pl.BlockSpec(memory_space=pltpu.HBM)
     return pl.pallas_call(
         kernel,
         out_shape=outs,
-        in_specs=[pl.BlockSpec(memory_space=pltpu.SMEM)] * len(scalars) + [vmem] * len(operands),
-        out_specs=[vmem] * len(outs),
+        in_specs=[pl.BlockSpec(memory_space=pltpu.SMEM)] * len(scalars)
+        + [vmem] * len(operands)
+        + [hbm] * len(fixed)
+        + [vmem] * len(late),
+        out_specs=[hbm if held else vmem] * len(outs),
         scratch_shapes=scratch,
-    )(*scalars, *operands)
+        input_output_aliases=alias or {},
+        compiler_params=pltpu.CompilerParams(vmem_limit_bytes=room),
+    )(*scalars, *operands, *fixed, *late)
 
 
 def far_of(i, n):
@@ -505,29 +584,26 @@
     near_other_rim = near_swap(jnp.stack([top[0], bottom[0]]))
     far_other_rim = far_swap(jnp.stack([top[1], bottom[1]]))
 
-    zero = jnp.minimum(lat_pos, 0)
     opened = jnp.asarray(open_tables(levels), bf16)
     cells = half_rows * levels * HALF_LON // 2
     small = jax.ShapeDtypeStruct((cells, wide), bf16)
     edge = jax.ShapeDtypeStruct((tokens, wide), bf16)
 
-    def scratch(count, width, depth):
-        rows = count * span
-        return [pltpu.VMEM((rows, depth), bf16)] * 2 + attention_scratch(rows, width)
-
     shared = [packed_first, output_first, gain_first[None], offset_first[None]]
-    shared += [merge_weight, merge_gain[None], merge_offset[None], opened]
-    shared += [
-        one_hot(np.stack(fine_gather(levels)), tokens, zero),
-        one_hot(patch_gather(levels, row_count), windows * span, zero),
-    ]
-    buffers = scratch(windows, inner, channels) + [pltpu.VMEM((windows * span, channels), bf16)]
+    shared += [merge_gain[None], merge_offset[None], opened]
+    table = jnp.asarray(index_table(levels, row_count))
+    shared += [table]
+    buffers = [pltpu.VMEM(merge_weight.shape, bf16), pltpu.SemaphoreType.DMA]
+    buffers += [pltpu.VMEM((windows * span, channels), bf16)]
+    buffers += attention_scratch(windows * span, inner, channels)
     (merged_near,) = call(
         side_kernel,
         [small],
         buffers,
         [scale_first, flags],
         [near, near_other, top, bottom, near_other_rim] + shared,
+        [merge_weight],
+        room=FIRST_BYTES,
     )
     other_near = far_swap(merged_near)
     merged_far, edge_up = call(
@@ -535,9 +611,10 @@
         [small, edge],
         buffers,
         [scale_first, flags],
-        [far, far_other, top, bottom, far_other_rim]
-        + shared
-        + [merged_near, one_hot(edge_gather(levels), padded(tokens // 2), zero)],
+        [far, far_other, top, bottom, far_other_rim] + shared,
+        [merge_weight],
+        [merged_near],
+        room=FIRST_BYTES,
     )
     other_far = far_swap(merged_far)
     other_rim = ring(edge_up, -1, far_of)
@@ -546,12 +623,6 @@
     windows = half_rows // WLAT
     share = levels // 2 * HALF_LON
 
-    def chosen(table):
-        odd_table, even_table = (jnp.asarray(table(levels, half_rows, e)) for e in (False, True))
-        return jnp.where(is_even, even_table, odd_table)
-
-    places = chosen(place_gather)
-    start = HALF_LAT * WLON * levels // 2
     back = jax.ShapeDtypeStruct((HALF_LAT * share, wide), bf16)
     second, send, back_same, back_near = call(
         second_kernel,
@@ -561,7 +632,7 @@
             back,
             back,
         ],
-        scratch(windows, second_inner, wide),
+        attention_scratch(windows * span, second_inner, wide),
         [scale_second, flags],
         [
             merged_near,
@@ -575,27 +646,35 @@
             gain_second[None],
             offset_second[None],
             opened,
-            one_hot(coarse_gather(levels, half_rows), padded(tokens), zero),
-            one_hot(chosen(send_gather), windows * span, zero),
+            table,
         ],
     )
     back_near = ring(back_near, 1, lambda j, m: j ^ 1)
     back_same = ring(back_same, 1, lambda j, m: j)
     received = near_swap(send)
+    shape = (half_rows, 1, WLON, levels // 2, wide)
+    whole = [jax.ShapeDtypeStruct(shape, bf16)]
+
+    def room(rows):
+        return [pltpu.VMEM((rows,) + shape[1:], bf16), pltpu.SemaphoreType.DMA]
+
     (out,) = call(
-        place_kernel,
-        [jax.ShapeDtypeStruct((half_rows, 1, WLON, levels // 2, wide), bf16)],
-        [],
-        [],
-        [
-            second,
-            received,
-            back_same,
-            back_near,
-            one_hot(places[0, start:], second.shape[0], zero),
-            one_hot(places[1, start:], received.shape[0], zero),
-            one_hot(places[2:, :start], back_same.shape[0], zero),
-        ],
+        late_kernel,
+        whole,
+        room(half_rows - HALF_LAT),
+        [flags],
+        [second, received, table],
+        held=True,
+    )
+    (out,) = call(
+        early_kernel,
+        whole,
+        room(HALF_LAT),
+        [flags],
+        [back_same, back_near, table],
+        [out],
+        alias={4: 0},
+        held=True,
     )
     return jnp.transpose(out, (0, 1, 3, 2, 4))
 

time: 86.7 us -> 78.8 us (0.909)
  Pallas kernels: 36.1 us -> 26.4 us
  waiting for transfers between devices: 15 us -> 23.8 us
  other arithmetic: 8.59 us -> 2.8 us
  starting transfers between devices: 21.3 us -> 19.5 us
    pallas_call x4 -> x5, Pallas kernels: 36.1 us -> 26.4 us  [call(): pl.pallas_call(kernel, out_shape=outs, in_specs=[pl.BlockSpec(memory_spac...]
    convert_element_type x8 -> x0, other arithmetic: 6.5 us -> none  [one_hot(): (index == lax.broadcasted_iota(jnp.int32, (1, width), 1)).astype(jnp.bflo...]
    ppermute x4, waiting for transfers between devices: 0.01 us -> 3.94 us  [far_swap(): return lax.ppermute(value, 'lon', [(i, far_of(i, n)) for i in range(n)])]
    ppermute x4, waiting for transfers between devices: 14.2 us -> 17.8 us  [ring(): return lax.ppermute(value, ('lat', 'lon'), links)]
    unnamed x48 -> x32, local copies, waits for them, and re-layouts: 3.99 us -> 1.12 us
    ppermute x4, starting transfers between devices: 6.35 us -> 3.86 us  [ring(): return lax.ppermute(value, ('lat', 'lon'), links)]
    ppermute x3, waiting for transfers between devices: 0.77 us -> 2.05 us  [near_swap(): lax.ppermute(value, 'lon', [(i, i ^ 1) for i in range(lax.axis_size('lon'...]
    reshape x1, local copies, waits for them, and re-layouts: 0.2 us -> 1.47 us  [body(): far = jnp.where(is_even, left, right).reshape(chunks, tokens, channels)]
  transfers between devices with their start and end apart: 13 -> 13, of which waited for: 5 -> 7; matrix products, arithmetic and copies ran while one was open for 9% -> 6% of each run, Pallas kernels for 29% -> 14%
where the time goes in v3:
time: 78.8 us; the launch traced here: 78.5 us
  Pallas kernels  26.4 us (34%)
  waiting for transfers between devices  23.8 us (30%)
  starting transfers between devices  19.5 us (25%)
  local copies, waits for them, and re-layouts  5.4 us (7%)
  other arithmetic  2.8 us (4%)
    pallas_call x5, Pallas kernels, call(): pl.pallas_call(kernel, out_shape=outs, in_specs=[pl.BlockSpec(memory_spac...  26.4 us
    ppermute x4, waiting for transfers between devices, ring(): return lax.ppermute(value, ('lat', 'lon'), links)  17.8 us
    ppermute x4, starting transfers between devices, far_swap(): return lax.ppermute(value, 'lon', [(i, far_of(i, n)) for i in range(n)])  7.99 us
    ppermute x2, starting transfers between devices, shift(): lax.ppermute(value, 'lat', [(i, i + by) for i in range(n) if 0 <= i + by...  7.44 us
    ppermute x4, waiting for transfers between devices, far_swap(): return lax.ppermute(value, 'lon', [(i, far_of(i, n)) for i in range(n)])  3.94 us
    ppermute x4, starting transfers between devices, ring(): return lax.ppermute(value, ('lat', 'lon'), links)  3.86 us
    ppermute x3, waiting for transfers between devices, near_swap(): lax.ppermute(value, 'lon', [(i, i ^ 1) for i in range(lax.axis_size('lon'...  2.05 us
  transfers between devices with their start and end apart: 13, of which 7 were waited for; matrix products, arithmetic and copies ran while one was open for 6% of the time, Pallas kernels for 14%

profile of v3, /device:TPU:0, one launch (start us, length us, event | category | flops | bytes accessed | tf_op | source)
XLA Modules:
  0.0 78.5 jit_solution(11621934634095077756)
XLA Ops:
  0.0 1.3 %broadcast_select_fusion = (bf16[24,4,6,512]{3,0,2,1:T(8,128)(2,1)S(1)}, bf16[24,4,6,512]{3,0,2,1:T(8,128)(2,1)S(1)}) fusion(pred[]{:T(512)S(6)} %eq.9, bf16[24,4,12,512]{3,0,2,1:T(8,128)(2,1)} %bitcast.20), kind=kLoop, calls=%fused_computation | loop fusion | flops 589824 | bytes 2359297 | tf_op jit(solution)/shard_map/jit(_where)/select_n | solution.py:578
  1.6 0.7 pad_maximum_fusion.1
  2.3 1.3 %collective-permute-start.2 = (bf16[2,72,512]{2,1,0:T(8,128)(2,1)}, bf16[2,72,512]{2,1,0:T(8,128)(2,1)S(1)}, u32[]{:S(2)}, u32[]{:S(2)}) collective-permute-start(bf16[2,72,512]{2,1,0:T(8,128)(2,1)} %pad_maximum_fusion.1), channel_id=1, source_target_pairs={{8,0},{16,8},{24,16},{9,1},{17,9},{25,17},{10,2},{18,10},{26,18},{... | collective-permute-start | bytes 442376 | tf_op jit(solution)/shard_map/ppermute | solution.py:539
  4.4 6.2 %collective-permute-start.1 = (bf16[2,72,512]{2,1,0:T(8,128)(2,1)}, bf16[2,72,512]{2,1,0:T(8,128)(2,1)}, u32[]{:S(2)}, u32[]{:S(2)}) collective-permute-start(bf16[2,72,512]{2,1,0:T(8,128)(2,1)} %pad_maximum_fusion), channel_id=1, source_target_pairs={{0,8},{8,16},{16,24},{1,9},{9,17},{17,25},{2,10},{10,18},{18,26},{... | collective-permute-start | bytes 442376 | tf_op jit(solution)/shard_map/ppermute | solution.py:539
  11.1 1.1 %copy.30 = bf16[24,4,6,512]{3,2,1,0:T(8,128)(2,1)} copy(bf16[24,4,6,512]{3,0,2,1:T(8,128)(2,1)S(1)} %get-tuple-element.17) | data formatting | bytes 1179648 | tf_op jit(solution)/shard_map/jit(_where)/select_n | solution.py:578
  12.2 1.5 %reshape.11.own_ref = bf16[8,72,512]{2,1,0:T(8,128)(2,1)S(1)} reshape(bf16[24,4,6,512]{3,2,1,0:T(8,128)(2,1)} %copy.30) | data formatting | bytes 1179648 | tf_op jit(solution)/shard_map/reshape | solution.py:578
  13.7 4.3 %collective-permute-start.4 = (bf16[8,72,512]{2,1,0:T(8,128)(2,1)S(1)}, bf16[8,72,512]{2,1,0:T(8,128)(2,1)}, u32[]{:S(2)}, u32[]{:S(2)}) collective-permute-start(bf16[8,72,512]{2,1,0:T(8,128)(2,1)S(1)} %reshape.11.own_ref), channel_id=1, source_target_pairs={{0,7},{1,2},{2,1},{3,4},{4,3},{5,6},{6,5},{7,0},{8,15},{9,10},{10,... | collective-permute-start | bytes 1769480 | tf_op jit(solution)/shard_map/ppermute | solution.py:528
  18.0 0.9 %fusion.2 = (bf16[1,72,512]{2,1,0:T(8,128)(2,1)S(1)}, bf16[1,72,512]{2,1,0:T(8,128)(2,1)S(1)}) fusion(bf16[2,72,512]{2,1,0:T(8,128)(2,1)} %collective-permute-done.1.top_ref), kind=kLoop, calls=%fused_computation.9 | loop fusion | bytes 294912 | tf_op jit(solution)/shard_map/slice | solution.py:585
  19.3 1.3 %collective-permute-done.3.other_rim_ref = bf16[2,72,512]{2,1,0:T(8,128)(2,1)S(1)} collective-permute-done((bf16[2,72,512]{2,1,0:T(8,128)(2,1)S(1)}, bf16[2,72,512]{2,1,0:T(8,128)(2,1)S(1)}, u32[]{:S(2)}, u32[]{:S(2)}) %collective-permute-start.3) | collective-permute-done | bytes 147488 | tf_op jit(solution)/shard_map/ppermute | solution.py:523
  20.6 1.0 %copy-done.4 = bf16[512,512]{1,0:T(8,128)(2,1)S(1)} copy-done((bf16[512,512]{1,0:T(8,128)(2,1)S(1)}, bf16[512,512]{1,0:T(8,128)(2,1)}, u32[]{:S(2)}) %copy-start.4) | copy-done | bytes 524312
  21.7 8.7 %shard_map.163.rest_0_.near_ref = bf16[144,1024]{1,0:T(8,128)(2,1)S(1)} custom-call(f32[8]{0:T(128)S(1)} %copy-done.13, s32[3]{0:T(128)S(1)} %compare_convert_fusion.flags, bf16[8,72,512]{2,1,0:T(8,128)(2,1)S(1)} %reshape.10.own_ref, bf16[8,72,512]{2,1,0:T(8,128)(2,1)} %collective-permute-done.other_ref, bf16[2,72,512]{2,1,0:T(8,128)(2,1)} %collective-permute-done.1.top_ref, ...), custom_call_target="tpu_custom_call" | custom-call | tf_op jit(solution)/shard_map/pallas_call | solution.py:504
  30.4 3.9 %collective-permute-done.5.other_rim_ref = bf16[2,72,512]{2,1,0:T(8,128)(2,1)S(1)} collective-permute-done((bf16[2,72,512]{2,1,0:T(8,128)(2,1)S(1)}, bf16[2,72,512]{2,1,0:T(8,128)(2,1)S(1)}, u32[]{:S(2)}, u32[]{:S(2)}) %collective-permute-start.5) | collective-permute-done | bytes 147488 | tf_op jit(solution)/shard_map/ppermute | solution.py:528
  34.3 9.0 %shard_map.164 = (bf16[144,1024]{1,0:T(8,128)(2,1)S(1)}, bf16[72,1024]{1,0:T(8,128)(2,1)S(1)}) custom-call(f32[8]{0:T(128)S(1)} %copy-done.13, s32[3]{0:T(128)S(1)} %compare_convert_fusion.flags, bf16[8,72,512]{2,1,0:T(8,128)(2,1)S(1)} %reshape.11.own_ref, bf16[8,72,512]{2,1,0:T(8,128)(2,1)} %collective-permute-done.4.other_ref, ...), custom_call_target="tpu_custom_call" | custom-call | tf_op jit(solution)/shard_map/pallas_call | solution.py:504
  43.4 1.7 %collective-permute-start.8 = (bf16[144,1024]{1,0:T(8,128)(2,1)S(1)}, bf16[144,1024]{1,0:T(8,128)(2,1)S(1)}, u32[]{:S(2)}, u32[]{:S(2)}) collective-permute-start(bf16[144,1024]{1,0:T(8,128)(2,1)S(1)} %get-tuple-element.11.far_ref), channel_id=1, source_target_pairs={{0,7},{1,2},{2,1},{3,4},{4,3},{5,6},{6,5},{7,0},{8,15},{9,10},{10,... | collective-permute-start | bytes 884744 | tf_op jit(solution)/shard_map/ppermute | solution.py:528
  45.1 1.9 %collective-permute-start.7 = (bf16[144,1024]{1,0:T(8,128)(2,1)S(1)}, bf16[144,1024]{1,0:T(8,128)(2,1)S(1)}, u32[]{:S(2)}, u32[]{:S(2)}) collective-permute-start(bf16[144,1024]{1,0:T(8,128)(2,1)S(1)} %shard_map.163.rest_0_.near_ref), channel_id=1, source_target_pairs={{0,7},{1,2},{2,1},{3,4},{4,3},{5,6},{6,5},{7,0},{8,15},{9,10},{10,... | collective-permute-start | bytes 884744 | tf_op jit(solution)/shard_map/ppermute | solution.py:528
  47.0 3.2 %collective-permute-start.9 = (bf16[72,1024]{1,0:T(8,128)(2,1)S(1)}, bf16[72,1024]{1,0:T(8,128)(2,1)S(1)}, u32[]{:S(2)}, u32[]{:S(2)}) collective-permute-start(bf16[72,1024]{1,0:T(8,128)(2,1)S(1)} %get-tuple-element.12), channel_id=1, source_target_pairs={{0,31},{1,26},{2,25},{3,28},{4,27},{5,30},{6,29},{7,24},{8,7},{9,2... | collective-permute-start | bytes 442376 | tf_op jit(solution)/shard_map/ppermute | solution.py:534
  50.2 2.0 %collective-permute-done.6.rim_ref = bf16[72,1024]{1,0:T(8,128)(2,1)S(1)} collective-permute-done((bf16[72,1024]{1,0:T(8,128)(2,1)S(1)}, bf16[72,1024]{1,0:T(8,128)(2,1)S(1)}, u32[]{:S(2)}, u32[]{:S(2)}) %collective-permute-start.6) | collective-permute-done | bytes 147488 | tf_op jit(solution)/shard_map/ppermute | solution.py:534
  52.1 12.3 %collective-permute-done.9.other_rim_ref = bf16[72,1024]{1,0:T(8,128)(2,1)S(1)} collective-permute-done((bf16[72,1024]{1,0:T(8,128)(2,1)S(1)}, bf16[72,1024]{1,0:T(8,128)(2,1)S(1)}, u32[]{:S(2)}, u32[]{:S(2)}) %collective-permute-start.9) | collective-permute-done | bytes 147488 | tf_op jit(solution)/shard_map/ppermute | solution.py:534
  64.5 5.2 %shard_map.165 = (bf16[288,1024]{1,0:T(8,128)(2,1)S(1)}, bf16[108,1024]{1,0:T(8,128)(2,1)S(1)}, bf16[36,1024]{1,0:T(8,128)(2,1)S(1)}, bf16[36,1024]{1,0:T(8,128)(2,1)S(1)}) custom-call(f32[8]{0:T(128)S(1)} %copy-done.14, s32[3]{0:T(128)S(1)} %compare_convert_fusion.flags, bf16[144,1024]{1,0:T(8,128)(2,1)S(1)} %shard_map.163.rest_0_.near_ref, ...), custom_call_target="tpu_custom_call" | custom-call | tf_op jit(solution)/shard_map/pallas_call | solution.py:504
  70.5 0.8 collective-permute-done.12.near_ref
  71.2 2.0 %shard_map.166._ = bf16[12,1,12,2,1024]{4,3,2,1,0:T(2,128)(2,1)} custom-call(s32[3]{0:T(128)S(1)} %compare_convert_fusion.flags, bf16[288,1024]{1,0:T(8,128)(2,1)S(1)} %get-tuple-element.15.second_ref, bf16[108,1024]{1,0:T(8,128)(2,1)S(1)} %collective-permute-done.12.near_ref, s32[576,18]{1,0:T(8,128)S(1)} %copy-done), custom_call_target="tpu_custom_call" | custom-call | tf_op jit(solution)/shard_map/pallas_call | solution.py:504
  73.2 2.8 %collective-permute-done.10.back_ref = bf16[36,1024]{1,0:T(8,128)(2,1)S(1)} collective-permute-done((bf16[36,1024]{1,0:T(8,128)(2,1)S(1)}, bf16[36,1024]{1,0:T(8,128)(2,1)S(1)}, u32[]{:S(2)}, u32[]{:S(2)}) %collective-permute-start.10) | collective-permute-done | bytes 73760 | tf_op jit(solution)/shard_map/ppermute | solution.py:534
  76.0 0.7 collective-permute-done.11.back_near_ref
  76.7 1.6 %shard_map.167 = bf16[12,1,12,2,1024]{4,3,2,1,0:T(2,128)(2,1)} custom-call(s32[3]{0:T(128)S(1)} %compare_convert_fusion.flags, bf16[36,1024]{1,0:T(8,128)(2,1)S(1)} %collective-permute-done.10.back_ref, bf16[36,1024]{1,0:T(8,128)(2,1)S(1)} %collective-permute-done.11.back_near_ref, s32[576,18]{1,0:T(8,128)S(1)} %copy-done, ...), custom_call_target="tpu_custom_call", output_to_operand_aliasing={{}: (4, {})} | custom-call | tf_op jit(solution)/shard_map/pallas_call | solution.py:504
  (60 shorter events, 2.7 us)
Async XLA Ops:
  2.3 15.7 %collective-permute-start.2 = (bf16[2,72,512]{2,1,0:T(8,128)(2,1)}, bf16[2,72,512]{2,1,0:T(8,128)(2,1)S(1)}, u32[]{:S(2)}, u32[]{:S(2)}) collective-permute-start(bf16[2,72,512]{2,1,0:T(8,128)(2,1)} %pad_maximum_fusion.1), channel_id=1, source_target_pairs={{8,0},{16,8},{24,16},{9,1},{17,9},{25,17},{10,2},{18,10},{26,18},{... | collective-permute-start | bytes 442376 | tf_op jit(solution)/shard_map/ppermute | solution.py:539
  4.4 13.6 %collective-permute-start.1 = (bf16[2,72,512]{2,1,0:T(8,128)(2,1)}, bf16[2,72,512]{2,1,0:T(8,128)(2,1)}, u32[]{:S(2)}, u32[]{:S(2)}) collective-permute-start(bf16[2,72,512]{2,1,0:T(8,128)(2,1)} %pad_maximum_fusion), channel_id=1, source_target_pairs={{0,8},{8,16},{16,24},{1,9},{9,17},{17,25},{2,10},{10,18},{18,26},{... | collective-permute-start | bytes 442376 | tf_op jit(solution)/shard_map/ppermute | solution.py:539
  11.0 9.6 %collective-permute-start = (bf16[8,72,512]{2,1,0:T(8,128)(2,1)S(1)}, bf16[8,72,512]{2,1,0:T(8,128)(2,1)}, u32[]{:S(2)}, u32[]{:S(2)}) collective-permute-start(bf16[8,72,512]{2,1,0:T(8,128)(2,1)S(1)} %reshape.10.own_ref), channel_id=1, source_target_pairs={{0,1},{1,0},{2,3},{3,2},{4,5},{5,4},{6,7},{7,6},{8,9},{9,8},{10,11... | collective-permute-start | bytes 1769480 | tf_op jit(solution)/shard_map/ppermute | solution.py:523
  12.2 8.4 %copy-start.3 = (bf16[2,2,144,144]{3,2,1,0:T(8,128)(2,1)S(1)}, bf16[2,2,144,144]{3,2,1,0:T(8,128)(2,1)}, u32[]{:S(2)}) copy-start(bf16[2,2,144,144]{3,2,1,0:T(8,128)(2,1)} %constant.30.clone.open_ref) | copy-start | bytes 497668
  12.2 8.4 %copy-start.7 = (f32[1024]{0:T(1024)S(1)}, f32[1024]{0:T(1024)}, u32[]{:S(2)}) copy-start(f32[1024]{0:T(1024)} %param.24) | copy-start | bytes 12292
  12.2 8.4 %copy-start.8 = (f32[1024]{0:T(1024)S(1)}, f32[1024]{0:T(1024)}, u32[]{:S(2)}) copy-start(f32[1024]{0:T(1024)} %param.25) | copy-start | bytes 12292
  12.2 8.4 %copy-start.9 = (f32[512]{0:T(512)S(1)}, f32[512]{0:T(512)}, u32[]{:S(2)}) copy-start(f32[512]{0:T(512)} %param.21) | copy-start | bytes 6148
  12.2 8.4 %copy-start.10 = (f32[512]{0:T(512)S(1)}, f32[512]{0:T(512)}, u32[]{:S(2)}) copy-start(f32[512]{0:T(512)} %param.22) | copy-start | bytes 6148
  13.7 20.6 %collective-permute-start.4 = (bf16[8,72,512]{2,1,0:T(8,128)(2,1)S(1)}, bf16[8,72,512]{2,1,0:T(8,128)(2,1)}, u32[]{:S(2)}, u32[]{:S(2)}) collective-permute-start(bf16[8,72,512]{2,1,0:T(8,128)(2,1)S(1)} %reshape.11.own_ref), channel_id=1, source_target_pairs={{0,7},{1,2},{2,1},{3,4},{4,3},{5,6},{6,5},{7,0},{8,15},{9,10},{10,... | collective-permute-start | bytes 1769480 | tf_op jit(solution)/shard_map/ppermute | solution.py:528
  19.0 15.3 %collective-permute-start.5 = (bf16[2,72,512]{2,1,0:T(8,128)(2,1)S(1)}, bf16[2,72,512]{2,1,0:T(8,128)(2,1)S(1)}, u32[]{:S(2)}, u32[]{:S(2)}) collective-permute-start(bf16[2,72,512]{2,1,0:T(8,128)(2,1)S(1)} %pad_maximum_fusion.3), channel_id=1, source_target_pairs={{0,7},{1,2},{2,1},{3,4},{4,3},{5,6},{6,5},{7,0},{8,15},{9,10},{10,... | collective-permute-start | bytes 442376 | tf_op jit(solution)/shard_map/ppermute | solution.py:528
  19.1 1.4 %collective-permute-start.3 = (bf16[2,72,512]{2,1,0:T(8,128)(2,1)S(1)}, bf16[2,72,512]{2,1,0:T(8,128)(2,1)S(1)}, u32[]{:S(2)}, u32[]{:S(2)}) collective-permute-start(bf16[2,72,512]{2,1,0:T(8,128)(2,1)S(1)} %pad_maximum_fusion.2), channel_id=1, source_target_pairs={{0,1},{1,0},{2,3},{3,2},{4,5},{5,4},{6,7},{7,6},{8,9},{9,8},{10,11... | collective-permute-start | bytes 442376 | tf_op jit(solution)/shard_map/ppermute | solution.py:523
  21.7 12.7 %copy-start.5 = (bf16[512,512]{1,0:T(8,128)(2,1)S(1)}, bf16[512,512]{1,0:T(8,128)(2,1)}, u32[]{:S(2)}) copy-start(bf16[512,512]{1,0:T(8,128)(2,1)} %output_ref.4) | copy-start | bytes 1572868
  30.3 34.1 %copy-start.6 = (bf16[512,1024]{1,0:T(8,128)(2,1)S(1)}, bf16[512,1024]{1,0:T(8,128)(2,1)}, u32[]{:S(2)}) copy-start(bf16[512,1024]{1,0:T(8,128)(2,1)} %output_ref.5) | copy-start | bytes 3145732
  30.4 34.1 %copy-start.11 = (f32[1024]{0:T(1024)S(1)}, f32[1024]{0:T(1024)}, u32[]{:S(2)}) copy-start(f32[1024]{0:T(1024)} %param.29) | copy-start | bytes 12292
  30.4 34.1 %copy-start.12 = (f32[1024]{0:T(1024)S(1)}, f32[1024]{0:T(1024)}, u32[]{:S(2)}) copy-start(f32[1024]{0:T(1024)} %param.30) | copy-start | bytes 12292
  30.4 34.1 %copy-start.14 = (f32[8]{0:T(128)S(1)}, f32[8]{0:T(128)}, u32[]{:S(2)}) copy-start(f32[8]{0:T(128)} %scale_ref.5) | copy-start | bytes 100
  34.3 30.1 %copy-start.2 = (bf16[1024,1536]{1,0:T(8,128)(2,1)S(1)}, bf16[1024,1536]{1,0:T(8,128)(2,1)}, u32[]{:S(2)}) copy-start(bf16[1024,1536]{1,0:T(8,128)(2,1)} %packed_ref.5) | copy-start | bytes 9437188
  43.4 21.1 %collective-permute-start.8 = (bf16[144,1024]{1,0:T(8,128)(2,1)S(1)}, bf16[144,1024]{1,0:T(8,128)(2,1)S(1)}, u32[]{:S(2)}, u32[]{:S(2)}) collective-permute-start(bf16[144,1024]{1,0:T(8,128)(2,1)S(1)} %get-tuple-element.11.far_ref), channel_id=1, source_target_pairs={{0,7},{1,2},{2,1},{3,4},{4,3},{5,6},{6,5},{7,0},{8,15},{9,10},{10,... | collective-permute-start | bytes 884744 | tf_op jit(solution)/shard_map/ppermute | solution.py:528
  45.1 19.3 %collective-permute-start.7 = (bf16[144,1024]{1,0:T(8,128)(2,1)S(1)}, bf16[144,1024]{1,0:T(8,128)(2,1)S(1)}, u32[]{:S(2)}, u32[]{:S(2)}) collective-permute-start(bf16[144,1024]{1,0:T(8,128)(2,1)S(1)} %shard_map.163.rest_0_.near_ref), channel_id=1, source_target_pairs={{0,7},{1,2},{2,1},{3,4},{4,3},{5,6},{6,5},{7,0},{8,15},{9,10},{10,... | collective-permute-start | bytes 884744 | tf_op jit(solution)/shard_map/ppermute | solution.py:528
  47.0 5.1 %collective-permute-start.6 = (bf16[72,1024]{1,0:T(8,128)(2,1)S(1)}, bf16[72,1024]{1,0:T(8,128)(2,1)S(1)}, u32[]{:S(2)}, u32[]{:S(2)}) collective-permute-start(bf16[72,1024]{1,0:T(8,128)(2,1)S(1)} %get-tuple-element.12), channel_id=1, source_target_pairs={{0,24},{1,25},{2,26},{3,27},{4,28},{5,29},{6,30},{7,31},{8,0},{9,1... | collective-permute-start | bytes 442376 | tf_op jit(solution)/shard_map/ppermute | solution.py:534
  47.0 17.4 %collective-permute-start.9 = (bf16[72,1024]{1,0:T(8,128)(2,1)S(1)}, bf16[72,1024]{1,0:T(8,128)(2,1)S(1)}, u32[]{:S(2)}, u32[]{:S(2)}) collective-permute-start(bf16[72,1024]{1,0:T(8,128)(2,1)S(1)} %get-tuple-element.12), channel_id=1, source_target_pairs={{0,31},{1,26},{2,25},{3,28},{4,27},{5,30},{6,29},{7,24},{8,7},{9,2... | collective-permute-start | bytes 442376 | tf_op jit(solution)/shard_map/ppermute | solution.py:534
  69.7 1.6 %collective-permute-start.12 = (bf16[108,1024]{1,0:T(8,128)(2,1)S(1)}, bf16[108,1024]{1,0:T(8,128)(2,1)S(1)}, u32[]{:S(2)}, u32[]{:S(2)}) collective-permute-start(bf16[108,1024]{1,0:T(8,128)(2,1)S(1)} %get-tuple-element.16), channel_id=1, source_target_pairs={{0,1},{1,0},{2,3},{3,2},{4,5},{5,4},{6,7},{7,6},{8,9},{9,8},{10,11... | collective-permute-start | bytes 663560 | tf_op jit(solution)/shard_map/ppermute | solution.py:523
  69.8 6.3 %collective-permute-start.10 = (bf16[36,1024]{1,0:T(8,128)(2,1)S(1)}, bf16[36,1024]{1,0:T(8,128)(2,1)S(1)}, u32[]{:S(2)}, u32[]{:S(2)}) collective-permute-start(bf16[36,1024]{1,0:T(8,128)(2,1)S(1)} %get-tuple-element.13), channel_id=1, source_target_pairs={{0,8},{1,9},{2,10},{3,11},{4,12},{5,13},{6,14},{7,15},{8,16},{9,17... | collective-permute-start | bytes 221192 | tf_op jit(solution)/shard_map/ppermute | solution.py:534
  70.4 6.3 %collective-permute-start.11 = (bf16[36,1024]{1,0:T(8,128)(2,1)S(1)}, bf16[36,1024]{1,0:T(8,128)(2,1)S(1)}, u32[]{:S(2)}, u32[]{:S(2)}) collective-permute-start(bf16[36,1024]{1,0:T(8,128)(2,1)S(1)} %get-tuple-element.14), channel_id=1, source_target_pairs={{0,9},{1,8},{2,11},{3,10},{4,13},{5,12},{6,15},{7,14},{8,17},{9,16... | collective-permute-start | bytes 221192 | tf_op jit(solution)/shard_map/ppermute | solution.py:534
  (5 other events, 33.2 us)

commit v4 on v3

--- a/solution.py
+++ b/solution.py
@@ -352,6 +352,40 @@
     return layer_norm(total, gain_ref[...], offset_ref[...]).astype(jnp.bfloat16)
 
 
+def split_kernel(flags, grid_hbm, near_ref, far_ref, up_ref, down_ref, grid_ref, sem):
+    fetch = pltpu.make_async_copy(grid_hbm, grid_ref, sem)
+    fetch.start()
+    levels, _, row_count, channels = grid_ref.shape
+    lines = levels * HALF_LON
+    chunks, tokens, _ = near_ref.shape
+    place = lax.broadcasted_iota(jnp.int32, (row_count * lines, 1), 0)
+    turn = one_hot(place % lines * row_count + place // lines, lines * row_count)
+    fetch.wait()
+    for side, dst in ((0, near_ref), (1, far_ref)):
+        right = flags[2] if side == 0 else 1 - flags[2]
+        half = grid_ref[:, pl.ds(right * HALF_LON, HALF_LON)].reshape(lines * row_count, channels)
+        rows = mm(turn, half)
+        for e in range(chunks):
+            chunk = rows[e * tokens : (e + 1) * tokens].astype(jnp.bfloat16)
+            dst[e] = chunk
+            if e == 0:
+                up_ref[side] = chunk
+            if e == chunks - 1:
+                down_ref[side] = chunk
+
+
+def load_kernel(*refs):
+    count = len(refs) // 2
+    copies = [
+        pltpu.make_async_copy(src, dst, refs[-1].at[i])
+        for i, (src, dst) in enumerate(zip(refs[:count], refs[count:-1]))
+    ]
+    for copy in copies:
+        copy.start()
+    for copy in copies:
+        copy.wait()
+
+
 def side_kernel(
     scale_ref,
     flags,
@@ -359,7 +393,8 @@
     other_ref,
     top_ref,
     bottom_ref,
-    other_rim_ref,
+    other_top_ref,
+    other_bottom_ref,
     packed_ref,
     output_ref,
     gain_ref,
@@ -376,8 +411,8 @@
     else:
         side, (near_ref, merged_ref, up_ref, *rest) = 1, rest
     merge_ref, sem, first, own, both, query, key, value, prob, ctx = rest
-    fetch = pltpu.make_async_copy(merge_hbm, merge_ref, sem)
-    fetch.start()
+    merge_copy = pltpu.make_async_copy(merge_hbm, merge_ref, sem)
+    merge_copy.start()
     chunks = own_ref.shape[0]
     tokens = own_ref.shape[1]
     span = open_ref.shape[0] * GROUP
@@ -385,7 +420,7 @@
     lines = []
     for src, top, bottom in (
         (own_ref, top_ref[side], bottom_ref[side]),
-        (other_ref, other_rim_ref[0], other_rim_ref[1]),
+        (other_ref, other_top_ref[0], other_bottom_ref[side]),
     ):
         lines.append([top] + [src[e] for e in range(chunks)] + [bottom])
     for w in range(chunks // 2 + 1):
@@ -397,7 +432,7 @@
     wraps = [flags[0]] + [None] * (chunks // 2 - 1) + [flags[1]]
     attend(wraps, query, key, value, open_ref, prob, ctx)
     first[...] = block_rows(own, ctx, output_ref, gain_ref, offset_ref)
-    fetch.wait()
+    merge_copy.wait()
     cells = 4 * merged_ref.shape[0]
     patch = one_hot(column_of(table_ref, PATCH, slice(0, cells)), first.shape[0])
     merged = merge_rows(first, patch, merge_ref, merge_gain_ref, merge_offset_ref)
@@ -496,11 +531,16 @@
     place(zip(index, (back_ref, back_near_ref)), out_ref, rows_ref, sem, 0)
 
 
+def in_hbm(value):
+    return pltpu.with_memory_space_constraint(value, pltpu.HBM)
+
+
 def call(
     kernel, outs, scratch, scalars, operands, fixed=(), late=(), alias=None, held=False, room=SECOND_BYTES
 ):
     vmem = pl.BlockSpec(memory_space=pltpu.VMEM)
     hbm = pl.BlockSpec(memory_space=pltpu.HBM)
+    fixed = [in_hbm(x) for x in fixed]
     return pl.pallas_call(
         kernel,
         out_shape=outs,
@@ -555,14 +595,13 @@
     gain_second,
     offset_second,
 ):
-    levels, row_count, _, channels = features.shape
+    levels, row_count, col_count, channels = features.shape
     inner = packed_first.shape[1] // 3
     second_inner = packed_second.shape[1] // 3
     wide = merge_weight.shape[1]
     half_rows = row_count // 2
     lat_pos = lax.axis_index("lat")
     odd = lax.axis_index("lon") % 2
-    is_even = odd == 0
     last = lax.axis_size("lat") - 1
     place = jnp.stack([lat_pos, lat_pos, 1 - odd])
     flags = (place == jnp.asarray([0, last, 1], jnp.int32)).astype(jnp.int32)
@@ -572,17 +611,22 @@
     chunks = row_count // HALF_LAT
     windows = chunks // 2 + 1
 
-    turned = jnp.transpose(features, (1, 0, 2, 3))
-    left, right = turned[:, :, :HALF_LON], turned[:, :, HALF_LON:]
-    near = jnp.where(is_even, right, left).reshape(chunks, tokens, channels)
-    far = jnp.where(is_even, left, right).reshape(chunks, tokens, channels)
-
+    half = jax.ShapeDtypeStruct((chunks, tokens, channels), bf16)
+    ends = jax.ShapeDtypeStruct((2, tokens, channels), bf16)
+    near, far, ups, downs = call(
+        split_kernel,
+        [half, half, ends, ends],
+        [pltpu.VMEM((levels, col_count, row_count, channels), bf16), pltpu.SemaphoreType.DMA],
+        [flags],
+        [],
+        [jnp.transpose(features, (0, 2, 1, 3))],
+    )
+    bottom = shift(ups, -1)
+    top = shift(downs, 1)
     near_other = near_swap(near)
-    bottom = shift(jnp.stack([near[0], far[0]]), -1)
-    top = shift(jnp.stack([near[-1], far[-1]]), 1)
     far_other = far_swap(far)
-    near_other_rim = near_swap(jnp.stack([top[0], bottom[0]]))
-    far_other_rim = far_swap(jnp.stack([top[1], bottom[1]]))
+    near_other_top, near_other_bottom = near_swap(top), near_swap(bottom)
+    far_rim = far_swap(jnp.stack([top[1], bottom[1]]))
 
     opened = jnp.asarray(open_tables(levels), bf16)
     cells = half_rows * levels * HALF_LON // 2
@@ -591,8 +635,17 @@
 
     shared = [packed_first, output_first, gain_first[None], offset_first[None]]
     shared += [merge_gain[None], merge_offset[None], opened]
-    table = jnp.asarray(index_table(levels, row_count))
-    shared += [table]
+    shared += [jnp.asarray(index_table(levels, row_count))]
+    shared = call(
+        load_kernel,
+        [jax.ShapeDtypeStruct(x.shape, x.dtype) for x in shared],
+        [pltpu.SemaphoreType.DMA((len(shared),))],
+        [],
+        [],
+        shared,
+    )
+    shared = list(shared)
+    opened, table = shared[-2:]
     buffers = [pltpu.VMEM(merge_weight.shape, bf16), pltpu.SemaphoreType.DMA]
     buffers += [pltpu.VMEM((windows * span, channels), bf16)]
     buffers += attention_scratch(windows * span, inner, channels)
@@ -600,8 +653,8 @@
         side_kernel,
         [small],
         buffers,
-        [scale_first, flags],
-        [near, near_other, top, bottom, near_other_rim] + shared,
+        [in_hbm(scale_first), flags],
+        [near, near_other, top, bottom, near_other_top, near_other_bottom] + shared,
         [merge_weight],
         room=FIRST_BYTES,
     )
@@ -610,8 +663,8 @@
         side_kernel,
         [small, edge],
         buffers,
-        [scale_first, flags],
-        [far, far_other, top, bottom, far_other_rim] + shared,
+        [in_hbm(scale_first), flags],
+        [far, far_other, top, bottom, far_rim, far_rim] + shared,
         [merge_weight],
         [merged_near],
         room=FIRST_BYTES,
@@ -633,7 +686,7 @@
             back,
         ],
         attention_scratch(windows * span, second_inner, wide),
-        [scale_second, flags],
+        [in_hbm(scale_second), flags],
         [
             merged_near,
             merged_far,

time: 78.8 us -> 74.5 us (0.945)
  local copies, waits for them, and re-layouts: 5.4 us -> 0.04 us
  Pallas kernels: 26.4 us -> 30.4 us
  other arithmetic: 2.8 us -> 0.75 us
  waiting for transfers between devices: 23.8 us -> 22.3 us
  starting transfers between devices: 19.5 us -> 20.3 us
    ppermute x2, waiting for transfers between devices: 0.01 us -> 5.72 us  [shift(): lax.ppermute(value, 'lat', [(i, i + by) for i in range(n) if 0 <= i + by...]
    pallas_call x5 -> x7, Pallas kernels: 26.4 us -> 30.4 us  [call(): pl.pallas_call(kernel, out_shape=outs, in_specs=[pl.BlockSpec(memory_spac...]
    ppermute x4, waiting for transfers between devices: 3.94 us -> 0.01 us  [far_swap(): return lax.ppermute(value, 'lon', [(i, far_of(i, n)) for i in range(n)])]
    ppermute x2, starting transfers between devices: 7.44 us -> 4.69 us  [shift(): lax.ppermute(value, 'lat', [(i, i + by) for i in range(n) if 0 <= i + by...]
    ppermute x4, starting transfers between devices: 7.99 us -> 10.2 us  [far_swap(): return lax.ppermute(value, 'lon', [(i, far_of(i, n)) for i in range(n)])]
    ppermute x4, waiting for transfers between devices: 17.8 us -> 15.8 us  [ring(): return lax.ppermute(value, ('lat', 'lon'), links)]
    reshape x2 -> x0, local copies, waits for them, and re-layouts: 1.67 us -> none  [the longest x1 1.47 us: body(): far = jnp.where(is_even, left, right).reshape(chunks, tokens, channels)]
    another operation x4 -> x1, other arithmetic: 1.4 us -> 0.02 us  [body(): far_rim = far_swap(jnp.stack([top[1], bottom[1]]))]
  transfers between devices with their start and end apart: 13 -> 14, of which waited for: 7 -> 6; matrix products, arithmetic and copies ran while one was open for 6% -> 0% of each run, Pallas kernels for 14% -> 16%
where the time goes in v4:
time: 74.5 us; the launch traced here: 74.3 us
  Pallas kernels  30.4 us (41%)
  waiting for transfers between devices  22.3 us (30%)
  starting transfers between devices  20.3 us (27%)
  other arithmetic  0.75 us (1%)
    pallas_call x7, Pallas kernels, call(): pl.pallas_call(kernel, out_shape=outs, in_specs=[pl.BlockSpec(memory_spac...  30.4 us
    ppermute x4, waiting for transfers between devices, ring(): return lax.ppermute(value, ('lat', 'lon'), links)  15.8 us
    ppermute x4, starting transfers between devices, far_swap(): return lax.ppermute(value, 'lon', [(i, far_of(i, n)) for i in range(n)])  10.2 us
    ppermute x2, waiting for transfers between devices, shift(): lax.ppermute(value, 'lat', [(i, i + by) for i in range(n) if 0 <= i + by...  5.72 us
    ppermute x4, starting transfers between devices, ring(): return lax.ppermute(value, ('lat', 'lon'), links)  4.84 us
    ppermute x2, starting transfers between devices, shift(): lax.ppermute(value, 'lat', [(i, i + by) for i in range(n) if 0 <= i + by...  4.69 us
  transfers between devices with their start and end apart: 14, of which 6 were waited for; matrix products, arithmetic and copies ran while one was open for 0% of the time, Pallas kernels for 16%

profile of v4, /device:TPU:0, one launch (start us, length us, event | category | flops | bytes accessed | tf_op | source)
XLA Modules:
  0.0 74.3 jit_solution(694277397954904842)
XLA Ops:
  0.0 0.7 compare_convert_fusion.flags
  0.7 2.9 %shard_map.163 = (bf16[8,72,512]{2,1,0:T(8,128)(2,1)S(1)}, bf16[8,72,512]{2,1,0:T(8,128)(2,1)S(1)}, bf16[2,72,512]{2,1,0:T(8,128)(2,1)S(1)}, bf16[2,72,512]{2,1,0:T(8,128)(2,1)S(1)}) custom-call(s32[3]{0:T(128)S(1)} %compare_convert_fusion.flags, bf16[4,12,24,512]{3,2,1,0:T(8,128)(2,1)} %bitcast.12), custom_call_target="tpu_custom_call" | custom-call | tf_op jit(solution)/shard_map/pallas_call | solution.py:544
  3.6 0.6 collective-permute-start
  4.2 4.7 %collective-permute-start.5 = (bf16[8,72,512]{2,1,0:T(8,128)(2,1)S(1)}, bf16[8,72,512]{2,1,0:T(8,128)(2,1)S(1)}, u32[]{:S(2)}, u32[]{:S(2)}) collective-permute-start(bf16[8,72,512]{2,1,0:T(8,128)(2,1)S(1)} %get-tuple-element.34.own_ref), channel_id=1, source_target_pairs={{0,7},{1,2},{2,1},{3,4},{4,3},{5,6},{6,5},{7,0},{8,15},{9,10},{10,... | collective-permute-start | bytes 1769480 | tf_op jit(solution)/shard_map/ppermute | solution.py:568
  8.9 3.4 %collective-permute-start.1 = (bf16[2,72,512]{2,1,0:T(8,128)(2,1)S(1)}, bf16[2,72,512]{2,1,0:T(8,128)(2,1)S(1)}, u32[]{:S(2)}, u32[]{:S(2)}) collective-permute-start(bf16[2,72,512]{2,1,0:T(8,128)(2,1)S(1)} %get-tuple-element.24), channel_id=1, source_target_pairs={{0,8},{8,16},{16,24},{1,9},{9,17},{17,25},{2,10},{10,18},{18,26},{... | collective-permute-start | bytes 442376 | tf_op jit(solution)/shard_map/ppermute | solution.py:579
  12.3 1.3 %collective-permute-start.2 = (bf16[2,72,512]{2,1,0:T(8,128)(2,1)S(1)}, bf16[2,72,512]{2,1,0:T(8,128)(2,1)S(1)}, u32[]{:S(2)}, u32[]{:S(2)}) collective-permute-start(bf16[2,72,512]{2,1,0:T(8,128)(2,1)S(1)} %get-tuple-element.25), channel_id=1, source_target_pairs={{8,0},{16,8},{24,16},{9,1},{17,9},{25,17},{10,2},{18,10},{26,18},{... | collective-permute-start | bytes 442376 | tf_op jit(solution)/shard_map/ppermute | solution.py:579
  13.6 1.3 %collective-permute-done.1.top_ref = bf16[2,72,512]{2,1,0:T(8,128)(2,1)S(1)} collective-permute-done((bf16[2,72,512]{2,1,0:T(8,128)(2,1)S(1)}, bf16[2,72,512]{2,1,0:T(8,128)(2,1)S(1)}, u32[]{:S(2)}, u32[]{:S(2)}) %collective-permute-start.1) | collective-permute-done | bytes 147488 | tf_op jit(solution)/shard_map/ppermute | solution.py:579
  15.0 4.4 %collective-permute-done.2.bottom_ref = bf16[2,72,512]{2,1,0:T(8,128)(2,1)S(1)} collective-permute-done((bf16[2,72,512]{2,1,0:T(8,128)(2,1)S(1)}, bf16[2,72,512]{2,1,0:T(8,128)(2,1)S(1)}, u32[]{:S(2)}, u32[]{:S(2)}) %collective-permute-start.2) | collective-permute-done | bytes 147488 | tf_op jit(solution)/shard_map/ppermute | solution.py:579
  19.4 1.9 %collective-permute-start.6 = (bf16[2,72,512]{2,1,0:T(8,128)(2,1)S(1)}, bf16[2,72,512]{2,1,0:T(8,128)(2,1)S(1)}, u32[]{:S(2)}, u32[]{:S(2)}) collective-permute-start(bf16[2,72,512]{2,1,0:T(8,128)(2,1)S(1)} %pad_maximum_fusion), channel_id=1, source_target_pairs={{0,7},{1,2},{2,1},{3,4},{4,3},{5,6},{6,5},{7,0},{8,15},{9,10},{10,... | collective-permute-start | bytes 442376 | tf_op jit(solution)/shard_map/ppermute | solution.py:568
  21.3 1.8 %shard_map.164 = (bf16[512,1536]{1,0:T(8,128)(2,1)S(1)}, bf16[512,512]{1,0:T(8,128)(2,1)S(1)}, f32[1,512]{1,0:T(1,128)S(1)}, f32[1,512]{1,0:T(1,128)S(1)}, f32[1...) custom-call(bf16[512,1536]{1,0:T(8,128)(2,1)} %refs_0_.1, ...), custom_call_target="tpu_custom_call" | custom-call | tf_op jit(solution)/shard_map/pallas_call | solution.py:544
  23.1 8.2 %shard_map.165.rest_0_.near_ref = bf16[144,1024]{1,0:T(8,128)(2,1)S(1)} custom-call(f32[8]{0:T(128)} %scale_ref.4, s32[3]{0:T(128)S(1)} %compare_convert_fusion.flags, bf16[8,72,512]{2,1,0:T(8,128)(2,1)S(1)} %get-tuple-element.23.own_ref, bf16[8,72,512]{2,1,0:T(8,128)(2,1)S(1)} %collective-permute-done.other_ref, ...), custom_call_target="tpu_custom_call" | custom-call | tf_op jit(solution)/shard_map/pallas_call | solution.py:544
  31.4 8.7 %shard_map.166 = (bf16[144,1024]{1,0:T(8,128)(2,1)S(1)}, bf16[72,1024]{1,0:T(8,128)(2,1)S(1)}) custom-call(f32[8]{0:T(128)} %scale_ref.4, s32[3]{0:T(128)S(1)} %compare_convert_fusion.flags, bf16[8,72,512]{2,1,0:T(8,128)(2,1)S(1)} %get-tuple-element.34.own_ref, bf16[8,72,512]{2,1,0:T(8,128)(2,1)S(1)} %collective-permute-done.5.other_ref, ...), custom_call_target="tpu_custom_call" | custom-call | tf_op jit(solution)/shard_map/pallas_call | solution.py:544
  40.0 1.8 %collective-permute-start.9 = (bf16[144,1024]{1,0:T(8,128)(2,1)S(1)}, bf16[144,1024]{1,0:T(8,128)(2,1)S(1)}, u32[]{:S(2)}, u32[]{:S(2)}) collective-permute-start(bf16[144,1024]{1,0:T(8,128)(2,1)S(1)} %get-tuple-element.35.far_ref), channel_id=1, source_target_pairs={{0,7},{1,2},{2,1},{3,4},{4,3},{5,6},{6,5},{7,0},{8,15},{9,10},{10,... | collective-permute-start | bytes 884744 | tf_op jit(solution)/shard_map/ppermute | solution.py:568
  41.8 1.8 %collective-permute-start.8 = (bf16[144,1024]{1,0:T(8,128)(2,1)S(1)}, bf16[144,1024]{1,0:T(8,128)(2,1)S(1)}, u32[]{:S(2)}, u32[]{:S(2)}) collective-permute-start(bf16[144,1024]{1,0:T(8,128)(2,1)S(1)} %shard_map.165.rest_0_.near_ref), channel_id=1, source_target_pairs={{0,7},{1,2},{2,1},{3,4},{4,3},{5,6},{6,5},{7,0},{8,15},{9,10},{10,... | collective-permute-start | bytes 884744 | tf_op jit(solution)/shard_map/ppermute | solution.py:568
  43.7 2.2 %collective-permute-start.10 = (bf16[72,1024]{1,0:T(8,128)(2,1)S(1)}, bf16[72,1024]{1,0:T(8,128)(2,1)S(1)}, u32[]{:S(2)}, u32[]{:S(2)}) collective-permute-start(bf16[72,1024]{1,0:T(8,128)(2,1)S(1)} %get-tuple-element.36), channel_id=1, source_target_pairs={{0,31},{1,26},{2,25},{3,28},{4,27},{5,30},{6,29},{7,24},{8,7},{9,2... | collective-permute-start | bytes 442376 | tf_op jit(solution)/shard_map/ppermute | solution.py:574
  45.9 1.9 %collective-permute-start.7 = (bf16[72,1024]{1,0:T(8,128)(2,1)S(1)}, bf16[72,1024]{1,0:T(8,128)(2,1)S(1)}, u32[]{:S(2)}, u32[]{:S(2)}) collective-permute-start(bf16[72,1024]{1,0:T(8,128)(2,1)S(1)} %get-tuple-element.36), channel_id=1, source_target_pairs={{0,24},{1,25},{2,26},{3,27},{4,28},{5,29},{6,30},{7,31},{8,0},{9,1... | collective-permute-start | bytes 442376 | tf_op jit(solution)/shard_map/ppermute | solution.py:574
  47.8 12.3 %collective-permute-done.10.other_rim_ref = bf16[72,1024]{1,0:T(8,128)(2,1)S(1)} collective-permute-done((bf16[72,1024]{1,0:T(8,128)(2,1)S(1)}, bf16[72,1024]{1,0:T(8,128)(2,1)S(1)}, u32[]{:S(2)}, u32[]{:S(2)}) %collective-permute-start.10) | collective-permute-done | bytes 147488 | tf_op jit(solution)/shard_map/ppermute | solution.py:574
  60.2 5.3 %shard_map.167 = (bf16[288,1024]{1,0:T(8,128)(2,1)S(1)}, bf16[108,1024]{1,0:T(8,128)(2,1)S(1)}, bf16[36,1024]{1,0:T(8,128)(2,1)S(1)}, bf16[36,1024]{1,0:T(8,128)(2,1)S(1)}) custom-call(f32[8]{0:T(128)} %scale_ref.5, s32[3]{0:T(128)S(1)} %compare_convert_fusion.flags, bf16[144,1024]{1,0:T(8,128)(2,1)S(1)} %shard_map.165.rest_0_.near_ref, ...), custom_call_target="tpu_custom_call" | custom-call | tf_op jit(solution)/shard_map/pallas_call | solution.py:544
  65.6 0.6 collective-permute-start.11
  66.3 0.8 %collective-permute-done.13.near_ref = bf16[108,1024]{1,0:T(8,128)(2,1)S(1)} collective-permute-done((bf16[108,1024]{1,0:T(8,128)(2,1)S(1)}, bf16[108,1024]{1,0:T(8,128)(2,1)S(1)}, u32[]{:S(2)}, u32[]{:S(2)}) %collective-permute-start.13) | collective-permute-done | bytes 221216 | tf_op jit(solution)/shard_map/ppermute | solution.py:563
  67.0 2.0 %shard_map.168._ = bf16[12,1,12,2,1024]{4,3,2,1,0:T(2,128)(2,1)} custom-call(s32[3]{0:T(128)S(1)} %compare_convert_fusion.flags, bf16[288,1024]{1,0:T(8,128)(2,1)S(1)} %get-tuple-element.39.second_ref, bf16[108,1024]{1,0:T(8,128)(2,1)S(1)} %collective-permute-done.13.near_ref, s32[576,18]{1,0:T(8,128)S(1)} %get-tuple-element.33.table_ref), custom_call_target="tpu_custom_call" | custom-call | tf_op jit(solution)/shard_map/pallas_call | solution.py:544
  69.1 2.8 %collective-permute-done.11.back_ref = bf16[36,1024]{1,0:T(8,128)(2,1)S(1)} collective-permute-done((bf16[36,1024]{1,0:T(8,128)(2,1)S(1)}, bf16[36,1024]{1,0:T(8,128)(2,1)S(1)}, u32[]{:S(2)}, u32[]{:S(2)}) %collective-permute-start.11) | collective-permute-done | bytes 73760 | tf_op jit(solution)/shard_map/ppermute | solution.py:574
  71.8 0.7 collective-permute-done.12.back_near_ref
  72.5 1.6 %shard_map.169 = bf16[12,1,12,2,1024]{4,3,2,1,0:T(2,128)(2,1)} custom-call(s32[3]{0:T(128)S(1)} %compare_convert_fusion.flags, bf16[36,1024]{1,0:T(8,128)(2,1)S(1)} %collective-permute-done.11.back_ref, bf16[36,1024]{1,0:T(8,128)(2,1)S(1)} %collective-permute-done.12.back_near_ref, ...), custom_call_target="tpu_custom_call", output_to_operand_aliasing={{}: (4, {})} | custom-call | tf_op jit(solution)/shard_map/pallas_call | solution.py:544
  (23 shorter events, 0.2 us)
Async XLA Ops:
  3.6 19.5 %collective-permute-start = (bf16[8,72,512]{2,1,0:T(8,128)(2,1)S(1)}, bf16[8,72,512]{2,1,0:T(8,128)(2,1)S(1)}, u32[]{:S(2)}, u32[]{:S(2)}) collective-permute-start(bf16[8,72,512]{2,1,0:T(8,128)(2,1)S(1)} %get-tuple-element.23.own_ref), channel_id=1, source_target_pairs={{0,1},{1,0},{2,3},{3,2},{4,5},{5,4},{6,7},{7,6},{8,9},{9,8},{10,11... | collective-permute-start | bytes 1769480 | tf_op jit(solution)/shard_map/ppermute | solution.py:563
  4.2 27.2 %collective-permute-start.5 = (bf16[8,72,512]{2,1,0:T(8,128)(2,1)S(1)}, bf16[8,72,512]{2,1,0:T(8,128)(2,1)S(1)}, u32[]{:S(2)}, u32[]{:S(2)}) collective-permute-start(bf16[8,72,512]{2,1,0:T(8,128)(2,1)S(1)} %get-tuple-element.34.own_ref), channel_id=1, source_target_pairs={{0,7},{1,2},{2,1},{3,4},{4,3},{5,6},{6,5},{7,0},{8,15},{9,10},{10,... | collective-permute-start | bytes 1769480 | tf_op jit(solution)/shard_map/ppermute | solution.py:568
  8.9 6.1 %collective-permute-start.1 = (bf16[2,72,512]{2,1,0:T(8,128)(2,1)S(1)}, bf16[2,72,512]{2,1,0:T(8,128)(2,1)S(1)}, u32[]{:S(2)}, u32[]{:S(2)}) collective-permute-start(bf16[2,72,512]{2,1,0:T(8,128)(2,1)S(1)} %get-tuple-element.24), channel_id=1, source_target_pairs={{0,8},{8,16},{16,24},{1,9},{9,17},{17,25},{2,10},{10,18},{18,26},{... | collective-permute-start | bytes 442376 | tf_op jit(solution)/shard_map/ppermute | solution.py:579
  12.3 7.0 %collective-permute-start.2 = (bf16[2,72,512]{2,1,0:T(8,128)(2,1)S(1)}, bf16[2,72,512]{2,1,0:T(8,128)(2,1)S(1)}, u32[]{:S(2)}, u32[]{:S(2)}) collective-permute-start(bf16[2,72,512]{2,1,0:T(8,128)(2,1)S(1)} %get-tuple-element.25), channel_id=1, source_target_pairs={{8,0},{16,8},{24,16},{9,1},{17,9},{25,17},{10,2},{18,10},{26,18},{... | collective-permute-start | bytes 442376 | tf_op jit(solution)/shard_map/ppermute | solution.py:579
  15.0 8.1 %collective-permute-start.3 = (bf16[2,72,512]{2,1,0:T(8,128)(2,1)S(1)}, bf16[2,72,512]{2,1,0:T(8,128)(2,1)S(1)}, u32[]{:S(2)}, u32[]{:S(2)}) collective-permute-start(bf16[2,72,512]{2,1,0:T(8,128)(2,1)S(1)} %collective-permute-done.1.top_ref), channel_id=1, source_target_pairs={{0,1},{1,0},{2,3},{3,2},{4,5},{5,4},{6,7},{7,6},{8,9},{9,8},{10,11... | collective-permute-start | bytes 442376 | tf_op jit(solution)/shard_map/ppermute | solution.py:563
  19.3 3.7 %collective-permute-start.4 = (bf16[2,72,512]{2,1,0:T(8,128)(2,1)S(1)}, bf16[2,72,512]{2,1,0:T(8,128)(2,1)S(1)}, u32[]{:S(2)}, u32[]{:S(2)}) collective-permute-start(bf16[2,72,512]{2,1,0:T(8,128)(2,1)S(1)} %collective-permute-done.2.bottom_ref), channel_id=1, source_target_pairs={{0,1},{1,0},{2,3},{3,2},{4,5},{5,4},{6,7},{7,6},{8,9},{9,8},{10,11... | collective-permute-start | bytes 442376 | tf_op jit(solution)/shard_map/ppermute | solution.py:563
  19.4 12.0 %collective-permute-start.6 = (bf16[2,72,512]{2,1,0:T(8,128)(2,1)S(1)}, bf16[2,72,512]{2,1,0:T(8,128)(2,1)S(1)}, u32[]{:S(2)}, u32[]{:S(2)}) collective-permute-start(bf16[2,72,512]{2,1,0:T(8,128)(2,1)S(1)} %pad_maximum_fusion), channel_id=1, source_target_pairs={{0,7},{1,2},{2,1},{3,4},{4,3},{5,6},{6,5},{7,0},{8,15},{9,10},{10,... | collective-permute-start | bytes 442376 | tf_op jit(solution)/shard_map/ppermute | solution.py:568
  31.3 28.8 %copy-start.1 = (bf16[512,1024]{1,0:T(8,128)(2,1)S(1)}, bf16[512,1024]{1,0:T(8,128)(2,1)}, u32[]{:S(2)}) copy-start(bf16[512,1024]{1,0:T(8,128)(2,1)} %output_ref.1) | copy-start | bytes 3145732
  31.3 28.8 %copy-start.2 = (f32[1024]{0:T(1024)S(1)}, f32[1024]{0:T(1024)}, u32[]{:S(2)}) copy-start(f32[1024]{0:T(1024)} %param.29) | copy-start | bytes 12292
  31.3 28.8 %copy-start.3 = (f32[1024]{0:T(1024)S(1)}, f32[1024]{0:T(1024)}, u32[]{:S(2)}) copy-start(f32[1024]{0:T(1024)} %param.30) | copy-start | bytes 12292
  31.4 28.8 %copy-start = (bf16[1024,1536]{1,0:T(8,128)(2,1)S(1)}, bf16[1024,1536]{1,0:T(8,128)(2,1)}, u32[]{:S(2)}) copy-start(bf16[1024,1536]{1,0:T(8,128)(2,1)} %packed_ref.1) | copy-start | bytes 9437188
  40.0 20.1 %collective-permute-start.9 = (bf16[144,1024]{1,0:T(8,128)(2,1)S(1)}, bf16[144,1024]{1,0:T(8,128)(2,1)S(1)}, u32[]{:S(2)}, u32[]{:S(2)}) collective-permute-start(bf16[144,1024]{1,0:T(8,128)(2,1)S(1)} %get-tuple-element.35.far_ref), channel_id=1, source_target_pairs={{0,7},{1,2},{2,1},{3,4},{4,3},{5,6},{6,5},{7,0},{8,15},{9,10},{10,... | collective-permute-start | bytes 884744 | tf_op jit(solution)/shard_map/ppermute | solution.py:568
  41.8 18.3 %collective-permute-start.8 = (bf16[144,1024]{1,0:T(8,128)(2,1)S(1)}, bf16[144,1024]{1,0:T(8,128)(2,1)S(1)}, u32[]{:S(2)}, u32[]{:S(2)}) collective-permute-start(bf16[144,1024]{1,0:T(8,128)(2,1)S(1)} %shard_map.165.rest_0_.near_ref), channel_id=1, source_target_pairs={{0,7},{1,2},{2,1},{3,4},{4,3},{5,6},{6,5},{7,0},{8,15},{9,10},{10,... | collective-permute-start | bytes 884744 | tf_op jit(solution)/shard_map/ppermute | solution.py:568
  43.7 16.5 %collective-permute-start.10 = (bf16[72,1024]{1,0:T(8,128)(2,1)S(1)}, bf16[72,1024]{1,0:T(8,128)(2,1)S(1)}, u32[]{:S(2)}, u32[]{:S(2)}) collective-permute-start(bf16[72,1024]{1,0:T(8,128)(2,1)S(1)} %get-tuple-element.36), channel_id=1, source_target_pairs={{0,31},{1,26},{2,25},{3,28},{4,27},{5,30},{6,29},{7,24},{8,7},{9,2... | collective-permute-start | bytes 442376 | tf_op jit(solution)/shard_map/ppermute | solution.py:574
  45.9 14.3 %collective-permute-start.7 = (bf16[72,1024]{1,0:T(8,128)(2,1)S(1)}, bf16[72,1024]{1,0:T(8,128)(2,1)S(1)}, u32[]{:S(2)}, u32[]{:S(2)}) collective-permute-start(bf16[72,1024]{1,0:T(8,128)(2,1)S(1)} %get-tuple-element.36), channel_id=1, source_target_pairs={{0,24},{1,25},{2,26},{3,27},{4,28},{5,29},{6,30},{7,31},{8,0},{9,1... | collective-permute-start | bytes 442376 | tf_op jit(solution)/shard_map/ppermute | solution.py:574
  65.5 1.6 %collective-permute-start.13 = (bf16[108,1024]{1,0:T(8,128)(2,1)S(1)}, bf16[108,1024]{1,0:T(8,128)(2,1)S(1)}, u32[]{:S(2)}, u32[]{:S(2)}) collective-permute-start(bf16[108,1024]{1,0:T(8,128)(2,1)S(1)} %get-tuple-element.40), channel_id=1, source_target_pairs={{0,1},{1,0},{2,3},{3,2},{4,5},{5,4},{6,7},{7,6},{8,9},{9,8},{10,11... | collective-permute-start | bytes 663560 | tf_op jit(solution)/shard_map/ppermute | solution.py:563
  65.6 6.3 %collective-permute-start.11 = (bf16[36,1024]{1,0:T(8,128)(2,1)S(1)}, bf16[36,1024]{1,0:T(8,128)(2,1)S(1)}, u32[]{:S(2)}, u32[]{:S(2)}) collective-permute-start(bf16[36,1024]{1,0:T(8,128)(2,1)S(1)} %get-tuple-element.37), channel_id=1, source_target_pairs={{0,8},{1,9},{2,10},{3,11},{4,12},{5,13},{6,14},{7,15},{8,16},{9,17... | collective-permute-start | bytes 221192 | tf_op jit(solution)/shard_map/ppermute | solution.py:574
  66.2 6.3 %collective-permute-start.12 = (bf16[36,1024]{1,0:T(8,128)(2,1)S(1)}, bf16[36,1024]{1,0:T(8,128)(2,1)S(1)}, u32[]{:S(2)}, u32[]{:S(2)}) collective-permute-start(bf16[36,1024]{1,0:T(8,128)(2,1)S(1)} %get-tuple-element.38), channel_id=1, source_target_pairs={{0,9},{1,8},{2,11},{3,10},{4,13},{5,12},{6,15},{7,14},{8,17},{9,16... | collective-permute-start | bytes 221192 | tf_op jit(solution)/shard_map/ppermute | solution.py:574

commit v5 on v4

--- a/solution.py
+++ b/solution.py
@@ -386,6 +386,52 @@
         copy.wait()
 
 
+def first_windows(
+    lines, wraps, table_ref, packed_ref, scale_ref, output_ref, gain_ref, offset_ref, open_ref, scratch
+):
+    own, both, query, key, value, prob, ctx = scratch
+    tokens = lines[0][0].shape[0]
+    span = open_ref.shape[0] * GROUP
+    pick = [one_hot(column_of(table_ref, PICK + s, slice(0, span)), tokens) for s in range(2)]
+    for w in range(len(wraps)):
+        mine, theirs = (
+            mm(pick[0], line[2 * w]) + mm(pick[1], line[2 * w + 1]) for line in lines
+        )
+        keep_window(w, mine, theirs, own, both)
+    project(own, both, packed_ref, scale_ref, query, key, value)
+    attend(wraps, query, key, value, open_ref, prob, ctx)
+    return block_rows(own, ctx, output_ref, gain_ref, offset_ref)
+
+
+def inner_kernel(
+    scale_ref,
+    own_ref,
+    other_ref,
+    packed_ref,
+    output_ref,
+    gain_ref,
+    offset_ref,
+    open_ref,
+    table_ref,
+    rows_ref,
+    *scratch,
+):
+    chunks = own_ref.shape[0]
+    lines = [[ref[e] for e in range(1, chunks - 1)] for ref in (own_ref, other_ref)]
+    rows_ref[...] = first_windows(
+        lines,
+        [None] * (chunks // 2 - 1),
+        table_ref,
+        packed_ref,
+        scale_ref,
+        output_ref,
+        gain_ref,
+        offset_ref,
+        open_ref,
+        scratch,
+    )
+
+
 def side_kernel(
     scale_ref,
     flags,
@@ -406,32 +452,41 @@
     merge_hbm,
     *rest,
 ):
-    if len(rest) == 11:
-        side, (merged_ref, *rest) = 0, rest
+    if len(rest) == 12:
+        side, (inner_ref, merged_ref, *rest) = 0, rest
     else:
         side, (near_ref, merged_ref, up_ref, *rest) = 1, rest
-    merge_ref, sem, first, own, both, query, key, value, prob, ctx = rest
+    merge_ref, sem, first, *scratch = rest
     merge_copy = pltpu.make_async_copy(merge_hbm, merge_ref, sem)
     merge_copy.start()
     chunks = own_ref.shape[0]
-    tokens = own_ref.shape[1]
     span = open_ref.shape[0] * GROUP
-    pick = [one_hot(column_of(table_ref, PICK + s, slice(0, span)), tokens) for s in range(2)]
+    inside = range(chunks) if side else (0, chunks - 1)
     lines = []
     for src, top, bottom in (
         (own_ref, top_ref[side], bottom_ref[side]),
         (other_ref, other_top_ref[0], other_bottom_ref[side]),
     ):
-        lines.append([top] + [src[e] for e in range(chunks)] + [bottom])
-    for w in range(chunks // 2 + 1):
-        mine, theirs = (
-            mm(pick[0], line[2 * w]) + mm(pick[1], line[2 * w + 1]) for line in lines
-        )
-        keep_window(w, mine, theirs, own, both)
-    project(own, both, packed_ref, scale_ref, query, key, value)
-    wraps = [flags[0]] + [None] * (chunks // 2 - 1) + [flags[1]]
-    attend(wraps, query, key, value, open_ref, prob, ctx)
-    first[...] = block_rows(own, ctx, output_ref, gain_ref, offset_ref)
+        lines.append([top] + [src[e] for e in inside] + [bottom])
+    wraps = [flags[0]] + [None] * (len(inside) // 2 - 1) + [flags[1]]
+    rows = first_windows(
+        lines,
+        wraps,
+        table_ref,
+        packed_ref,
+        scale_ref,
+        output_ref,
+        gain_ref,
+        offset_ref,
+        open_ref,
+        scratch,
+    )
+    if side:
+        first[...] = rows
+    else:
+        first[:span] = rows[:span]
+        first[span : first.shape[0] - span] = inner_ref[...]
+        first[first.shape[0] - span :] = rows[span:]
     merge_copy.wait()
     cells = 4 * merged_ref.shape[0]
     patch = one_hot(column_of(table_ref, PATCH, slice(0, cells)), first.shape[0])
@@ -648,21 +703,28 @@
     opened, table = shared[-2:]
     buffers = [pltpu.VMEM(merge_weight.shape, bf16), pltpu.SemaphoreType.DMA]
     buffers += [pltpu.VMEM((windows * span, channels), bf16)]
-    buffers += attention_scratch(windows * span, inner, channels)
+    (inner_rows,) = call(
+        inner_kernel,
+        [jax.ShapeDtypeStruct(((windows - 2) * span, channels), bf16)],
+        attention_scratch((windows - 2) * span, inner, channels),
+        [in_hbm(scale_first)],
+        [near, near_other] + shared[:4] + shared[-2:],
+    )
     (merged_near,) = call(
         side_kernel,
         [small],
-        buffers,
+        buffers + attention_scratch(2 * span, inner, channels),
         [in_hbm(scale_first), flags],
         [near, near_other, top, bottom, near_other_top, near_other_bottom] + shared,
         [merge_weight],
+        [inner_rows],
         room=FIRST_BYTES,
     )
     other_near = far_swap(merged_near)
     merged_far, edge_up = call(
         side_kernel,
         [small, edge],
-        buffers,
+        buffers + attention_scratch(windows * span, inner, channels),
         [in_hbm(scale_first), flags],
         [far, far_other, top, bottom, far_rim, far_rim] + shared,
         [merge_weight],

time: 74.5 us -> 75.8 us (1.017)
  Pallas kernels: 30.4 us -> 31.7 us
    pallas_call x7 -> x8, Pallas kernels: 30.4 us -> 31.7 us  [call(): pl.pallas_call(kernel, out_shape=outs, in_specs=[pl.BlockSpec(memory_spac...]
  transfers between devices with their start and end apart: 14 -> 14, of which waited for: 6 -> 6; matrix products, arithmetic and copies ran while one was open for 0% -> 0% of each run, Pallas kernels for 16% -> 17%
where the time goes in v5:
time: 75.8 us; the launch traced here: 75.5 us
  Pallas kernels  31.7 us (42%)
  waiting for transfers between devices  22.4 us (30%)
  starting transfers between devices  20.3 us (27%)
    pallas_call x8, Pallas kernels, call(): pl.pallas_call(kernel, out_shape=outs, in_specs=[pl.BlockSpec(memory_spac...  31.7 us
    ppermute x4, waiting for transfers between devices, ring(): return lax.ppermute(value, ('lat', 'lon'), links)  15.8 us
    ppermute x4, starting transfers between devices, far_swap(): return lax.ppermute(value, 'lon', [(i, far_of(i, n)) for i in range(n)])  10.2 us
    ppermute x2, waiting for transfers between devices, shift(): lax.ppermute(value, 'lat', [(i, i + by) for i in range(n) if 0 <= i + by...  5.72 us
    ppermute x4, starting transfers between devices, ring(): return lax.ppermute(value, ('lat', 'lon'), links)  4.82 us
    ppermute x2, starting transfers between devices, shift(): lax.ppermute(value, 'lat', [(i, i + by) for i in range(n) if 0 <= i + by...  4.69 us
  transfers between devices with their start and end apart: 14, of which 6 were waited for; matrix products, arithmetic and copies ran while one was open for 0% of the time, Pallas kernels for 17%

profile of v5, /device:TPU:0, one launch (start us, length us, event | category | flops | bytes accessed | tf_op | source)
XLA Modules:
  0.0 75.5 jit_solution(9238522173832930904)
XLA Ops:
  0.0 0.7 compare_convert_fusion.flags
  0.7 2.9 %shard_map.163 = (bf16[8,72,512]{2,1,0:T(8,128)(2,1)S(1)}, bf16[8,72,512]{2,1,0:T(8,128)(2,1)S(1)}, bf16[2,72,512]{2,1,0:T(8,128)(2,1)S(1)}, bf16[2,72,512]{2,1,0:T(8,128)(2,1)S(1)}) custom-call(s32[3]{0:T(128)S(1)} %compare_convert_fusion.flags, bf16[4,12,24,512]{3,2,1,0:T(8,128)(2,1)} %bitcast.12), custom_call_target="tpu_custom_call" | custom-call | tf_op jit(solution)/shard_map/pallas_call | solution.py:599
  4.2 4.7 %collective-permute-start.5 = (bf16[8,72,512]{2,1,0:T(8,128)(2,1)S(1)}, bf16[8,72,512]{2,1,0:T(8,128)(2,1)S(1)}, u32[]{:S(2)}, u32[]{:S(2)}) collective-permute-start(bf16[8,72,512]{2,1,0:T(8,128)(2,1)S(1)} %get-tuple-element.34.own_ref), channel_id=1, source_target_pairs={{0,7},{1,2},{2,1},{3,4},{4,3},{5,6},{6,5},{7,0},{8,15},{9,10},{10,... | collective-permute-start | bytes 1769480 | tf_op jit(solution)/shard_map/ppermute | solution.py:623
  8.9 3.4 %collective-permute-start.1 = (bf16[2,72,512]{2,1,0:T(8,128)(2,1)S(1)}, bf16[2,72,512]{2,1,0:T(8,128)(2,1)S(1)}, u32[]{:S(2)}, u32[]{:S(2)}) collective-permute-start(bf16[2,72,512]{2,1,0:T(8,128)(2,1)S(1)} %get-tuple-element.24), channel_id=1, source_target_pairs={{0,8},{8,16},{16,24},{1,9},{9,17},{17,25},{2,10},{10,18},{18,26},{... | collective-permute-start | bytes 442376 | tf_op jit(solution)/shard_map/ppermute | solution.py:634
  12.3 1.3 %collective-permute-start.2 = (bf16[2,72,512]{2,1,0:T(8,128)(2,1)S(1)}, bf16[2,72,512]{2,1,0:T(8,128)(2,1)S(1)}, u32[]{:S(2)}, u32[]{:S(2)}) collective-permute-start(bf16[2,72,512]{2,1,0:T(8,128)(2,1)S(1)} %get-tuple-element.25), channel_id=1, source_target_pairs={{8,0},{16,8},{24,16},{9,1},{17,9},{25,17},{10,2},{18,10},{26,18},{... | collective-permute-start | bytes 442376 | tf_op jit(solution)/shard_map/ppermute | solution.py:634
  13.6 1.3 %collective-permute-done.1.top_ref = bf16[2,72,512]{2,1,0:T(8,128)(2,1)S(1)} collective-permute-done((bf16[2,72,512]{2,1,0:T(8,128)(2,1)S(1)}, bf16[2,72,512]{2,1,0:T(8,128)(2,1)S(1)}, u32[]{:S(2)}, u32[]{:S(2)}) %collective-permute-start.1) | collective-permute-done | bytes 147488 | tf_op jit(solution)/shard_map/ppermute | solution.py:634
  15.0 4.4 %collective-permute-done.2.bottom_ref = bf16[2,72,512]{2,1,0:T(8,128)(2,1)S(1)} collective-permute-done((bf16[2,72,512]{2,1,0:T(8,128)(2,1)S(1)}, bf16[2,72,512]{2,1,0:T(8,128)(2,1)S(1)}, u32[]{:S(2)}, u32[]{:S(2)}) %collective-permute-start.2) | collective-permute-done | bytes 147488 | tf_op jit(solution)/shard_map/ppermute | solution.py:634
  19.4 1.9 %collective-permute-start.6 = (bf16[2,72,512]{2,1,0:T(8,128)(2,1)S(1)}, bf16[2,72,512]{2,1,0:T(8,128)(2,1)S(1)}, u32[]{:S(2)}, u32[]{:S(2)}) collective-permute-start(bf16[2,72,512]{2,1,0:T(8,128)(2,1)S(1)} %pad_maximum_fusion), channel_id=1, source_target_pairs={{0,7},{1,2},{2,1},{3,4},{4,3},{5,6},{6,5},{7,0},{8,15},{9,10},{10,... | collective-permute-start | bytes 442376 | tf_op jit(solution)/shard_map/ppermute | solution.py:623
  21.3 1.8 %shard_map.164 = (bf16[512,1536]{1,0:T(8,128)(2,1)S(1)}, bf16[512,512]{1,0:T(8,128)(2,1)S(1)}, f32[1,512]{1,0:T(1,128)S(1)}, f32[1,512]{1,0:T(1,128)S(1)}, f32[1...) custom-call(bf16[512,1536]{1,0:T(8,128)(2,1)} %refs_0_.1, ...), custom_call_target="tpu_custom_call" | custom-call | tf_op jit(solution)/shard_map/pallas_call | solution.py:599
  23.1 4.4 %shard_map.165.rest_0_ = bf16[432,512]{1,0:T(8,128)(2,1)S(1)} custom-call(f32[8]{0:T(128)} %scale_ref.6, bf16[8,72,512]{2,1,0:T(8,128)(2,1)S(1)} %get-tuple-element.23.own_ref, bf16[8,72,512]{2,1,0:T(8,128)(2,1)S(1)} %collective-permute-done.other_ref, bf16[512,1536]{1,0:T(8,128)(2,1)S(1)} %get-tuple-element.26.packed_ref, ...), custom_call_target="tpu_custom_call" | custom-call | tf_op jit(solution)/shard_map/pallas_call | solution.py:599
  27.5 5.0 %shard_map.166.rest_0_.near_ref = bf16[144,1024]{1,0:T(8,128)(2,1)S(1)} custom-call(f32[8]{0:T(128)} %scale_ref.6, s32[3]{0:T(128)S(1)} %compare_convert_fusion.flags, bf16[8,72,512]{2,1,0:T(8,128)(2,1)S(1)} %get-tuple-element.23.own_ref, bf16[8,72,512]{2,1,0:T(8,128)(2,1)S(1)} %collective-permute-done.other_ref, ...), custom_call_target="tpu_custom_call" | custom-call | tf_op jit(solution)/shard_map/pallas_call | solution.py:599
  32.6 8.7 %shard_map.167 = (bf16[144,1024]{1,0:T(8,128)(2,1)S(1)}, bf16[72,1024]{1,0:T(8,128)(2,1)S(1)}) custom-call(f32[8]{0:T(128)} %scale_ref.6, s32[3]{0:T(128)S(1)} %compare_convert_fusion.flags, bf16[8,72,512]{2,1,0:T(8,128)(2,1)S(1)} %get-tuple-element.34.own_ref, bf16[8,72,512]{2,1,0:T(8,128)(2,1)S(1)} %collective-permute-done.5.other_ref, ...), custom_call_target="tpu_custom_call" | custom-call | tf_op jit(solution)/shard_map/pallas_call | solution.py:599
  41.3 1.8 %collective-permute-start.9 = (bf16[144,1024]{1,0:T(8,128)(2,1)S(1)}, bf16[144,1024]{1,0:T(8,128)(2,1)S(1)}, u32[]{:S(2)}, u32[]{:S(2)}) collective-permute-start(bf16[144,1024]{1,0:T(8,128)(2,1)S(1)} %get-tuple-element.35.far_ref), channel_id=1, source_target_pairs={{0,7},{1,2},{2,1},{3,4},{4,3},{5,6},{6,5},{7,0},{8,15},{9,10},{10,... | collective-permute-start | bytes 884744 | tf_op jit(solution)/shard_map/ppermute | solution.py:623
  43.1 1.8 %collective-permute-start.8 = (bf16[144,1024]{1,0:T(8,128)(2,1)S(1)}, bf16[144,1024]{1,0:T(8,128)(2,1)S(1)}, u32[]{:S(2)}, u32[]{:S(2)}) collective-permute-start(bf16[144,1024]{1,0:T(8,128)(2,1)S(1)} %shard_map.166.rest_0_.near_ref), channel_id=1, source_target_pairs={{0,7},{1,2},{2,1},{3,4},{4,3},{5,6},{6,5},{7,0},{8,15},{9,10},{10,... | collective-permute-start | bytes 884744 | tf_op jit(solution)/shard_map/ppermute | solution.py:623
  44.9 2.2 %collective-permute-start.10 = (bf16[72,1024]{1,0:T(8,128)(2,1)S(1)}, bf16[72,1024]{1,0:T(8,128)(2,1)S(1)}, u32[]{:S(2)}, u32[]{:S(2)}) collective-permute-start(bf16[72,1024]{1,0:T(8,128)(2,1)S(1)} %get-tuple-element.36), channel_id=1, source_target_pairs={{0,31},{1,26},{2,25},{3,28},{4,27},{5,30},{6,29},{7,24},{8,7},{9,2... | collective-permute-start | bytes 442376 | tf_op jit(solution)/shard_map/ppermute | solution.py:629
  47.1 1.9 %collective-permute-start.7 = (bf16[72,1024]{1,0:T(8,128)(2,1)S(1)}, bf16[72,1024]{1,0:T(8,128)(2,1)S(1)}, u32[]{:S(2)}, u32[]{:S(2)}) collective-permute-start(bf16[72,1024]{1,0:T(8,128)(2,1)S(1)} %get-tuple-element.36), channel_id=1, source_target_pairs={{0,24},{1,25},{2,26},{3,27},{4,28},{5,29},{6,30},{7,31},{8,0},{9,1... | collective-permute-start | bytes 442376 | tf_op jit(solution)/shard_map/ppermute | solution.py:629
  49.0 12.3 %collective-permute-done.10.other_rim_ref = bf16[72,1024]{1,0:T(8,128)(2,1)S(1)} collective-permute-done((bf16[72,1024]{1,0:T(8,128)(2,1)S(1)}, bf16[72,1024]{1,0:T(8,128)(2,1)S(1)}, u32[]{:S(2)}, u32[]{:S(2)}) %collective-permute-start.10) | collective-permute-done | bytes 147488 | tf_op jit(solution)/shard_map/ppermute | solution.py:629
  61.4 5.3 %shard_map.168 = (bf16[288,1024]{1,0:T(8,128)(2,1)S(1)}, bf16[108,1024]{1,0:T(8,128)(2,1)S(1)}, bf16[36,1024]{1,0:T(8,128)(2,1)S(1)}, bf16[36,1024]{1,0:T(8,128)(2,1)S(1)}) custom-call(f32[8]{0:T(128)} %scale_ref.7, s32[3]{0:T(128)S(1)} %compare_convert_fusion.flags, bf16[144,1024]{1,0:T(8,128)(2,1)S(1)} %shard_map.166.rest_0_.near_ref, ...), custom_call_target="tpu_custom_call" | custom-call | tf_op jit(solution)/shard_map/pallas_call | solution.py:599
  66.8 0.6 collective-permute-start.11
  67.5 0.8 %collective-permute-done.13.near_ref = bf16[108,1024]{1,0:T(8,128)(2,1)S(1)} collective-permute-done((bf16[108,1024]{1,0:T(8,128)(2,1)S(1)}, bf16[108,1024]{1,0:T(8,128)(2,1)S(1)}, u32[]{:S(2)}, u32[]{:S(2)}) %collective-permute-start.13) | collective-permute-done | bytes 221216 | tf_op jit(solution)/shard_map/ppermute | solution.py:618
  68.3 2.0 %shard_map.169._ = bf16[12,1,12,2,1024]{4,3,2,1,0:T(2,128)(2,1)} custom-call(s32[3]{0:T(128)S(1)} %compare_convert_fusion.flags, bf16[288,1024]{1,0:T(8,128)(2,1)S(1)} %get-tuple-element.39.second_ref, bf16[108,1024]{1,0:T(8,128)(2,1)S(1)} %collective-permute-done.13.near_ref, s32[576,18]{1,0:T(8,128)S(1)} %get-tuple-element.33.table_ref), custom_call_target="tpu_custom_call" | custom-call | tf_op jit(solution)/shard_map/pallas_call | solution.py:599
  70.3 2.8 %collective-permute-done.11.back_ref = bf16[36,1024]{1,0:T(8,128)(2,1)S(1)} collective-permute-done((bf16[36,1024]{1,0:T(8,128)(2,1)S(1)}, bf16[36,1024]{1,0:T(8,128)(2,1)S(1)}, u32[]{:S(2)}, u32[]{:S(2)}) %collective-permute-start.11) | collective-permute-done | bytes 73760 | tf_op jit(solution)/shard_map/ppermute | solution.py:629
  73.1 0.7 collective-permute-done.12.back_near_ref
  73.8 1.6 %shard_map.170 = bf16[12,1,12,2,1024]{4,3,2,1,0:T(2,128)(2,1)} custom-call(s32[3]{0:T(128)S(1)} %compare_convert_fusion.flags, bf16[36,1024]{1,0:T(8,128)(2,1)S(1)} %collective-permute-done.11.back_ref, bf16[36,1024]{1,0:T(8,128)(2,1)S(1)} %collective-permute-done.12.back_near_ref, ...), custom_call_target="tpu_custom_call", output_to_operand_aliasing={{}: (4, {})} | custom-call | tf_op jit(solution)/shard_map/pallas_call | solution.py:599
  (24 shorter events, 0.8 us)
Async XLA Ops:
  3.6 19.4 %collective-permute-start = (bf16[8,72,512]{2,1,0:T(8,128)(2,1)S(1)}, bf16[8,72,512]{2,1,0:T(8,128)(2,1)S(1)}, u32[]{:S(2)}, u32[]{:S(2)}) collective-permute-start(bf16[8,72,512]{2,1,0:T(8,128)(2,1)S(1)} %get-tuple-element.23.own_ref), channel_id=1, source_target_pairs={{0,1},{1,0},{2,3},{3,2},{4,5},{5,4},{6,7},{7,6},{8,9},{9,8},{10,11... | collective-permute-start | bytes 1769480 | tf_op jit(solution)/shard_map/ppermute | solution.py:618
  4.2 28.4 %collective-permute-start.5 = (bf16[8,72,512]{2,1,0:T(8,128)(2,1)S(1)}, bf16[8,72,512]{2,1,0:T(8,128)(2,1)S(1)}, u32[]{:S(2)}, u32[]{:S(2)}) collective-permute-start(bf16[8,72,512]{2,1,0:T(8,128)(2,1)S(1)} %get-tuple-element.34.own_ref), channel_id=1, source_target_pairs={{0,7},{1,2},{2,1},{3,4},{4,3},{5,6},{6,5},{7,0},{8,15},{9,10},{10,... | collective-permute-start | bytes 1769480 | tf_op jit(solution)/shard_map/ppermute | solution.py:623
  8.9 6.1 %collective-permute-start.1 = (bf16[2,72,512]{2,1,0:T(8,128)(2,1)S(1)}, bf16[2,72,512]{2,1,0:T(8,128)(2,1)S(1)}, u32[]{:S(2)}, u32[]{:S(2)}) collective-permute-start(bf16[2,72,512]{2,1,0:T(8,128)(2,1)S(1)} %get-tuple-element.24), channel_id=1, source_target_pairs={{0,8},{8,16},{16,24},{1,9},{9,17},{17,25},{2,10},{10,18},{18,26},{... | collective-permute-start | bytes 442376 | tf_op jit(solution)/shard_map/ppermute | solution.py:634
  12.3 7.0 %collective-permute-start.2 = (bf16[2,72,512]{2,1,0:T(8,128)(2,1)S(1)}, bf16[2,72,512]{2,1,0:T(8,128)(2,1)S(1)}, u32[]{:S(2)}, u32[]{:S(2)}) collective-permute-start(bf16[2,72,512]{2,1,0:T(8,128)(2,1)S(1)} %get-tuple-element.25), channel_id=1, source_target_pairs={{8,0},{16,8},{24,16},{9,1},{17,9},{25,17},{10,2},{18,10},{26,18},{... | collective-permute-start | bytes 442376 | tf_op jit(solution)/shard_map/ppermute | solution.py:634
  15.0 12.6 %collective-permute-start.3 = (bf16[2,72,512]{2,1,0:T(8,128)(2,1)S(1)}, bf16[2,72,512]{2,1,0:T(8,128)(2,1)S(1)}, u32[]{:S(2)}, u32[]{:S(2)}) collective-permute-start(bf16[2,72,512]{2,1,0:T(8,128)(2,1)S(1)} %collective-permute-done.1.top_ref), channel_id=1, source_target_pairs={{0,1},{1,0},{2,3},{3,2},{4,5},{5,4},{6,7},{7,6},{8,9},{9,8},{10,11... | collective-permute-start | bytes 442376 | tf_op jit(solution)/shard_map/ppermute | solution.py:618
  19.3 8.2 %collective-permute-start.4 = (bf16[2,72,512]{2,1,0:T(8,128)(2,1)S(1)}, bf16[2,72,512]{2,1,0:T(8,128)(2,1)S(1)}, u32[]{:S(2)}, u32[]{:S(2)}) collective-permute-start(bf16[2,72,512]{2,1,0:T(8,128)(2,1)S(1)} %collective-permute-done.2.bottom_ref), channel_id=1, source_target_pairs={{0,1},{1,0},{2,3},{3,2},{4,5},{5,4},{6,7},{7,6},{8,9},{9,8},{10,11... | collective-permute-start | bytes 442376 | tf_op jit(solution)/shard_map/ppermute | solution.py:618
  19.4 13.2 %collective-permute-start.6 = (bf16[2,72,512]{2,1,0:T(8,128)(2,1)S(1)}, bf16[2,72,512]{2,1,0:T(8,128)(2,1)S(1)}, u32[]{:S(2)}, u32[]{:S(2)}) collective-permute-start(bf16[2,72,512]{2,1,0:T(8,128)(2,1)S(1)} %pad_maximum_fusion), channel_id=1, source_target_pairs={{0,7},{1,2},{2,1},{3,4},{4,3},{5,6},{6,5},{7,0},{8,15},{9,10},{10,... | collective-permute-start | bytes 442376 | tf_op jit(solution)/shard_map/ppermute | solution.py:623
  32.5 28.8 %copy-start.1 = (bf16[512,1024]{1,0:T(8,128)(2,1)S(1)}, bf16[512,1024]{1,0:T(8,128)(2,1)}, u32[]{:S(2)}) copy-start(bf16[512,1024]{1,0:T(8,128)(2,1)} %output_ref.1) | copy-start | bytes 3145732
  32.5 28.8 %copy-start.2 = (f32[1024]{0:T(1024)S(1)}, f32[1024]{0:T(1024)}, u32[]{:S(2)}) copy-start(f32[1024]{0:T(1024)} %param.29) | copy-start | bytes 12292
  32.5 28.8 %copy-start.3 = (f32[1024]{0:T(1024)S(1)}, f32[1024]{0:T(1024)}, u32[]{:S(2)}) copy-start(f32[1024]{0:T(1024)} %param.30) | copy-start | bytes 12292
  32.6 28.8 %copy-start = (bf16[1024,1536]{1,0:T(8,128)(2,1)S(1)}, bf16[1024,1536]{1,0:T(8,128)(2,1)}, u32[]{:S(2)}) copy-start(bf16[1024,1536]{1,0:T(8,128)(2,1)} %packed_ref.1) | copy-start | bytes 9437188
  41.3 20.1 %collective-permute-start.9 = (bf16[144,1024]{1,0:T(8,128)(2,1)S(1)}, bf16[144,1024]{1,0:T(8,128)(2,1)S(1)}, u32[]{:S(2)}, u32[]{:S(2)}) collective-permute-start(bf16[144,1024]{1,0:T(8,128)(2,1)S(1)} %get-tuple-element.35.far_ref), channel_id=1, source_target_pairs={{0,7},{1,2},{2,1},{3,4},{4,3},{5,6},{6,5},{7,0},{8,15},{9,10},{10,... | collective-permute-start | bytes 884744 | tf_op jit(solution)/shard_map/ppermute | solution.py:623
  43.1 18.3 %collective-permute-start.8 = (bf16[144,1024]{1,0:T(8,128)(2,1)S(1)}, bf16[144,1024]{1,0:T(8,128)(2,1)S(1)}, u32[]{:S(2)}, u32[]{:S(2)}) collective-permute-start(bf16[144,1024]{1,0:T(8,128)(2,1)S(1)} %shard_map.166.rest_0_.near_ref), channel_id=1, source_target_pairs={{0,7},{1,2},{2,1},{3,4},{4,3},{5,6},{6,5},{7,0},{8,15},{9,10},{10,... | collective-permute-start | bytes 884744 | tf_op jit(solution)/shard_map/ppermute | solution.py:623
  44.9 16.5 %collective-permute-start.10 = (bf16[72,1024]{1,0:T(8,128)(2,1)S(1)}, bf16[72,1024]{1,0:T(8,128)(2,1)S(1)}, u32[]{:S(2)}, u32[]{:S(2)}) collective-permute-start(bf16[72,1024]{1,0:T(8,128)(2,1)S(1)} %get-tuple-element.36), channel_id=1, source_target_pairs={{0,31},{1,26},{2,25},{3,28},{4,27},{5,30},{6,29},{7,24},{8,7},{9,2... | collective-permute-start | bytes 442376 | tf_op jit(solution)/shard_map/ppermute | solution.py:629
  47.1 14.3 %collective-permute-start.7 = (bf16[72,1024]{1,0:T(8,128)(2,1)S(1)}, bf16[72,1024]{1,0:T(8,128)(2,1)S(1)}, u32[]{:S(2)}, u32[]{:S(2)}) collective-permute-start(bf16[72,1024]{1,0:T(8,128)(2,1)S(1)} %get-tuple-element.36), channel_id=1, source_target_pairs={{0,24},{1,25},{2,26},{3,27},{4,28},{5,29},{6,30},{7,31},{8,0},{9,1... | collective-permute-start | bytes 442376 | tf_op jit(solution)/shard_map/ppermute | solution.py:629
  66.7 1.6 %collective-permute-start.13 = (bf16[108,1024]{1,0:T(8,128)(2,1)S(1)}, bf16[108,1024]{1,0:T(8,128)(2,1)S(1)}, u32[]{:S(2)}, u32[]{:S(2)}) collective-permute-start(bf16[108,1024]{1,0:T(8,128)(2,1)S(1)} %get-tuple-element.40), channel_id=1, source_target_pairs={{0,1},{1,0},{2,3},{3,2},{4,5},{5,4},{6,7},{7,6},{8,9},{9,8},{10,11... | collective-permute-start | bytes 663560 | tf_op jit(solution)/shard_map/ppermute | solution.py:618
  66.8 6.3 %collective-permute-start.11 = (bf16[36,1024]{1,0:T(8,128)(2,1)S(1)}, bf16[36,1024]{1,0:T(8,128)(2,1)S(1)}, u32[]{:S(2)}, u32[]{:S(2)}) collective-permute-start(bf16[36,1024]{1,0:T(8,128)(2,1)S(1)} %get-tuple-element.37), channel_id=1, source_target_pairs={{0,8},{1,9},{2,10},{3,11},{4,12},{5,13},{6,14},{7,15},{8,16},{9,17... | collective-permute-start | bytes 221192 | tf_op jit(solution)/shard_map/ppermute | solution.py:629
  67.4 6.3 %collective-permute-start.12 = (bf16[36,1024]{1,0:T(8,128)(2,1)S(1)}, bf16[36,1024]{1,0:T(8,128)(2,1)S(1)}, u32[]{:S(2)}, u32[]{:S(2)}) collective-permute-start(bf16[36,1024]{1,0:T(8,128)(2,1)S(1)} %get-tuple-element.38), channel_id=1, source_target_pairs={{0,9},{1,8},{2,11},{3,10},{4,13},{5,12},{6,15},{7,14},{8,17},{9,16... | collective-permute-start | bytes 221192 | tf_op jit(solution)/shard_map/ppermute | solution.py:629

commit v6 on v5

--- a/solution.py
+++ b/solution.py
@@ -1,3 +1,4 @@
+import functools
 import math
 
 import jax
@@ -501,12 +502,86 @@
         ).astype(jnp.bfloat16)
 
 
-def second_kernel(
+def coarse_rows(w, span, near_ref, far_ref, rim_ref, table_ref, last):
+    small = rim_ref.shape[0] // 2
+    low, high = coarse_reach(w, small, near_ref.shape[0])
+    reach = [(0, low, high), (1, low, high)] + ([(2, 0, 2 * small)] if last else [])
+    rows = 0.0
+    for s, low, high in reach:
+        index = column_of(table_ref, COARSE + s, slice(w * span, (w + 1) * span))
+        rows += mm(one_hot(index, high - low), (near_ref, far_ref, rim_ref)[s][low:high])
+    return rows
+
+
+def head_sums():
+    block = 2 * LANES
+    rows = lax.broadcasted_iota(jnp.int32, (block, block), 0) // (LANES // 2)
+    cols = lax.broadcasted_iota(jnp.int32, (block, block), 1) // (LANES // 2)
+    return (rows == cols).astype(jnp.float32).astype(jnp.bfloat16)
+
+
+def mine_kernel(
+    span,
     scale_ref,
-    flags,
     near_ref,
     far_ref,
     rim_ref,
+    packed_ref,
+    table_ref,
+    own_ref,
+    query_ref,
+    key_ref,
+    value_ref,
+):
+    windows = own_ref.shape[0] // span
+    for w in range(windows):
+        rows = coarse_rows(w, span, near_ref, far_ref, rim_ref, table_ref, w == windows - 1)
+        own_ref[w * span : (w + 1) * span] = rows.astype(jnp.bfloat16)
+    width = key_ref.shape[1]
+    block = 2 * LANES
+    same = head_sums()
+    lane = lax.broadcasted_iota(jnp.int32, (1, block), 1)
+    first = (lane % LANES < LANES // 2).astype(jnp.float32)
+    head = lane // (LANES // 2)
+
+    def multiply(task, _):
+        start = "qkv".index(task[0]) * width + task[1] * block
+        return mm(own_ref[...], packed_ref[:, start : start + block])
+
+    def measure(task, rows):
+        return rows, None if task[0] == "v" else mm((rows * rows).astype(jnp.bfloat16), same)
+
+    def keep(task, held):
+        kind, j = task
+        rows, total = held
+        at = slice(j * block, (j + 1) * block)
+        if kind == "v":
+            value_ref[:, at] = rows
+            return
+        rows = rows * lax.rsqrt(total + unit_eps)
+        if kind == "k":
+            key_ref[:, at] = rows
+            return
+        scale = jnp.zeros((1, block), jnp.float32)
+        for h in range(2 * block // LANES):
+            scale = jnp.where(head == h, scale_ref[j * 2 * block // LANES + h], scale)
+        scale = scale * math.log2(math.e)
+        left, right = rows * (scale * first), rows * (scale * (1.0 - first))
+        for g in range(rows.shape[0] // GROUP):
+            mine = slice(g * GROUP, (g + 1) * GROUP)
+            query_ref[2 * g * GROUP : 2 * (g + 1) * GROUP, at] = jnp.concatenate(
+                [left[mine], right[mine]], axis=0
+            ).astype(jnp.bfloat16)
+
+    staged([(k, j) for j in range(width // block) for k in "qkv"], [multiply, measure, keep])
+
+
+def second_kernel(
+    flags,
+    own_ref,
+    query_ref,
+    own_key_ref,
+    own_value_ref,
     other_near_ref,
     other_far_ref,
     other_rim_ref,
@@ -520,32 +595,46 @@
     send_ref,
     return_ref,
     return_near_ref,
-    own,
-    both,
-    query,
+    other,
     key,
     value,
     prob,
     ctx,
 ):
     span = open_ref.shape[0] * GROUP
-    windows = own.shape[0] // span
-    small = rim_ref.shape[0] // 2
+    windows = own_ref.shape[0] // span
     for w in range(windows):
-        low, high = coarse_reach(w, small, near_ref.shape[0])
-        reach = [(0, low, high), (1, low, high)]
-        if w == windows - 1:
-            reach.append((2, 0, 2 * small))
-        mine = theirs = 0.0
-        for s, low, high in reach:
-            at = slice(w * span, (w + 1) * span)
-            pick = one_hot(column_of(table_ref, COARSE + s, at), high - low)
-            mine += mm(pick, (near_ref, far_ref, rim_ref)[s][low:high])
-            theirs += mm(pick, (other_near_ref, other_far_ref, other_rim_ref)[s][low:high])
-        keep_window(w, mine, theirs, own, both)
-    project(own, both, packed_ref, scale_ref, query, key, value)
-    attend([None] * (windows - 1) + [flags[1]], query, key, value, open_ref, prob, ctx)
-    second = block_rows(own, ctx, output_ref, gain_ref, offset_ref)
+        rows = coarse_rows(
+            w, span, other_near_ref, other_far_ref, other_rim_ref, table_ref, w == windows - 1
+        )
+        other[w * span : (w + 1) * span] = rows.astype(jnp.bfloat16)
+    width = own_key_ref.shape[1]
+    block = 2 * LANES
+    same = head_sums()
+
+    def multiply(task, _):
+        start = "qkv".index(task[0]) * width + task[1] * block
+        return mm(other[...], packed_ref[:, start : start + block])
+
+    def measure(task, rows):
+        return rows, None if task[0] == "v" else mm((rows * rows).astype(jnp.bfloat16), same)
+
+    def keep(task, held):
+        kind, j = task
+        rows, total = held
+        at = slice(j * block, (j + 1) * block)
+        if kind == "k":
+            rows = rows * lax.rsqrt(total + unit_eps)
+        source, dst = (own_key_ref, key) if kind == "k" else (own_value_ref, value)
+        for g in range(rows.shape[0] // GROUP):
+            mine = slice(g * GROUP, (g + 1) * GROUP)
+            dst[2 * g * GROUP : 2 * (g + 1) * GROUP, at] = jnp.concatenate(
+                [source[mine, at], rows[mine]], axis=0
+            ).astype(jnp.bfloat16)
+
+    staged([(k, j) for j in range(width // block) for k in "kv"], [multiply, measure, keep])
+    attend([None] * (windows - 1) + [flags[1]], query_ref, key, value, open_ref, prob, ctx)
+    second = block_rows(own_ref, ctx, output_ref, gain_ref, offset_ref)
     second_ref[...] = second
     counts = [padded(ref.shape[0]) for ref in (send_ref, return_ref, return_near_ref)]
     index = parity_column(table_ref, SEND, 1, flags[2], slice(0, sum(counts)))
@@ -739,6 +828,19 @@
     share = levels // 2 * HALF_LON
 
     back = jax.ShapeDtypeStruct((HALF_LAT * share, wide), bf16)
+    rows = windows * span
+    mine = call(
+        functools.partial(mine_kernel, span),
+        [
+            jax.ShapeDtypeStruct((rows, wide), bf16),
+            jax.ShapeDtypeStruct((2 * rows, second_inner), bf16),
+            jax.ShapeDtypeStruct((rows, second_inner), jnp.float32),
+            jax.ShapeDtypeStruct((rows, second_inner), jnp.float32),
+        ],
+        [],
+        [in_hbm(scale_second)],
+        [merged_near, merged_far, rim, packed_second, table],
+    )
     second, send, back_same, back_near = call(
         second_kernel,
         [
@@ -747,12 +849,10 @@
             back,
             back,
         ],
-        attention_scratch(windows * span, second_inner, wide),
-        [in_hbm(scale_second), flags],
+        [pltpu.VMEM((rows, wide), bf16)] + attention_scratch(rows, second_inner, wide)[3:],
+        [flags],
         [
-            merged_near,
-            merged_far,
-            rim,
+            *mine,
             other_near,
             other_far,
             other_rim,

time: 75.8 us -> 74.1 us (0.978)
  waiting for transfers between devices: 22.4 us -> 20.2 us
  Pallas kernels: 31.7 us -> 32.5 us
    ppermute x4, waiting for transfers between devices: 15.8 us -> 13.7 us  [ring(): return lax.ppermute(value, ('lat', 'lon'), links)]
    pallas_call x8 -> x9, Pallas kernels: 31.7 us -> 32.5 us  [call(): pl.pallas_call(kernel, out_shape=outs, in_specs=[pl.BlockSpec(memory_spac...]
  transfers between devices with their start and end apart: 14 -> 14, of which waited for: 6 -> 7; matrix products, arithmetic and copies ran while one was open for 0% -> 0% of each run, Pallas kernels for 17% -> 21%
where the time goes in v6:
time: 74.1 us; the launch traced here: 73.8 us
  Pallas kernels  32.5 us (44%)
  waiting for transfers between devices  20.2 us (27%)
  starting transfers between devices  20.1 us (27%)
  other arithmetic  0.75 us (1%)
    pallas_call x9, Pallas kernels, call(): pl.pallas_call(kernel, out_shape=outs, in_specs=[pl.BlockSpec(memory_spac...  32.5 us
    ppermute x4, waiting for transfers between devices, ring(): return lax.ppermute(value, ('lat', 'lon'), links)  13.7 us
    ppermute x4, starting transfers between devices, far_swap(): return lax.ppermute(value, 'lon', [(i, far_of(i, n)) for i in range(n)])  10.2 us
    ppermute x2, waiting for transfers between devices, shift(): lax.ppermute(value, 'lat', [(i, i + by) for i in range(n) if 0 <= i + by...  5.72 us
    ppermute x2, starting transfers between devices, shift(): lax.ppermute(value, 'lat', [(i, i + by) for i in range(n) if 0 <= i + by...  4.69 us
    ppermute x4, starting transfers between devices, ring(): return lax.ppermute(value, ('lat', 'lon'), links)  4.55 us
  transfers between devices with their start and end apart: 14, of which 7 were waited for; matrix products, arithmetic and copies ran while one was open for 0% of the time, Pallas kernels for 21%

profile of v6, /device:TPU:0, one launch (start us, length us, event | category | flops | bytes accessed | tf_op | source)
XLA Modules:
  0.0 73.8 jit_solution(12898833023604328971)
XLA Ops:
  0.0 0.7 compare_convert_fusion.flags
  0.7 2.9 %shard_map.163 = (bf16[8,72,512]{2,1,0:T(8,128)(2,1)S(1)}, bf16[8,72,512]{2,1,0:T(8,128)(2,1)S(1)}, bf16[2,72,512]{2,1,0:T(8,128)(2,1)S(1)}, bf16[2,72,512]{2,1,0:T(8,128)(2,1)S(1)}) custom-call(s32[3]{0:T(128)S(1)} %compare_convert_fusion.flags, bf16[4,12,24,512]{3,2,1,0:T(8,128)(2,1)} %bitcast.12), custom_call_target="tpu_custom_call" | custom-call | tf_op jit(solution)/shard_map/pallas_call | solution.py:688
  4.2 4.7 %collective-permute-start.5 = (bf16[8,72,512]{2,1,0:T(8,128)(2,1)S(1)}, bf16[8,72,512]{2,1,0:T(8,128)(2,1)S(1)}, u32[]{:S(2)}, u32[]{:S(2)}) collective-permute-start(bf16[8,72,512]{2,1,0:T(8,128)(2,1)S(1)} %get-tuple-element.38.own_ref), channel_id=1, source_target_pairs={{0,7},{1,2},{2,1},{3,4},{4,3},{5,6},{6,5},{7,0},{8,15},{9,10},{10,... | collective-permute-start | bytes 1769480 | tf_op jit(solution)/shard_map/ppermute | solution.py:712
  8.9 3.4 %collective-permute-start.1 = (bf16[2,72,512]{2,1,0:T(8,128)(2,1)S(1)}, bf16[2,72,512]{2,1,0:T(8,128)(2,1)S(1)}, u32[]{:S(2)}, u32[]{:S(2)}) collective-permute-start(bf16[2,72,512]{2,1,0:T(8,128)(2,1)S(1)} %get-tuple-element.28), channel_id=1, source_target_pairs={{0,8},{8,16},{16,24},{1,9},{9,17},{17,25},{2,10},{10,18},{18,26},{... | collective-permute-start | bytes 442376 | tf_op jit(solution)/shard_map/ppermute | solution.py:723
  12.3 1.3 %collective-permute-start.2 = (bf16[2,72,512]{2,1,0:T(8,128)(2,1)S(1)}, bf16[2,72,512]{2,1,0:T(8,128)(2,1)S(1)}, u32[]{:S(2)}, u32[]{:S(2)}) collective-permute-start(bf16[2,72,512]{2,1,0:T(8,128)(2,1)S(1)} %get-tuple-element.29), channel_id=1, source_target_pairs={{8,0},{16,8},{24,16},{9,1},{17,9},{25,17},{10,2},{18,10},{26,18},{... | collective-permute-start | bytes 442376 | tf_op jit(solution)/shard_map/ppermute | solution.py:723
  13.6 1.3 %collective-permute-done.1.top_ref = bf16[2,72,512]{2,1,0:T(8,128)(2,1)S(1)} collective-permute-done((bf16[2,72,512]{2,1,0:T(8,128)(2,1)S(1)}, bf16[2,72,512]{2,1,0:T(8,128)(2,1)S(1)}, u32[]{:S(2)}, u32[]{:S(2)}) %collective-permute-start.1) | collective-permute-done | bytes 147488 | tf_op jit(solution)/shard_map/ppermute | solution.py:723
  15.0 4.4 %collective-permute-done.2.bottom_ref = bf16[2,72,512]{2,1,0:T(8,128)(2,1)S(1)} collective-permute-done((bf16[2,72,512]{2,1,0:T(8,128)(2,1)S(1)}, bf16[2,72,512]{2,1,0:T(8,128)(2,1)S(1)}, u32[]{:S(2)}, u32[]{:S(2)}) %collective-permute-start.2) | collective-permute-done | bytes 147488 | tf_op jit(solution)/shard_map/ppermute | solution.py:723
  19.4 1.9 %collective-permute-start.6 = (bf16[2,72,512]{2,1,0:T(8,128)(2,1)S(1)}, bf16[2,72,512]{2,1,0:T(8,128)(2,1)S(1)}, u32[]{:S(2)}, u32[]{:S(2)}) collective-permute-start(bf16[2,72,512]{2,1,0:T(8,128)(2,1)S(1)} %pad_maximum_fusion), channel_id=1, source_target_pairs={{0,7},{1,2},{2,1},{3,4},{4,3},{5,6},{6,5},{7,0},{8,15},{9,10},{10,... | collective-permute-start | bytes 442376 | tf_op jit(solution)/shard_map/ppermute | solution.py:712
  21.3 1.8 %shard_map.164 = (bf16[512,1536]{1,0:T(8,128)(2,1)S(1)}, bf16[512,512]{1,0:T(8,128)(2,1)S(1)}, f32[1,512]{1,0:T(1,128)S(1)}, f32[1,512]{1,0:T(1,128)S(1)}, f32[1...) custom-call(bf16[512,1536]{1,0:T(8,128)(2,1)} %refs_0_.1, ...), custom_call_target="tpu_custom_call" | custom-call | tf_op jit(solution)/shard_map/pallas_call | solution.py:688
  23.1 4.4 %shard_map.165.rest_0_ = bf16[432,512]{1,0:T(8,128)(2,1)S(1)} custom-call(f32[8]{0:T(128)} %scale_ref.6, bf16[8,72,512]{2,1,0:T(8,128)(2,1)S(1)} %get-tuple-element.27.own_ref, bf16[8,72,512]{2,1,0:T(8,128)(2,1)S(1)} %collective-permute-done.other_ref, bf16[512,1536]{1,0:T(8,128)(2,1)S(1)} %get-tuple-element.30.packed_ref, ...), custom_call_target="tpu_custom_call" | custom-call | tf_op jit(solution)/shard_map/pallas_call | solution.py:688
  27.5 5.0 %shard_map.166.rest_0_.near_ref = bf16[144,1024]{1,0:T(8,128)(2,1)S(1)} custom-call(f32[8]{0:T(128)} %scale_ref.6, s32[3]{0:T(128)S(1)} %compare_convert_fusion.flags, bf16[8,72,512]{2,1,0:T(8,128)(2,1)S(1)} %get-tuple-element.27.own_ref, bf16[8,72,512]{2,1,0:T(8,128)(2,1)S(1)} %collective-permute-done.other_ref, ...), custom_call_target="tpu_custom_call" | custom-call | tf_op jit(solution)/shard_map/pallas_call | solution.py:688
  32.6 8.7 %shard_map.167 = (bf16[144,1024]{1,0:T(8,128)(2,1)S(1)}, bf16[72,1024]{1,0:T(8,128)(2,1)S(1)}) custom-call(f32[8]{0:T(128)} %scale_ref.6, s32[3]{0:T(128)S(1)} %compare_convert_fusion.flags, bf16[8,72,512]{2,1,0:T(8,128)(2,1)S(1)} %get-tuple-element.38.own_ref, bf16[8,72,512]{2,1,0:T(8,128)(2,1)S(1)} %collective-permute-done.5.other_ref, ...), custom_call_target="tpu_custom_call" | custom-call | tf_op jit(solution)/shard_map/pallas_call | solution.py:688
  41.2 1.8 %collective-permute-start.9 = (bf16[144,1024]{1,0:T(8,128)(2,1)S(1)}, bf16[144,1024]{1,0:T(8,128)(2,1)S(1)}, u32[]{:S(2)}, u32[]{:S(2)}) collective-permute-start(bf16[144,1024]{1,0:T(8,128)(2,1)S(1)} %get-tuple-element.39.far_ref), channel_id=1, source_target_pairs={{0,7},{1,2},{2,1},{3,4},{4,3},{5,6},{6,5},{7,0},{8,15},{9,10},{10,... | collective-permute-start | bytes 884744 | tf_op jit(solution)/shard_map/ppermute | solution.py:712
  43.0 1.8 %collective-permute-start.8 = (bf16[144,1024]{1,0:T(8,128)(2,1)S(1)}, bf16[144,1024]{1,0:T(8,128)(2,1)S(1)}, u32[]{:S(2)}, u32[]{:S(2)}) collective-permute-start(bf16[144,1024]{1,0:T(8,128)(2,1)S(1)} %shard_map.166.rest_0_.near_ref), channel_id=1, source_target_pairs={{0,7},{1,2},{2,1},{3,4},{4,3},{5,6},{6,5},{7,0},{8,15},{9,10},{10,... | collective-permute-start | bytes 884744 | tf_op jit(solution)/shard_map/ppermute | solution.py:712
  44.9 3.9 %collective-permute-start.10 = (bf16[72,1024]{1,0:T(8,128)(2,1)S(1)}, bf16[72,1024]{1,0:T(8,128)(2,1)S(1)}, u32[]{:S(2)}, u32[]{:S(2)}) collective-permute-start(bf16[72,1024]{1,0:T(8,128)(2,1)S(1)} %get-tuple-element.40), channel_id=1, source_target_pairs={{0,31},{1,26},{2,25},{3,28},{4,27},{5,30},{6,29},{7,24},{8,7},{9,2... | collective-permute-start | bytes 442376 | tf_op jit(solution)/shard_map/ppermute | solution.py:718
  48.7 1.3 %collective-permute-done.7.rim_ref = bf16[72,1024]{1,0:T(8,128)(2,1)S(1)} collective-permute-done((bf16[72,1024]{1,0:T(8,128)(2,1)S(1)}, bf16[72,1024]{1,0:T(8,128)(2,1)S(1)}, u32[]{:S(2)}, u32[]{:S(2)}) %collective-permute-start.7) | collective-permute-done | bytes 147488 | tf_op jit(solution)/shard_map/ppermute | solution.py:718
  50.0 2.4 %shard_map.168 = (bf16[288,1024]{1,0:T(8,128)(2,1)S(1)}, bf16[576,512]{1,0:T(8,128)(2,1)S(1)}, f32[288,512]{1,0:T(8,128)S(1)}, f32[288,512]{1,0:T(8,128)S(1)}) custom-call(f32[8]{0:T(128)} %scale_ref.7, bf16[144,1024]{1,0:T(8,128)(2,1)S(1)} %shard_map.166.rest_0_.near_ref, bf16[144,1024]{1,0:T(8,128)(2,1)S(1)} %get-tuple-element.39.far_ref, ...), custom_call_target="tpu_custom_call" | custom-call | tf_op jit(solution)/shard_map/pallas_call | solution.py:688
  52.4 8.9 %collective-permute-done.10.other_rim_ref = bf16[72,1024]{1,0:T(8,128)(2,1)S(1)} collective-permute-done((bf16[72,1024]{1,0:T(8,128)(2,1)S(1)}, bf16[72,1024]{1,0:T(8,128)(2,1)S(1)}, u32[]{:S(2)}, u32[]{:S(2)}) %collective-permute-start.10) | collective-permute-done | bytes 147488 | tf_op jit(solution)/shard_map/ppermute | solution.py:718
  61.3 3.7 %shard_map.169 = (bf16[288,1024]{1,0:T(8,128)(2,1)S(1)}, bf16[108,1024]{1,0:T(8,128)(2,1)S(1)}, bf16[36,1024]{1,0:T(8,128)(2,1)S(1)}, bf16[36,1024]{1,0:T(8,128)(2,1)S(1)}) custom-call(s32[3]{0:T(128)S(1)} %compare_convert_fusion.flags, bf16[288,1024]{1,0:T(8,128)(2,1)S(1)} %get-tuple-element.41.own_ref, bf16[576,512]{1,0:T(8,128)(2,1)S(1)} %get-tuple-element.42.query_ref, ...), custom_call_target="tpu_custom_call" | custom-call | tf_op jit(solution)/shard_map/pallas_call | solution.py:688
  65.8 0.8 %collective-permute-done.13.near_ref = bf16[108,1024]{1,0:T(8,128)(2,1)S(1)} collective-permute-done((bf16[108,1024]{1,0:T(8,128)(2,1)S(1)}, bf16[108,1024]{1,0:T(8,128)(2,1)S(1)}, u32[]{:S(2)}, u32[]{:S(2)}) %collective-permute-start.13) | collective-permute-done | bytes 221216 | tf_op jit(solution)/shard_map/ppermute | solution.py:707
  66.6 2.0 %shard_map.170._ = bf16[12,1,12,2,1024]{4,3,2,1,0:T(2,128)(2,1)} custom-call(s32[3]{0:T(128)S(1)} %compare_convert_fusion.flags, bf16[288,1024]{1,0:T(8,128)(2,1)S(1)} %get-tuple-element.47.second_ref, bf16[108,1024]{1,0:T(8,128)(2,1)S(1)} %collective-permute-done.13.near_ref, s32[576,18]{1,0:T(8,128)S(1)} %get-tuple-element.37.table_ref), custom_call_target="tpu_custom_call" | custom-call | tf_op jit(solution)/shard_map/pallas_call | solution.py:688
  68.6 2.8 %collective-permute-done.11.back_ref = bf16[36,1024]{1,0:T(8,128)(2,1)S(1)} collective-permute-done((bf16[36,1024]{1,0:T(8,128)(2,1)S(1)}, bf16[36,1024]{1,0:T(8,128)(2,1)S(1)}, u32[]{:S(2)}, u32[]{:S(2)}) %collective-permute-start.11) | collective-permute-done | bytes 73760 | tf_op jit(solution)/shard_map/ppermute | solution.py:718
  71.4 0.7 collective-permute-done.12.back_near_ref
  72.1 1.6 %shard_map.171 = bf16[12,1,12,2,1024]{4,3,2,1,0:T(2,128)(2,1)} custom-call(s32[3]{0:T(128)S(1)} %compare_convert_fusion.flags, bf16[36,1024]{1,0:T(8,128)(2,1)S(1)} %collective-permute-done.11.back_ref, bf16[36,1024]{1,0:T(8,128)(2,1)S(1)} %collective-permute-done.12.back_near_ref, ...), custom_call_target="tpu_custom_call", output_to_operand_aliasing={{}: (4, {})} | custom-call | tf_op jit(solution)/shard_map/pallas_call | solution.py:688
  (25 shorter events, 1.4 us)
Async XLA Ops:
  3.6 19.4 %collective-permute-start = (bf16[8,72,512]{2,1,0:T(8,128)(2,1)S(1)}, bf16[8,72,512]{2,1,0:T(8,128)(2,1)S(1)}, u32[]{:S(2)}, u32[]{:S(2)}) collective-permute-start(bf16[8,72,512]{2,1,0:T(8,128)(2,1)S(1)} %get-tuple-element.27.own_ref), channel_id=1, source_target_pairs={{0,1},{1,0},{2,3},{3,2},{4,5},{5,4},{6,7},{7,6},{8,9},{9,8},{10,11... | collective-permute-start | bytes 1769480 | tf_op jit(solution)/shard_map/ppermute | solution.py:707
  4.2 28.3 %collective-permute-start.5 = (bf16[8,72,512]{2,1,0:T(8,128)(2,1)S(1)}, bf16[8,72,512]{2,1,0:T(8,128)(2,1)S(1)}, u32[]{:S(2)}, u32[]{:S(2)}) collective-permute-start(bf16[8,72,512]{2,1,0:T(8,128)(2,1)S(1)} %get-tuple-element.38.own_ref), channel_id=1, source_target_pairs={{0,7},{1,2},{2,1},{3,4},{4,3},{5,6},{6,5},{7,0},{8,15},{9,10},{10,... | collective-permute-start | bytes 1769480 | tf_op jit(solution)/shard_map/ppermute | solution.py:712
  8.9 6.1 %collective-permute-start.1 = (bf16[2,72,512]{2,1,0:T(8,128)(2,1)S(1)}, bf16[2,72,512]{2,1,0:T(8,128)(2,1)S(1)}, u32[]{:S(2)}, u32[]{:S(2)}) collective-permute-start(bf16[2,72,512]{2,1,0:T(8,128)(2,1)S(1)} %get-tuple-element.28), channel_id=1, source_target_pairs={{0,8},{8,16},{16,24},{1,9},{9,17},{17,25},{2,10},{10,18},{18,26},{... | collective-permute-start | bytes 442376 | tf_op jit(solution)/shard_map/ppermute | solution.py:723
  12.3 7.0 %collective-permute-start.2 = (bf16[2,72,512]{2,1,0:T(8,128)(2,1)S(1)}, bf16[2,72,512]{2,1,0:T(8,128)(2,1)S(1)}, u32[]{:S(2)}, u32[]{:S(2)}) collective-permute-start(bf16[2,72,512]{2,1,0:T(8,128)(2,1)S(1)} %get-tuple-element.29), channel_id=1, source_target_pairs={{8,0},{16,8},{24,16},{9,1},{17,9},{25,17},{10,2},{18,10},{26,18},{... | collective-permute-start | bytes 442376 | tf_op jit(solution)/shard_map/ppermute | solution.py:723
  15.0 12.6 %collective-permute-start.3 = (bf16[2,72,512]{2,1,0:T(8,128)(2,1)S(1)}, bf16[2,72,512]{2,1,0:T(8,128)(2,1)S(1)}, u32[]{:S(2)}, u32[]{:S(2)}) collective-permute-start(bf16[2,72,512]{2,1,0:T(8,128)(2,1)S(1)} %collective-permute-done.1.top_ref), channel_id=1, source_target_pairs={{0,1},{1,0},{2,3},{3,2},{4,5},{5,4},{6,7},{7,6},{8,9},{9,8},{10,11... | collective-permute-start | bytes 442376 | tf_op jit(solution)/shard_map/ppermute | solution.py:707
  19.3 8.2 %collective-permute-start.4 = (bf16[2,72,512]{2,1,0:T(8,128)(2,1)S(1)}, bf16[2,72,512]{2,1,0:T(8,128)(2,1)S(1)}, u32[]{:S(2)}, u32[]{:S(2)}) collective-permute-start(bf16[2,72,512]{2,1,0:T(8,128)(2,1)S(1)} %collective-permute-done.2.bottom_ref), channel_id=1, source_target_pairs={{0,1},{1,0},{2,3},{3,2},{4,5},{5,4},{6,7},{7,6},{8,9},{9,8},{10,11... | collective-permute-start | bytes 442376 | tf_op jit(solution)/shard_map/ppermute | solution.py:707
  19.4 13.1 %collective-permute-start.6 = (bf16[2,72,512]{2,1,0:T(8,128)(2,1)S(1)}, bf16[2,72,512]{2,1,0:T(8,128)(2,1)S(1)}, u32[]{:S(2)}, u32[]{:S(2)}) collective-permute-start(bf16[2,72,512]{2,1,0:T(8,128)(2,1)S(1)} %pad_maximum_fusion), channel_id=1, source_target_pairs={{0,7},{1,2},{2,1},{3,4},{4,3},{5,6},{6,5},{7,0},{8,15},{9,10},{10,... | collective-permute-start | bytes 442376 | tf_op jit(solution)/shard_map/ppermute | solution.py:712
  32.5 17.4 %copy-start = (bf16[1024,1536]{1,0:T(8,128)(2,1)S(1)}, bf16[1024,1536]{1,0:T(8,128)(2,1)}, u32[]{:S(2)}) copy-start(bf16[1024,1536]{1,0:T(8,128)(2,1)} %packed_ref.3) | copy-start | bytes 9437188
  41.2 20.1 %collective-permute-start.9 = (bf16[144,1024]{1,0:T(8,128)(2,1)S(1)}, bf16[144,1024]{1,0:T(8,128)(2,1)S(1)}, u32[]{:S(2)}, u32[]{:S(2)}) collective-permute-start(bf16[144,1024]{1,0:T(8,128)(2,1)S(1)} %get-tuple-element.39.far_ref), channel_id=1, source_target_pairs={{0,7},{1,2},{2,1},{3,4},{4,3},{5,6},{6,5},{7,0},{8,15},{9,10},{10,... | collective-permute-start | bytes 884744 | tf_op jit(solution)/shard_map/ppermute | solution.py:712
  43.0 18.3 %collective-permute-start.8 = (bf16[144,1024]{1,0:T(8,128)(2,1)S(1)}, bf16[144,1024]{1,0:T(8,128)(2,1)S(1)}, u32[]{:S(2)}, u32[]{:S(2)}) collective-permute-start(bf16[144,1024]{1,0:T(8,128)(2,1)S(1)} %shard_map.166.rest_0_.near_ref), channel_id=1, source_target_pairs={{0,7},{1,2},{2,1},{3,4},{4,3},{5,6},{6,5},{7,0},{8,15},{9,10},{10,... | collective-permute-start | bytes 884744 | tf_op jit(solution)/shard_map/ppermute | solution.py:712
  44.8 16.5 %copy-start.1 = (bf16[512,1024]{1,0:T(8,128)(2,1)S(1)}, bf16[512,1024]{1,0:T(8,128)(2,1)}, u32[]{:S(2)}) copy-start(bf16[512,1024]{1,0:T(8,128)(2,1)} %output_ref.1) | copy-start | bytes 3145732
  44.8 16.5 %copy-start.2 = (f32[1024]{0:T(1024)S(1)}, f32[1024]{0:T(1024)}, u32[]{:S(2)}) copy-start(f32[1024]{0:T(1024)} %param.29) | copy-start | bytes 12292
  44.8 16.5 %copy-start.3 = (f32[1024]{0:T(1024)S(1)}, f32[1024]{0:T(1024)}, u32[]{:S(2)}) copy-start(f32[1024]{0:T(1024)} %param.30) | copy-start | bytes 12292
  44.8 5.1 %collective-permute-start.7 = (bf16[72,1024]{1,0:T(8,128)(2,1)S(1)}, bf16[72,1024]{1,0:T(8,128)(2,1)S(1)}, u32[]{:S(2)}, u32[]{:S(2)}) collective-permute-start(bf16[72,1024]{1,0:T(8,128)(2,1)S(1)} %get-tuple-element.40), channel_id=1, source_target_pairs={{0,24},{1,25},{2,26},{3,27},{4,28},{5,29},{6,30},{7,31},{8,0},{9,1... | collective-permute-start | bytes 442376 | tf_op jit(solution)/shard_map/ppermute | solution.py:718
  44.9 16.5 %collective-permute-start.10 = (bf16[72,1024]{1,0:T(8,128)(2,1)S(1)}, bf16[72,1024]{1,0:T(8,128)(2,1)S(1)}, u32[]{:S(2)}, u32[]{:S(2)}) collective-permute-start(bf16[72,1024]{1,0:T(8,128)(2,1)S(1)} %get-tuple-element.40), channel_id=1, source_target_pairs={{0,31},{1,26},{2,25},{3,28},{4,27},{5,30},{6,29},{7,24},{8,7},{9,2... | collective-permute-start | bytes 442376 | tf_op jit(solution)/shard_map/ppermute | solution.py:718
  65.1 1.6 %collective-permute-start.13 = (bf16[108,1024]{1,0:T(8,128)(2,1)S(1)}, bf16[108,1024]{1,0:T(8,128)(2,1)S(1)}, u32[]{:S(2)}, u32[]{:S(2)}) collective-permute-start(bf16[108,1024]{1,0:T(8,128)(2,1)S(1)} %get-tuple-element.48), channel_id=1, source_target_pairs={{0,1},{1,0},{2,3},{3,2},{4,5},{5,4},{6,7},{7,6},{8,9},{9,8},{10,11... | collective-permute-start | bytes 663560 | tf_op jit(solution)/shard_map/ppermute | solution.py:707
  65.1 6.3 %collective-permute-start.11 = (bf16[36,1024]{1,0:T(8,128)(2,1)S(1)}, bf16[36,1024]{1,0:T(8,128)(2,1)S(1)}, u32[]{:S(2)}, u32[]{:S(2)}) collective-permute-start(bf16[36,1024]{1,0:T(8,128)(2,1)S(1)} %get-tuple-element.45), channel_id=1, source_target_pairs={{0,8},{1,9},{2,10},{3,11},{4,12},{5,13},{6,14},{7,15},{8,16},{9,17... | collective-permute-start | bytes 221192 | tf_op jit(solution)/shard_map/ppermute | solution.py:718
  65.8 6.3 %collective-permute-start.12 = (bf16[36,1024]{1,0:T(8,128)(2,1)S(1)}, bf16[36,1024]{1,0:T(8,128)(2,1)S(1)}, u32[]{:S(2)}, u32[]{:S(2)}) collective-permute-start(bf16[36,1024]{1,0:T(8,128)(2,1)S(1)} %get-tuple-element.46), channel_id=1, source_target_pairs={{0,9},{1,8},{2,11},{3,10},{4,13},{5,12},{6,15},{7,14},{8,17},{9,16... | collective-permute-start | bytes 221192 | tf_op jit(solution)/shard_map/ppermute | solution.py:718

commit v7 on v6

--- a/solution.py
+++ b/solution.py
@@ -649,13 +649,15 @@
 def place(pieces, out_ref, rows_ref, sem, low):
     rows, _, columns, pair, _ = rows_ref.shape
     block = sum(mm(one_hot(index, ref.shape[0]), ref[...]) for index, ref in pieces)
+    copies = []
     for r in range(rows):
         for c in range(columns):
             at = (r * columns + c) * pair
             rows_ref[r, 0, c] = block[at : at + pair].astype(jnp.bfloat16)
-    copy = pltpu.make_async_copy(rows_ref, out_ref.at[low : low + rows], sem)
-    copy.start()
-    copy.wait()
+        copies.append(pltpu.make_async_copy(rows_ref.at[r], out_ref.at[low + r], sem.at[r]))
+        copies[-1].start()
+    for copy in copies:
+        copy.wait()
 
 
 def place_columns(flags, table_ref, out_ref, which, early):
@@ -871,7 +873,7 @@
     whole = [jax.ShapeDtypeStruct(shape, bf16)]
 
     def room(rows):
-        return [pltpu.VMEM((rows,) + shape[1:], bf16), pltpu.SemaphoreType.DMA]
+        return [pltpu.VMEM((rows,) + shape[1:], bf16), pltpu.SemaphoreType.DMA((rows,))]
 
     (out,) = call(
         late_kernel,

time: 74.1 us -> 74.1 us (level)
  no operation moved by 1% of the time
where the time goes in v7:
time: 74.1 us; the launch traced here: 73.8 us
  Pallas kernels  32.5 us (44%)
  waiting for transfers between devices  20.2 us (27%)
  starting transfers between devices  20.1 us (27%)
  other arithmetic  0.75 us (1%)
    pallas_call x9, Pallas kernels, call(): pl.pallas_call(kernel, out_shape=outs, in_specs=[pl.BlockSpec(memory_spac...  32.5 us
    ppermute x4, waiting for transfers between devices, ring(): return lax.ppermute(value, ('lat', 'lon'), links)  13.7 us
    ppermute x4, starting transfers between devices, far_swap(): return lax.ppermute(value, 'lon', [(i, far_of(i, n)) for i in range(n)])  10.2 us
    ppermute x2, waiting for transfers between devices, shift(): lax.ppermute(value, 'lat', [(i, i + by) for i in range(n) if 0 <= i + by...  5.72 us
    ppermute x2, starting transfers between devices, shift(): lax.ppermute(value, 'lat', [(i, i + by) for i in range(n) if 0 <= i + by...  4.69 us
    ppermute x4, starting transfers between devices, ring(): return lax.ppermute(value, ('lat', 'lon'), links)  4.55 us
  transfers between devices with their start and end apart: 14, of which 7 were waited for; matrix products, arithmetic and copies ran while one was open for 0% of the time, Pallas kernels for 21%

profile of v7, /device:TPU:0, one launch (start us, length us, event | category | flops | bytes accessed | tf_op | source)
XLA Modules:
  0.0 73.8 jit_solution(10142284619207944385)
XLA Ops:
  0.0 0.7 compare_convert_fusion.flags
  0.7 2.9 %shard_map.163 = (bf16[8,72,512]{2,1,0:T(8,128)(2,1)S(1)}, bf16[8,72,512]{2,1,0:T(8,128)(2,1)S(1)}, bf16[2,72,512]{2,1,0:T(8,128)(2,1)S(1)}, bf16[2,72,512]{2,1,0:T(8,128)(2,1)S(1)}) custom-call(s32[3]{0:T(128)S(1)} %compare_convert_fusion.flags, bf16[4,12,24,512]{3,2,1,0:T(8,128)(2,1)} %bitcast.12), custom_call_target="tpu_custom_call" | custom-call | tf_op jit(solution)/shard_map/pallas_call | solution.py:690
  4.2 4.7 %collective-permute-start.5 = (bf16[8,72,512]{2,1,0:T(8,128)(2,1)S(1)}, bf16[8,72,512]{2,1,0:T(8,128)(2,1)S(1)}, u32[]{:S(2)}, u32[]{:S(2)}) collective-permute-start(bf16[8,72,512]{2,1,0:T(8,128)(2,1)S(1)} %get-tuple-element.38.own_ref), channel_id=1, source_target_pairs={{0,7},{1,2},{2,1},{3,4},{4,3},{5,6},{6,5},{7,0},{8,15},{9,10},{10,... | collective-permute-start | bytes 1769480 | tf_op jit(solution)/shard_map/ppermute | solution.py:714
  8.9 3.4 %collective-permute-start.1 = (bf16[2,72,512]{2,1,0:T(8,128)(2,1)S(1)}, bf16[2,72,512]{2,1,0:T(8,128)(2,1)S(1)}, u32[]{:S(2)}, u32[]{:S(2)}) collective-permute-start(bf16[2,72,512]{2,1,0:T(8,128)(2,1)S(1)} %get-tuple-element.28), channel_id=1, source_target_pairs={{0,8},{8,16},{16,24},{1,9},{9,17},{17,25},{2,10},{10,18},{18,26},{... | collective-permute-start | bytes 442376 | tf_op jit(solution)/shard_map/ppermute | solution.py:725
  12.3 1.3 %collective-permute-start.2 = (bf16[2,72,512]{2,1,0:T(8,128)(2,1)S(1)}, bf16[2,72,512]{2,1,0:T(8,128)(2,1)S(1)}, u32[]{:S(2)}, u32[]{:S(2)}) collective-permute-start(bf16[2,72,512]{2,1,0:T(8,128)(2,1)S(1)} %get-tuple-element.29), channel_id=1, source_target_pairs={{8,0},{16,8},{24,16},{9,1},{17,9},{25,17},{10,2},{18,10},{26,18},{... | collective-permute-start | bytes 442376 | tf_op jit(solution)/shard_map/ppermute | solution.py:725
  13.6 1.3 %collective-permute-done.1.top_ref = bf16[2,72,512]{2,1,0:T(8,128)(2,1)S(1)} collective-permute-done((bf16[2,72,512]{2,1,0:T(8,128)(2,1)S(1)}, bf16[2,72,512]{2,1,0:T(8,128)(2,1)S(1)}, u32[]{:S(2)}, u32[]{:S(2)}) %collective-permute-start.1) | collective-permute-done | bytes 147488 | tf_op jit(solution)/shard_map/ppermute | solution.py:725
  15.0 4.4 %collective-permute-done.2.bottom_ref = bf16[2,72,512]{2,1,0:T(8,128)(2,1)S(1)} collective-permute-done((bf16[2,72,512]{2,1,0:T(8,128)(2,1)S(1)}, bf16[2,72,512]{2,1,0:T(8,128)(2,1)S(1)}, u32[]{:S(2)}, u32[]{:S(2)}) %collective-permute-start.2) | collective-permute-done | bytes 147488 | tf_op jit(solution)/shard_map/ppermute | solution.py:725
  19.4 1.9 %collective-permute-start.6 = (bf16[2,72,512]{2,1,0:T(8,128)(2,1)S(1)}, bf16[2,72,512]{2,1,0:T(8,128)(2,1)S(1)}, u32[]{:S(2)}, u32[]{:S(2)}) collective-permute-start(bf16[2,72,512]{2,1,0:T(8,128)(2,1)S(1)} %pad_maximum_fusion), channel_id=1, source_target_pairs={{0,7},{1,2},{2,1},{3,4},{4,3},{5,6},{6,5},{7,0},{8,15},{9,10},{10,... | collective-permute-start | bytes 442376 | tf_op jit(solution)/shard_map/ppermute | solution.py:714
  21.3 1.8 %shard_map.164 = (bf16[512,1536]{1,0:T(8,128)(2,1)S(1)}, bf16[512,512]{1,0:T(8,128)(2,1)S(1)}, f32[1,512]{1,0:T(1,128)S(1)}, f32[1,512]{1,0:T(1,128)S(1)}, f32[1...) custom-call(bf16[512,1536]{1,0:T(8,128)(2,1)} %refs_0_.1, ...), custom_call_target="tpu_custom_call" | custom-call | tf_op jit(solution)/shard_map/pallas_call | solution.py:690
  23.1 4.4 %shard_map.165.rest_0_ = bf16[432,512]{1,0:T(8,128)(2,1)S(1)} custom-call(f32[8]{0:T(128)} %scale_ref.6, bf16[8,72,512]{2,1,0:T(8,128)(2,1)S(1)} %get-tuple-element.27.own_ref, bf16[8,72,512]{2,1,0:T(8,128)(2,1)S(1)} %collective-permute-done.other_ref, bf16[512,1536]{1,0:T(8,128)(2,1)S(1)} %get-tuple-element.30.packed_ref, ...), custom_call_target="tpu_custom_call" | custom-call | tf_op jit(solution)/shard_map/pallas_call | solution.py:690
  27.5 5.0 %shard_map.166.rest_0_.near_ref = bf16[144,1024]{1,0:T(8,128)(2,1)S(1)} custom-call(f32[8]{0:T(128)} %scale_ref.6, s32[3]{0:T(128)S(1)} %compare_convert_fusion.flags, bf16[8,72,512]{2,1,0:T(8,128)(2,1)S(1)} %get-tuple-element.27.own_ref, bf16[8,72,512]{2,1,0:T(8,128)(2,1)S(1)} %collective-permute-done.other_ref, ...), custom_call_target="tpu_custom_call" | custom-call | tf_op jit(solution)/shard_map/pallas_call | solution.py:690
  32.6 8.7 %shard_map.167 = (bf16[144,1024]{1,0:T(8,128)(2,1)S(1)}, bf16[72,1024]{1,0:T(8,128)(2,1)S(1)}) custom-call(f32[8]{0:T(128)} %scale_ref.6, s32[3]{0:T(128)S(1)} %compare_convert_fusion.flags, bf16[8,72,512]{2,1,0:T(8,128)(2,1)S(1)} %get-tuple-element.38.own_ref, bf16[8,72,512]{2,1,0:T(8,128)(2,1)S(1)} %collective-permute-done.5.other_ref, ...), custom_call_target="tpu_custom_call" | custom-call | tf_op jit(solution)/shard_map/pallas_call | solution.py:690
  41.2 1.8 %collective-permute-start.9 = (bf16[144,1024]{1,0:T(8,128)(2,1)S(1)}, bf16[144,1024]{1,0:T(8,128)(2,1)S(1)}, u32[]{:S(2)}, u32[]{:S(2)}) collective-permute-start(bf16[144,1024]{1,0:T(8,128)(2,1)S(1)} %get-tuple-element.39.far_ref), channel_id=1, source_target_pairs={{0,7},{1,2},{2,1},{3,4},{4,3},{5,6},{6,5},{7,0},{8,15},{9,10},{10,... | collective-permute-start | bytes 884744 | tf_op jit(solution)/shard_map/ppermute | solution.py:714
  43.0 1.8 %collective-permute-start.8 = (bf16[144,1024]{1,0:T(8,128)(2,1)S(1)}, bf16[144,1024]{1,0:T(8,128)(2,1)S(1)}, u32[]{:S(2)}, u32[]{:S(2)}) collective-permute-start(bf16[144,1024]{1,0:T(8,128)(2,1)S(1)} %shard_map.166.rest_0_.near_ref), channel_id=1, source_target_pairs={{0,7},{1,2},{2,1},{3,4},{4,3},{5,6},{6,5},{7,0},{8,15},{9,10},{10,... | collective-permute-start | bytes 884744 | tf_op jit(solution)/shard_map/ppermute | solution.py:714
  44.9 3.9 %collective-permute-start.10 = (bf16[72,1024]{1,0:T(8,128)(2,1)S(1)}, bf16[72,1024]{1,0:T(8,128)(2,1)S(1)}, u32[]{:S(2)}, u32[]{:S(2)}) collective-permute-start(bf16[72,1024]{1,0:T(8,128)(2,1)S(1)} %get-tuple-element.40), channel_id=1, source_target_pairs={{0,31},{1,26},{2,25},{3,28},{4,27},{5,30},{6,29},{7,24},{8,7},{9,2... | collective-permute-start | bytes 442376 | tf_op jit(solution)/shard_map/ppermute | solution.py:720
  48.7 1.3 %collective-permute-done.7.rim_ref = bf16[72,1024]{1,0:T(8,128)(2,1)S(1)} collective-permute-done((bf16[72,1024]{1,0:T(8,128)(2,1)S(1)}, bf16[72,1024]{1,0:T(8,128)(2,1)S(1)}, u32[]{:S(2)}, u32[]{:S(2)}) %collective-permute-start.7) | collective-permute-done | bytes 147488 | tf_op jit(solution)/shard_map/ppermute | solution.py:720
  50.0 2.4 %shard_map.168 = (bf16[288,1024]{1,0:T(8,128)(2,1)S(1)}, bf16[576,512]{1,0:T(8,128)(2,1)S(1)}, f32[288,512]{1,0:T(8,128)S(1)}, f32[288,512]{1,0:T(8,128)S(1)}) custom-call(f32[8]{0:T(128)} %scale_ref.7, bf16[144,1024]{1,0:T(8,128)(2,1)S(1)} %shard_map.166.rest_0_.near_ref, bf16[144,1024]{1,0:T(8,128)(2,1)S(1)} %get-tuple-element.39.far_ref, ...), custom_call_target="tpu_custom_call" | custom-call | tf_op jit(solution)/shard_map/pallas_call | solution.py:690
  52.4 8.9 %collective-permute-done.10.other_rim_ref = bf16[72,1024]{1,0:T(8,128)(2,1)S(1)} collective-permute-done((bf16[72,1024]{1,0:T(8,128)(2,1)S(1)}, bf16[72,1024]{1,0:T(8,128)(2,1)S(1)}, u32[]{:S(2)}, u32[]{:S(2)}) %collective-permute-start.10) | collective-permute-done | bytes 147488 | tf_op jit(solution)/shard_map/ppermute | solution.py:720
  61.3 3.7 %shard_map.169 = (bf16[288,1024]{1,0:T(8,128)(2,1)S(1)}, bf16[108,1024]{1,0:T(8,128)(2,1)S(1)}, bf16[36,1024]{1,0:T(8,128)(2,1)S(1)}, bf16[36,1024]{1,0:T(8,128)(2,1)S(1)}) custom-call(s32[3]{0:T(128)S(1)} %compare_convert_fusion.flags, bf16[288,1024]{1,0:T(8,128)(2,1)S(1)} %get-tuple-element.41.own_ref, bf16[576,512]{1,0:T(8,128)(2,1)S(1)} %get-tuple-element.42.query_ref, ...), custom_call_target="tpu_custom_call" | custom-call | tf_op jit(solution)/shard_map/pallas_call | solution.py:690
  65.8 0.8 %collective-permute-done.13.near_ref = bf16[108,1024]{1,0:T(8,128)(2,1)S(1)} collective-permute-done((bf16[108,1024]{1,0:T(8,128)(2,1)S(1)}, bf16[108,1024]{1,0:T(8,128)(2,1)S(1)}, u32[]{:S(2)}, u32[]{:S(2)}) %collective-permute-start.13) | collective-permute-done | bytes 221216 | tf_op jit(solution)/shard_map/ppermute | solution.py:709
  66.6 2.0 %shard_map.170._ = bf16[12,1,12,2,1024]{4,3,2,1,0:T(2,128)(2,1)} custom-call(s32[3]{0:T(128)S(1)} %compare_convert_fusion.flags, bf16[288,1024]{1,0:T(8,128)(2,1)S(1)} %get-tuple-element.47.second_ref, bf16[108,1024]{1,0:T(8,128)(2,1)S(1)} %collective-permute-done.13.near_ref, s32[576,18]{1,0:T(8,128)S(1)} %get-tuple-element.37.table_ref), custom_call_target="tpu_custom_call" | custom-call | tf_op jit(solution)/shard_map/pallas_call | solution.py:690
  68.6 2.8 %collective-permute-done.11.back_ref = bf16[36,1024]{1,0:T(8,128)(2,1)S(1)} collective-permute-done((bf16[36,1024]{1,0:T(8,128)(2,1)S(1)}, bf16[36,1024]{1,0:T(8,128)(2,1)S(1)}, u32[]{:S(2)}, u32[]{:S(2)}) %collective-permute-start.11) | collective-permute-done | bytes 73760 | tf_op jit(solution)/shard_map/ppermute | solution.py:720
  71.4 0.7 collective-permute-done.12.back_near_ref
  72.1 1.6 %shard_map.171 = bf16[12,1,12,2,1024]{4,3,2,1,0:T(2,128)(2,1)} custom-call(s32[3]{0:T(128)S(1)} %compare_convert_fusion.flags, bf16[36,1024]{1,0:T(8,128)(2,1)S(1)} %collective-permute-done.11.back_ref, bf16[36,1024]{1,0:T(8,128)(2,1)S(1)} %collective-permute-done.12.back_near_ref, ...), custom_call_target="tpu_custom_call", output_to_operand_aliasing={{}: (4, {})} | custom-call | tf_op jit(solution)/shard_map/pallas_call | solution.py:690
  (25 shorter events, 1.4 us)
Async XLA Ops:
  3.6 19.4 %collective-permute-start = (bf16[8,72,512]{2,1,0:T(8,128)(2,1)S(1)}, bf16[8,72,512]{2,1,0:T(8,128)(2,1)S(1)}, u32[]{:S(2)}, u32[]{:S(2)}) collective-permute-start(bf16[8,72,512]{2,1,0:T(8,128)(2,1)S(1)} %get-tuple-element.27.own_ref), channel_id=1, source_target_pairs={{0,1},{1,0},{2,3},{3,2},{4,5},{5,4},{6,7},{7,6},{8,9},{9,8},{10,11... | collective-permute-start | bytes 1769480 | tf_op jit(solution)/shard_map/ppermute | solution.py:709
  4.2 28.3 %collective-permute-start.5 = (bf16[8,72,512]{2,1,0:T(8,128)(2,1)S(1)}, bf16[8,72,512]{2,1,0:T(8,128)(2,1)S(1)}, u32[]{:S(2)}, u32[]{:S(2)}) collective-permute-start(bf16[8,72,512]{2,1,0:T(8,128)(2,1)S(1)} %get-tuple-element.38.own_ref), channel_id=1, source_target_pairs={{0,7},{1,2},{2,1},{3,4},{4,3},{5,6},{6,5},{7,0},{8,15},{9,10},{10,... | collective-permute-start | bytes 1769480 | tf_op jit(solution)/shard_map/ppermute | solution.py:714
  8.9 6.1 %collective-permute-start.1 = (bf16[2,72,512]{2,1,0:T(8,128)(2,1)S(1)}, bf16[2,72,512]{2,1,0:T(8,128)(2,1)S(1)}, u32[]{:S(2)}, u32[]{:S(2)}) collective-permute-start(bf16[2,72,512]{2,1,0:T(8,128)(2,1)S(1)} %get-tuple-element.28), channel_id=1, source_target_pairs={{0,8},{8,16},{16,24},{1,9},{9,17},{17,25},{2,10},{10,18},{18,26},{... | collective-permute-start | bytes 442376 | tf_op jit(solution)/shard_map/ppermute | solution.py:725
  12.3 7.0 %collective-permute-start.2 = (bf16[2,72,512]{2,1,0:T(8,128)(2,1)S(1)}, bf16[2,72,512]{2,1,0:T(8,128)(2,1)S(1)}, u32[]{:S(2)}, u32[]{:S(2)}) collective-permute-start(bf16[2,72,512]{2,1,0:T(8,128)(2,1)S(1)} %get-tuple-element.29), channel_id=1, source_target_pairs={{8,0},{16,8},{24,16},{9,1},{17,9},{25,17},{10,2},{18,10},{26,18},{... | collective-permute-start | bytes 442376 | tf_op jit(solution)/shard_map/ppermute | solution.py:725
  15.0 12.6 %collective-permute-start.3 = (bf16[2,72,512]{2,1,0:T(8,128)(2,1)S(1)}, bf16[2,72,512]{2,1,0:T(8,128)(2,1)S(1)}, u32[]{:S(2)}, u32[]{:S(2)}) collective-permute-start(bf16[2,72,512]{2,1,0:T(8,128)(2,1)S(1)} %collective-permute-done.1.top_ref), channel_id=1, source_target_pairs={{0,1},{1,0},{2,3},{3,2},{4,5},{5,4},{6,7},{7,6},{8,9},{9,8},{10,11... | collective-permute-start | bytes 442376 | tf_op jit(solution)/shard_map/ppermute | solution.py:709
  19.3 8.2 %collective-permute-start.4 = (bf16[2,72,512]{2,1,0:T(8,128)(2,1)S(1)}, bf16[2,72,512]{2,1,0:T(8,128)(2,1)S(1)}, u32[]{:S(2)}, u32[]{:S(2)}) collective-permute-start(bf16[2,72,512]{2,1,0:T(8,128)(2,1)S(1)} %collective-permute-done.2.bottom_ref), channel_id=1, source_target_pairs={{0,1},{1,0},{2,3},{3,2},{4,5},{5,4},{6,7},{7,6},{8,9},{9,8},{10,11... | collective-permute-start | bytes 442376 | tf_op jit(solution)/shard_map/ppermute | solution.py:709
  19.4 13.1 %collective-permute-start.6 = (bf16[2,72,512]{2,1,0:T(8,128)(2,1)S(1)}, bf16[2,72,512]{2,1,0:T(8,128)(2,1)S(1)}, u32[]{:S(2)}, u32[]{:S(2)}) collective-permute-start(bf16[2,72,512]{2,1,0:T(8,128)(2,1)S(1)} %pad_maximum_fusion), channel_id=1, source_target_pairs={{0,7},{1,2},{2,1},{3,4},{4,3},{5,6},{6,5},{7,0},{8,15},{9,10},{10,... | collective-permute-start | bytes 442376 | tf_op jit(solution)/shard_map/ppermute | solution.py:714
  32.5 17.4 %copy-start = (bf16[1024,1536]{1,0:T(8,128)(2,1)S(1)}, bf16[1024,1536]{1,0:T(8,128)(2,1)}, u32[]{:S(2)}) copy-start(bf16[1024,1536]{1,0:T(8,128)(2,1)} %packed_ref.3) | copy-start | bytes 9437188
  41.2 20.1 %collective-permute-start.9 = (bf16[144,1024]{1,0:T(8,128)(2,1)S(1)}, bf16[144,1024]{1,0:T(8,128)(2,1)S(1)}, u32[]{:S(2)}, u32[]{:S(2)}) collective-permute-start(bf16[144,1024]{1,0:T(8,128)(2,1)S(1)} %get-tuple-element.39.far_ref), channel_id=1, source_target_pairs={{0,7},{1,2},{2,1},{3,4},{4,3},{5,6},{6,5},{7,0},{8,15},{9,10},{10,... | collective-permute-start | bytes 884744 | tf_op jit(solution)/shard_map/ppermute | solution.py:714
  43.0 18.3 %collective-permute-start.8 = (bf16[144,1024]{1,0:T(8,128)(2,1)S(1)}, bf16[144,1024]{1,0:T(8,128)(2,1)S(1)}, u32[]{:S(2)}, u32[]{:S(2)}) collective-permute-start(bf16[144,1024]{1,0:T(8,128)(2,1)S(1)} %shard_map.166.rest_0_.near_ref), channel_id=1, source_target_pairs={{0,7},{1,2},{2,1},{3,4},{4,3},{5,6},{6,5},{7,0},{8,15},{9,10},{10,... | collective-permute-start | bytes 884744 | tf_op jit(solution)/shard_map/ppermute | solution.py:714
  44.8 16.5 %copy-start.1 = (bf16[512,1024]{1,0:T(8,128)(2,1)S(1)}, bf16[512,1024]{1,0:T(8,128)(2,1)}, u32[]{:S(2)}) copy-start(bf16[512,1024]{1,0:T(8,128)(2,1)} %output_ref.1) | copy-start | bytes 3145732
  44.8 16.5 %copy-start.2 = (f32[1024]{0:T(1024)S(1)}, f32[1024]{0:T(1024)}, u32[]{:S(2)}) copy-start(f32[1024]{0:T(1024)} %param.29) | copy-start | bytes 12292
  44.8 16.5 %copy-start.3 = (f32[1024]{0:T(1024)S(1)}, f32[1024]{0:T(1024)}, u32[]{:S(2)}) copy-start(f32[1024]{0:T(1024)} %param.30) | copy-start | bytes 12292
  44.8 5.1 %collective-permute-start.7 = (bf16[72,1024]{1,0:T(8,128)(2,1)S(1)}, bf16[72,1024]{1,0:T(8,128)(2,1)S(1)}, u32[]{:S(2)}, u32[]{:S(2)}) collective-permute-start(bf16[72,1024]{1,0:T(8,128)(2,1)S(1)} %get-tuple-element.40), channel_id=1, source_target_pairs={{0,24},{1,25},{2,26},{3,27},{4,28},{5,29},{6,30},{7,31},{8,0},{9,1... | collective-permute-start | bytes 442376 | tf_op jit(solution)/shard_map/ppermute | solution.py:720
  44.9 16.5 %collective-permute-start.10 = (bf16[72,1024]{1,0:T(8,128)(2,1)S(1)}, bf16[72,1024]{1,0:T(8,128)(2,1)S(1)}, u32[]{:S(2)}, u32[]{:S(2)}) collective-permute-start(bf16[72,1024]{1,0:T(8,128)(2,1)S(1)} %get-tuple-element.40), channel_id=1, source_target_pairs={{0,31},{1,26},{2,25},{3,28},{4,27},{5,30},{6,29},{7,24},{8,7},{9,2... | collective-permute-start | bytes 442376 | tf_op jit(solution)/shard_map/ppermute | solution.py:720
  65.1 1.6 %collective-permute-start.13 = (bf16[108,1024]{1,0:T(8,128)(2,1)S(1)}, bf16[108,1024]{1,0:T(8,128)(2,1)S(1)}, u32[]{:S(2)}, u32[]{:S(2)}) collective-permute-start(bf16[108,1024]{1,0:T(8,128)(2,1)S(1)} %get-tuple-element.48), channel_id=1, source_target_pairs={{0,1},{1,0},{2,3},{3,2},{4,5},{5,4},{6,7},{7,6},{8,9},{9,8},{10,11... | collective-permute-start | bytes 663560 | tf_op jit(solution)/shard_map/ppermute | solution.py:709
  65.1 6.3 %collective-permute-start.11 = (bf16[36,1024]{1,0:T(8,128)(2,1)S(1)}, bf16[36,1024]{1,0:T(8,128)(2,1)S(1)}, u32[]{:S(2)}, u32[]{:S(2)}) collective-permute-start(bf16[36,1024]{1,0:T(8,128)(2,1)S(1)} %get-tuple-element.45), channel_id=1, source_target_pairs={{0,8},{1,9},{2,10},{3,11},{4,12},{5,13},{6,14},{7,15},{8,16},{9,17... | collective-permute-start | bytes 221192 | tf_op jit(solution)/shard_map/ppermute | solution.py:720
  65.8 6.3 %collective-permute-start.12 = (bf16[36,1024]{1,0:T(8,128)(2,1)S(1)}, bf16[36,1024]{1,0:T(8,128)(2,1)S(1)}, u32[]{:S(2)}, u32[]{:S(2)}) collective-permute-start(bf16[36,1024]{1,0:T(8,128)(2,1)S(1)} %get-tuple-element.46), channel_id=1, source_target_pairs={{0,9},{1,8},{2,11},{3,10},{4,13},{5,12},{6,15},{7,14},{8,17},{9,16... | collective-permute-start | bytes 221192 | tf_op jit(solution)/shard_map/ppermute | solution.py:720
